TPU v7x, 256 devices: a whole 4x4x8 slice. The times are simulated.
256 devices in a mesh: tm: 32 (over y, z), dom: 8 (over x, core).
Axes of the slice: x: 4, y: 4, z: 8, core: 2. Of those that a mesh axis runs over, the one named last changes fastest.
Arguments:
- iterates: float32 [64, 2, 4096, 256], P('tm', None, 'dom'), may hold values from -6 to 6
- noise_draws: bfloat16 [64, 2, 4096, 256], P('tm', None, 'dom'), may hold values from -6 to 6
- drift_scale: float32 [64], P('tm'), may hold values from 0.05 to 0.2
- noise_scale: float32 [64], P('tm'), may hold values from 0.05 to 0.2
- step_embed: float32 [64, 256], P('tm'), may hold values from -3 to 3
- self_weight: bfloat16 [2, 256, 256], replicated, may hold values from -0.375 to 0.375
- neighbor_weight: bfloat16 [2, 256, 256], replicated, may hold values from -0.375 to 0.375
- output_weight: bfloat16 [2, 256, 256], replicated, may hold values from -0.375 to 0.375
- drift_weight: bfloat16 [256, 256], replicated, may hold values from -0.375 to 0.375
- local_columns: int32 [32, 4], P('dom'), may hold values from 0 to 3
- tile_values: bfloat16 [32, 4, 128, 128], P('dom'), may hold values from -0.25 to 0.25
- send_blocks: int32 [8, 2, 2], P('dom'), may hold values from 0 to 3
- receive_rows: int32 [8, 2, 2], P('dom'), may hold values from 0 to 3
- remote_values: bfloat16 [8, 2, 2, 128, 128], P('dom'), may hold values from -0.5 to 0.5
Outputs:
- next_iterates: float32 [64, 2, 4096, 256], P('tm', None, 'dom')
Inputs may be any that keep to these rules, and one draw needn't show every extreme that they name: `local_columns`: column block within the tile's own partition. In round r partition p sends its blocks send_blocks[p, r, :] to partition p XOR 2**r. `receive_rows`: row block within the receiving partition.
All inputs are finite; a program needn't handle non-finite values.
Results may differ from a plain program's by a relative error of at most 0.006.
Values may be sent and summed in bfloat16 or wider, within the bound.
No kernel may reach another device: no remote copies, remote signals or barrier semaphores. Data moves between devices by JAX's collectives and lax.ppermute only.
A program may use at most 128 MiB of HBM per device.

v0:
```python
import jax
import jax.numpy as jnp
from jax import lax
from jax.sharding import PartitionSpec as P


def from_partner(value, axis, bit):
    return lax.ppermute(value, axis, [(i, i ^ 1 << bit) for i in range(lax.axis_size(axis))])


def broadcast(value, axis, root):
    mine = lax.axis_index(axis) == root
    return lax.psum(jnp.where(mine, value, jnp.zeros_like(value)), axis)


def prefix(value, axis, combine, identity):
    peers, position = (lax.axis_size(axis), lax.axis_index(axis))
    everything = lax.all_gather(value, axis)
    start = jnp.broadcast_to(jnp.asarray(identity, value.dtype), value.shape)

    def turn(k, before):
        reached = k < position
        new = combine(before, everything[k])
        return jnp.where(reached, new, before)

    return lax.fori_loop(0, peers, turn, start)


def add_terms(earlier, later):
    return earlier + later


def local(
    iterates,
    noise_draws,
    drift_scale,
    noise_scale,
    step_embed,
    self_weight,
    neighbor_weight,
    output_weight,
    drift_weight,
    local_columns,
    tile_values,
    send_blocks,
    receive_rows,
    remote_values,
):
    step_count, shower_count, cell_count, feature_width = iterates.shape
    block_size = tile_values.shape[2]
    per_part = cell_count // block_size
    row_count = step_count * shower_count
    hidden = iterates.astype(jnp.bfloat16)
    for layer in range(self_weight.shape[0]):
        blocked = hidden.reshape(row_count, per_part, block_size, feature_width)
        columns = blocked[:, local_columns]
        summed = jnp.einsum(
            "rjab,mrjbd->mrad", tile_values, columns, preferred_element_type=jnp.float32
        )
        for round_index in range(send_blocks.shape[1]):
            outgoing = blocked[:, send_blocks[0, round_index]]
            incoming = from_partner(outgoing, "dom", round_index)
            remote_terms = jnp.einsum(
                "kab,mkbd->mkad",
                remote_values[0, round_index],
                incoming,
                preferred_element_type=jnp.float32,
            )
            select = (
                receive_rows[0, round_index][None, :] == jnp.arange(per_part)[:, None]
            ).astype(jnp.float32)
            summed = summed + jnp.einsum(
                "rk,mkad->mrad", select, remote_terms, precision=lax.Precision.HIGHEST
            )
        mixed = summed.reshape(hidden.shape).astype(jnp.bfloat16)
        preact = jnp.dot(hidden, self_weight[layer], preferred_element_type=jnp.float32)
        preact = (
            preact
            + jnp.dot(mixed, neighbor_weight[layer], preferred_element_type=jnp.float32)
            + step_embed[:, None, None, :]
        )
        activated = jax.nn.silu(preact).astype(jnp.bfloat16)
        hidden = (
            hidden.astype(jnp.float32)
            + jnp.dot(activated, output_weight[layer], preferred_element_type=jnp.float32)
        ).astype(jnp.bfloat16)
    drift = jnp.dot(hidden, drift_weight, preferred_element_type=jnp.float32)
    increments = drift_scale[:, None, None, None] * drift + noise_scale[
        :, None, None, None
    ] * noise_draws.astype(jnp.float32)
    running = jnp.cumsum(increments, axis=0)
    device_total = running[-1]
    first_state = iterates[0]
    base_state = broadcast(first_state.astype(jnp.bfloat16), "tm", 0).astype(first_state.dtype)
    earlier_sum = prefix(device_total, "tm", add_terms, jnp.zeros_like(device_total))
    offset = base_state + earlier_sum
    return offset[None] + running


def solution(mesh):
    return jax.shard_map(
        local,
        mesh=mesh,
        in_specs=(
            P("tm", None, "dom", None),
            P("tm", None, "dom", None),
            P("tm"),
            P("tm"),
            P("tm", None),
            P(),
            P(),
            P(),
            P(),
            P("dom", None),
            P("dom", None, None, None),
            P("dom", None, None),
            P("dom", None, None),
            P("dom", None, None, None, None),
        ),
        out_specs=P("tm", None, "dom", None),
        check_vma=False,
    )
```

profile of v0, /device:TPU:2, one launch (start us, length us, event | category | flops | bytes accessed | tf_op | source)
XLA Modules:
  0.0 479.8 jit_solution(3738714084763059030)
XLA Ops:
  7.3 1.7 convert.3
  12.2 2.3 collective-permute-start.1
  14.6 1.8 fusion.26
  16.4 2.8 gather_fusion
  22.6 4.7 collective-permute-done.1
  28.6 2.3 copy.44
  30.9 3.6 fusion.46
  34.5 2.3 fusion.50
  39.1 2.8 add_convert_fusion.1
  44.1 2.8 gather_fusion.3
  47.9 1.7 collective-permute-start.3
  49.6 1.8 fusion.21
  51.4 2.3 convolution_bitcast_fusion.1
  53.7 2.3 copy.49
  56.0 6.5 %collective-permute-done.3 = bf16[4,2,128,256]{2,3,0,1:T(8,128)(2,1)S(1)} collective-permute-done((bf16[4,2,128,256]{2,3,0,1:T(8,128)(2,1)}, bf16[4,2,128,256]{2,3,0,1:T(8,128)(2,1)S(1)}, u32[]{:S(2)}, u32[]{:S(2)}) %collective-permute-start.3) | collective-permute-done | bytes 524320 | tf_op jit(solution)/shard_map/ppermute | solution.py:8
  63.7 2.3 copy.52
  66.0 3.6 fusion.44
  69.6 3.5 fusion.48
  75.9 1.8 multiply_convert_fusion
  77.7 3.4 fusion.9
  81.1 2.3 fusion.4
  86.7 234.9 %all-gather.2.cloned.1.call-done = f32[32,2,512,256]{3,2,1,0:T(8,128)} async-done(((f32[1,2,512,256]{3,2,1,0:T(8,128)}), f32[32,2,512,256]{3,2,1,0:T(8,128)}) %all-gather.2.cloned.1.call-update) | async-done | bytes 33554448 | tf_op jit(solution)/shard_map/all_gather | solution.py:18
  321.6 50.1 %while.14 = (s32[]{:T(128)}, f32[2,512,256]{2,1,0:T(8,128)S(1)}, s32[]{:T(128)}, f32[32,2,512,256]{3,2,1,0:T(8,128)}, s32[]{:T(128)}, /*index=5*/s32[]{:T(128)}) while((s32[]{:T(128)}, f32[2,512,256]{2,1,0:T(8,128)S(1)}, s32[]{:T(128)}, f32[32,2,512,256]{3,2,1,0:T(8,128)}, s32[]{:T(128)}, /*index=5*/s32[]{:T(128)}) %tuple.35), condition=%wide.region_3.4_spmd.clone, body=%wide.region_2.3_spmd.clone.sunk | while | flops 786436 | bytes 3145829 | solution.py:26
  371.8 97.9 %all-reduce.2.cloned.1.call-done = bf16[2,512,256]{2,1,0:T(8,128)(2,1)} async-done(((bf16[2,512,256]{2,1,0:T(8,128)(2,1)}), bf16[2,512,256]{2,1,0:T(8,128)(2,1)}) %all-reduce.2.cloned.1.call-update) | async-done | bytes 524304 | tf_op jit(solution)/shard_map/psum | solution.py:13
  (105 shorter events, 74.2 us)
Async XLA Ops:
  6.5 30.3 %copy-start = (bf16[4,4,128,128]{3,2,1,0:T(8,128)(2,1)S(1)}, bf16[4,4,128,128]{3,2,1,0:T(8,128)(2,1)}, u32[]{:S(2)}) copy-start(bf16[4,4,128,128]{3,2,1,0:T(8,128)(2,1)} %param.26) | copy-start | bytes 1572868
  6.5 315.1 %all-gather.2.cloned.1.call-start = ((), (), s32[]{:S(2)}) async-start(), calls=%async_computation.1 | async-start | bytes 34603008 | tf_op jit(solution)/shard_map/all_gather | solution.py:18
  9.0 5.5 %copy-start.12 = (s32[4,4]{1,0:T(4,128)S(1)}, s32[4,4]{1,0:T(4,128)}, u32[]{:S(2)}) copy-start(s32[4,4]{1,0:T(4,128)} %param.25) | copy-start | bytes 196
  9.0 5.6 %copy-start.7 = (bf16[2,256,256]{2,1,0:T(8,128)(2,1)S(1)}, bf16[2,256,256]{2,1,0:T(8,128)(2,1)}, u32[]{:S(2)}) copy-start(bf16[2,256,256]{2,1,0:T(8,128)(2,1)} %param.21) | copy-start | bytes 786436
  10.6 9.1 %collective-permute-start = (bf16[4,2,128,256]{2,3,0,1:T(8,128)(2,1)}, bf16[4,2,128,256]{2,3,0,1:T(8,128)(2,1)S(1)}, u32[]{:S(2)}, u32[]{:S(2)}) collective-permute-start(bf16[4,2,128,256]{2,3,0,1:T(8,128)(2,1)} %bitcast.14), channel_id=1, source_target_pairs={{0,1},{1,0},{2,3},{3,2},{4,5},{5,4},{6,7},{7,6},{8,9},{9,8},{10,11... | collective-permute-start | bytes 1572872 | tf_op jit(solution)/shard_map/ppermute | solution.py:8
  12.2 15.1 %collective-permute-start.1 = (bf16[4,2,128,256]{2,3,0,1:T(8,128)(2,1)}, bf16[4,2,128,256]{2,3,0,1:T(8,128)(2,1)S(1)}, u32[]{:S(2)}, u32[]{:S(2)}) collective-permute-start(bf16[4,2,128,256]{2,3,0,1:T(8,128)(2,1)} %bitcast.186), channel_id=1, source_target_pairs={{0,2},{1,3},{2,0},{3,1},{4,6},{5,7},{6,4},{7,5},{8,10},{9,11},{10,... | collective-permute-start | bytes 1572872 | tf_op jit(solution)/shard_map/ppermute | solution.py:8
  16.4 2.8 copy-start.13
  16.4 3.4 copy-start.6
  30.9 6.0 %copy-start.2 = (bf16[16,4,128,256]{3,2,1,0:T(8,128)(2,1)S(1)}, bf16[16,4,128,256]{3,2,1,0:T(8,128)(2,1)}, u32[]{:S(2)}) copy-start(bf16[16,4,128,256]{3,2,1,0:T(8,128)(2,1)} %gather_fusion) | copy-start | bytes 12582916
  38.0 1.1 copy-start.16
  43.5 7.9 %collective-permute-start.2 = (bf16[4,2,128,256]{2,3,0,1:T(8,128)(2,1)}, bf16[4,2,128,256]{2,3,0,1:T(8,128)(2,1)}, u32[]{:S(2)}, u32[]{:S(2)}) collective-permute-start(bf16[4,2,128,256]{2,3,0,1:T(8,128)(2,1)} %bitcast.187), channel_id=1, source_target_pairs={{0,1},{1,0},{2,3},{3,2},{4,5},{5,4},{6,7},{7,6},{8,9},{9,8},{10,11... | collective-permute-start | bytes 1572872 | tf_op jit(solution)/shard_map/ppermute | solution.py:8
  47.9 14.5 %collective-permute-start.3 = (bf16[4,2,128,256]{2,3,0,1:T(8,128)(2,1)}, bf16[4,2,128,256]{2,3,0,1:T(8,128)(2,1)S(1)}, u32[]{:S(2)}, u32[]{:S(2)}) collective-permute-start(bf16[4,2,128,256]{2,3,0,1:T(8,128)(2,1)} %bitcast.188), channel_id=1, source_target_pairs={{0,2},{1,3},{2,0},{3,1},{4,6},{5,7},{6,4},{7,5},{8,10},{9,11},{10,... | collective-permute-start | bytes 1572872 | tf_op jit(solution)/shard_map/ppermute | solution.py:8
  56.0 10.0 %copy-start.11 = (s32[2]{0:T(128)S(1)}, s32[2]{0:T(128)}, u32[]{:S(2)}) copy-start(s32[2]{0:T(128)} %get-tuple-element.109) | copy-start | bytes 28
  66.0 7.1 %copy-start.1 = (bf16[16,4,128,256]{3,2,1,0:T(8,128)(2,1)S(1)}, bf16[16,4,128,256]{3,2,1,0:T(8,128)(2,1)}, u32[]{:S(2)}) copy-start(bf16[16,4,128,256]{3,2,1,0:T(8,128)(2,1)} %gather_fusion.3) | copy-start | bytes 12582916
  73.1 1.3 copy-start.17
  73.1 1.3 copy-start.18
  74.3 1.6 copy-start.5
  75.9 1.8 copy-start.8
  75.9 1.8 copy-start.10
  77.7 3.4 copy-start.14
  77.7 3.4 copy-start.15
  83.4 1.3 copy-start.3
  85.8 383.9 %all-reduce.2.cloned.1.call-start = ((), (), s32[]{:S(2)}) async-start(), calls=%async_computation | async-start | bytes 1048576 | tf_op jit(solution)/shard_map/psum | solution.py:13
  469.7 1.7 copy-start.4
  (1 other events, 1.1 us)
Sparse Core Ops, SparseCore 0:
  85.9 235.6 all-gather.1
  325.0 144.5 all-reduce.1
where the time goes:
time: 481 us; the launch traced here: 480 us
  waiting for transfers between devices  344 us (72%)
  other arithmetic  57.8 us (12%)
  matrix products  33 us (7%)
  local copies, waits for them, and re-layouts  26.5 us (6%)
  between operations  13.7 us (3%)
    all_gather x1, waiting for transfers between devices, prefix(): everything = lax.all_gather(value, axis)  235 us
    psum x1, waiting for transfers between devices, broadcast(): return lax.psum(jnp.where(mine, value, jnp.zeros_like(value)), axis)  97.9 us
    select_n x32, other arithmetic, turn(): return jnp.where(reached, new, before)  49.4 us
    dot_general x4, matrix products, local(): jnp.einsum('rk,mkad->mrad', select, remote_terms, precision=lax.Precision...  13 us
    ppermute x4, waiting for transfers between devices, from_partner(): lax.ppermute(value, axis, [(i, i ^ 1 << bit) for i in range(lax.axis_size...  11.2 us
  transfers between devices with their start and end apart: 6, of which 4 were waited for; matrix products, arithmetic and copies ran while one was open for 15% of the time, Pallas kernels for 0%

commit v1 on v0

v1 whole, which is shorter than its diff:
```python
import jax
import jax.numpy as jnp
from jax import lax
from jax.experimental import pallas as pl
from jax.experimental.pallas import tpu as pltpu
from jax.sharding import PartitionSpec as P

F32 = jnp.float32
BF16 = jnp.bfloat16
COLS = 8
ROWS = 4

VMEM = pl.BlockSpec(memory_space=pltpu.VMEM)
SMEM = pl.BlockSpec(memory_space=pltpu.SMEM)


def dot(a, b):
    return jnp.dot(a, b, preferred_element_type=F32)


def vmem_call(body, outs, in_specs, name):
    return pl.pallas_call(
        body,
        out_shape=outs,
        in_specs=in_specs,
        out_specs=jax.tree.map(lambda _: VMEM, outs),
        name=name,
    )


def pack(iterates, send_blocks, block):
    steps, showers, cells, width = iterates.shape
    rounds, sent = send_blocks.shape[1:]
    rows = steps * showers

    def body(blocks_ref, it_ref, h_ref, *send_refs):
        for row in range(rows):
            h_ref[row] = it_ref[row // showers, row % showers].astype(BF16)
        for r in range(rounds):
            for k in range(sent):
                at = pl.ds(blocks_ref[0, r, k] * block, block)
                for row in range(rows):
                    send_refs[r][row, k] = h_ref[row, at, :]

    send = jax.ShapeDtypeStruct((rows, sent, block, width), BF16)
    outs = [jax.ShapeDtypeStruct((rows, cells, width), BF16)] + [send] * rounds
    return vmem_call(body, outs, [SMEM, VMEM], "pack")(send_blocks, iterates)


def near(hidden, incoming, embed, weight, columns, tiles, remote, receive):
    rows, cells, width = hidden.shape
    parts, per_row, block, _ = tiles.shape
    sent = incoming.shape[1]
    repeat = rows // embed.shape[0]

    def body(col_ref, recv_ref, h_ref, in_ref, emb_ref, w_ref, tile_ref, rem_ref, agg_ref, pre_ref):
        for b in range(parts):
            wide = jnp.concatenate([tile_ref[b, j] for j in range(per_row)], axis=1)
            for row in range(rows):
                tall = jnp.concatenate(
                    [h_ref[row, pl.ds(col_ref[b, j] * block, block), :] for j in range(per_row)], axis=0
                )
                agg_ref[row, b * block : (b + 1) * block, :] = dot(wide, tall)
        for k in range(sent):
            at = pl.ds(recv_ref[0, 0, k] * block, block)
            for row in range(rows):
                agg_ref[row, at, :] += dot(rem_ref[0, 0, k], in_ref[row, k])
        for row in range(rows):
            pre_ref[row] = dot(h_ref[row], w_ref[...]) + emb_ref[row // repeat][None, :]

    out = jax.ShapeDtypeStruct((rows, cells, width), F32)
    return vmem_call(body, [out, out], [SMEM, SMEM] + [VMEM] * 6, "near")(
        columns, receive, hidden, incoming, embed, weight, tiles, remote
    )


def update(recv_ref, h_ref, in_ref, agg_ref, pre_ref, wn_ref, wo_ref, rem_ref, sum_ref, row):
    sent, block = in_ref.shape[1], in_ref.shape[2]
    sum_ref[...] = agg_ref[row]
    for k in range(sent):
        at = pl.ds(recv_ref[0, 1, k] * block, block)
        sum_ref[at, :] += dot(rem_ref[0, 1, k], in_ref[row, k])
    preact = pre_ref[row] + dot(sum_ref[...].astype(BF16), wn_ref[...])
    half = 0.5 * preact
    activated = (half + half * jnp.tanh(half)).astype(BF16)
    return (h_ref[row].astype(F32) + dot(activated, wo_ref[...])).astype(BF16)


def far(hidden, incoming, agg, pre, neighbor, output, remote, receive, send_blocks):
    rows, cells, width = hidden.shape
    rounds, sent = send_blocks.shape[1:]
    block = incoming.shape[2]

    def body(recv_ref, blocks_ref, h_ref, in_ref, agg_ref, pre_ref, wn_ref, wo_ref, rem_ref, out_ref, s0, s1, sum_ref):
        send_refs = (s0, s1)
        for row in range(rows):
            out_ref[row] = update(recv_ref, h_ref, in_ref, agg_ref, pre_ref, wn_ref, wo_ref, rem_ref, sum_ref, row)
            for r in range(rounds):
                for k in range(sent):
                    send_refs[r][row, k] = out_ref[row, pl.ds(blocks_ref[0, r, k] * block, block), :]

    send = jax.ShapeDtypeStruct((rows, sent, block, width), BF16)
    outs = [jax.ShapeDtypeStruct((rows, cells, width), BF16)] + [send] * rounds
    return pl.pallas_call(
        body,
        out_shape=outs,
        in_specs=[SMEM, SMEM] + [VMEM] * 7,
        out_specs=[VMEM] * len(outs),
        scratch_shapes=[pltpu.VMEM((cells, width), F32)],
        name="far",
    )(receive, send_blocks, hidden, incoming, agg, pre, neighbor, output, remote)


def finish(hidden, incoming, agg, pre, neighbor, output, remote, receive, drift_weight, scale, noise_part):
    rows, cells, width = hidden.shape
    steps = scale.shape[0]
    showers = rows // steps

    def body(recv_ref, scale_ref, h_ref, in_ref, agg_ref, pre_ref, wn_ref, wo_ref, rem_ref, wd_ref, nz_ref, run_ref, tot_ref, sum_ref):
        for shower in range(showers):
            total = None
            for step in range(steps):
                row = step * showers + shower
                last = update(recv_ref, h_ref, in_ref, agg_ref, pre_ref, wn_ref, wo_ref, rem_ref, sum_ref, row)
                drift = scale_ref[step] * dot(last, wd_ref[...])
                total = drift if total is None else total + drift
                run_ref[row] = total + nz_ref[row]
            tot_ref[shower] = run_ref[(steps - 1) * showers + shower].astype(BF16)

    outs = [
        jax.ShapeDtypeStruct((rows, cells, width), F32),
        jax.ShapeDtypeStruct((showers, cells, width), BF16),
    ]
    return pl.pallas_call(
        body,
        out_shape=outs,
        in_specs=[SMEM, SMEM] + [VMEM] * 9,
        out_specs=[VMEM] * 2,
        scratch_shapes=[pltpu.VMEM((cells, width), F32)],
        name="finish",
    )(receive, scale, hidden, incoming, agg, pre, neighbor, output, remote, drift_weight, noise_part)


def row_total(parts):
    def body(p_ref, o_ref):
        total = p_ref[0].astype(F32)
        for z in range(1, parts.shape[0]):
            total = total + p_ref[z].astype(F32)
        o_ref[...] = total.astype(BF16)

    return vmem_call(body, jax.ShapeDtypeStruct(parts.shape[1:], BF16), [VMEM], "row_total")(parts)


def row_prefix(parts, below):
    def body(p_ref, b0, b1, b2, o_ref):
        total = b0[...].astype(F32) + b1[...].astype(F32) + b2[...].astype(F32)
        for z in range(parts.shape[0]):
            o_ref[z] = total.astype(BF16)
            total = total + p_ref[z].astype(F32)

    return vmem_call(body, jax.ShapeDtypeStruct(parts.shape, BF16), [VMEM] * 4, "row_prefix")(parts, *below)


def local(
    iterates,
    noise_draws,
    drift_scale,
    noise_scale,
    step_embed,
    self_weight,
    neighbor_weight,
    output_weight,
    drift_weight,
    local_columns,
    tile_values,
    send_blocks,
    receive_rows,
    remote_values,
):
    steps, showers, cells, width = iterates.shape
    block = tile_values.shape[2]
    rows = steps * showers
    layers = self_weight.shape[0]
    parts = lax.axis_size("dom")
    near_pairs = [(i, i ^ 1) for i in range(parts)]
    far_pairs = [(i, i ^ 2) for i in range(parts)]
    groups = [[y * COLS + z for z in range(COLS)] for y in range(ROWS)]

    first = (lax.axis_index("tm") == 0).astype(F32)
    noise = noise_scale[:, None, None, None] * noise_draws.astype(F32)
    noise_part = jnp.cumsum(noise, axis=0) + first * iterates[:1]
    noise_part = noise_part.reshape(rows, cells, width)

    hidden, send0, send1 = pack(iterates, send_blocks, block)
    for layer in range(layers):
        in0 = lax.ppermute(send0, "dom", near_pairs)
        in1 = lax.ppermute(send1, "dom", far_pairs)
        agg, pre = near(
            hidden, in0, step_embed, self_weight[layer], local_columns, tile_values, remote_values, receive_rows
        )
        if layer + 1 < layers:
            hidden, send0, send1 = far(
                hidden, in1, agg, pre, neighbor_weight[layer], output_weight[layer], remote_values, receive_rows, send_blocks
            )
    running, total = finish(
        hidden, in1, agg, pre, neighbor_weight[layer], output_weight[layer], remote_values, receive_rows,
        drift_weight, drift_scale, noise_part,
    )
    pieces = total.reshape(COLS, -1, width)
    pieces = lax.all_to_all(pieces, "tm", 0, 0, axis_index_groups=groups)
    whole = row_total(pieces)
    below = [
        lax.ppermute(
            whole, "tm", [(y * COLS + z, (y + up) * COLS + z) for y in range(ROWS - up) for z in range(COLS)]
        )
        for up in range(1, ROWS)
    ]
    earlier = lax.all_to_all(row_prefix(pieces, below), "tm", 0, 0, axis_index_groups=groups)
    earlier = earlier.reshape(showers, cells, width).astype(F32)
    return running.reshape(steps, showers, cells, width) + earlier[None]


def solution(mesh):
    return jax.shard_map(
        local,
        mesh=mesh,
        in_specs=(
            P("tm", None, "dom", None),
            P("tm", None, "dom", None),
            P("tm"),
            P("tm"),
            P("tm", None),
            P(),
            P(),
            P(),
            P(),
            P("dom", None),
            P("dom", None, None, None),
            P("dom", None, None),
            P("dom", None, None),
            P("dom", None, None, None, None),
        ),
        out_specs=P("tm", None, "dom", None),
        check_vma=False,
    )
```

time: 481 us -> 107 us (0.22)
  waiting for transfers between devices: 344 us -> 13.3 us
  other arithmetic: 57.8 us -> 3.28 us
  blocking collectives: 0 us -> 41.6 us
  matrix products: 33 us -> 0 us
  Pallas kernels: 0 us -> 29.2 us
  local copies, waits for them, and re-layouts: 26.5 us -> 5.44 us
  between operations: 13.7 us -> 0.12 us
  starting transfers between devices: 4.06 us -> 13.1 us
    all_gather x1 -> x0, waiting for transfers between devices: 235 us -> none  [prefix(): everything = lax.all_gather(value, axis)]
    psum x1 -> x0, waiting for transfers between devices: 97.9 us -> none  [broadcast(): return lax.psum(jnp.where(mine, value, jnp.zeros_like(value)), axis)]
    select_n x35 -> x0, other arithmetic: 51 us -> none  [the longest x32 49.4 us: turn(): return jnp.where(reached, new, before)]
    all_to_all x0 -> x2, blocking collectives: none -> 41.6 us  [the longest x1 24.3 us: local(): pieces = lax.all_to_all(pieces, 'tm', 0, 0, axis_index_groups=groups)]
    dot_general x15 -> x0, matrix products: 33 us -> none  [the longest x4 13 us: local(): jnp.einsum('rk,mkad->mrad', select, remote_terms, precision=lax.Precision...]
    pallas_call x0 -> x7, Pallas kernels: none -> 29.2 us  [the longest x2 9 us: near(): vmem_call(body, [out, out], [SMEM, SMEM] + [VMEM] * 6, 'near')]
    gather x10 -> x0, local copies, waits for them, and re-layouts: 11.9 us -> none  [the longest x8 6.35 us: local(): outgoing = blocked[:, send_blocks[0, round_index]]]
    ppermute x4 -> x7, starting transfers between devices: 4.02 us -> 13.1 us  [the longest x3 8.96 us: local(): lax.ppermute(whole, 'tm', [(y * COLS + z, (y + up) * COLS + z) for y in r...]
  transfers between devices with their start and end apart: 6 -> 7, of which waited for: 4 -> 4; matrix products, arithmetic and copies ran while one was open for 15% -> 3% of each run, Pallas kernels for 0% -> 8%
where the time goes in v1:
time: 107 us; the launch traced here: 106 us
  blocking collectives  41.6 us (39%)
  Pallas kernels  29.2 us (27%)
  waiting for transfers between devices  13.3 us (12%)
  starting transfers between devices  13.1 us (12%)
  local copies, waits for them, and re-layouts  5.44 us (5%)
  other arithmetic  3.28 us (3%)
    all_to_all x1, blocking collectives, local(): pieces = lax.all_to_all(pieces, 'tm', 0, 0, axis_index_groups=groups)  24.3 us
    all_to_all x1, blocking collectives, local(): lax.all_to_all(row_prefix(pieces, below), 'tm', 0, 0, axis_index_groups=g...  17.2 us
    ppermute x2, waiting for transfers between devices, local(): in1 = lax.ppermute(send1, 'dom', far_pairs)  10.7 us
    pallas_call x2, Pallas kernels, near(): vmem_call(body, [out, out], [SMEM, SMEM] + [VMEM] * 6, 'near')  9 us
    ppermute x3, starting transfers between devices, local(): lax.ppermute(whole, 'tm', [(y * COLS + z, (y + up) * COLS + z) for y in r...  8.96 us
    pallas_call x1, Pallas kernels, finish(): pl.pallas_call(body, out_shape=outs, in_specs=[SMEM, SMEM] + [VMEM] * 9,...  7.18 us
    pallas_call x1, Pallas kernels, far(): pl.pallas_call(body, out_shape=outs, in_specs=[SMEM, SMEM] + [VMEM] * 7,...  6.11 us
    ppermute x2, starting transfers between devices, local(): in1 = lax.ppermute(send1, 'dom', far_pairs)  4.09 us
  transfers between devices with their start and end apart: 7, of which 4 were waited for; matrix products, arithmetic and copies ran while one was open for 3% of the time, Pallas kernels for 8%

profile of v1, /device:TPU:2, one launch (start us, length us, event | category | flops | bytes accessed | tf_op | source)
XLA Modules:
  0.0 106.0 jit_solution(16278884187609091456)
XLA Ops:
  0.0 3.1 %pack.1 = (bf16[4,512,256]{2,1,0:T(8,128)(2,1)}, bf16[4,2,128,256]{3,2,1,0:T(8,128)(2,1)}, bf16[4,2,128,256]{3,2,1,0:T(8,128)(2,1)}) custom-call(s32[1,2,2]{2,1,0:T(2,128)} %blocks_ref.3, f32[2,2,512,256]{3,2,1,0:T(8,128)} %it_ref.1), custom_call_target="tpu_custom_call" | custom-call | tf_op jit(solution)/shard_map/pack/pallas_call | solution.py:47
  3.1 2.3 %collective-permute-start = (bf16[4,2,128,256]{3,2,1,0:T(8,128)(2,1)}, bf16[4,2,128,256]{3,2,1,0:T(8,128)(2,1)S(1)}, u32[]{:S(2)}, u32[]{:S(2)}) collective-permute-start(bf16[4,2,128,256]{3,2,1,0:T(8,128)(2,1)} %get-tuple-element.18), channel_id=1, source_target_pairs={{0,2},{1,3},{2,0},{3,1},{4,6},{5,7},{6,4},{7,5},{8,10},{9,11},{10,... | collective-permute-start | bytes 1572872 | tf_op jit(solution)/shard_map/ppermute | solution.py:197
  6.1 0.8 slice_bitcast_fusion
  6.9 0.8 copy-done.4
  7.7 4.5 %near.2 = (f32[4,512,256]{2,1,0:T(8,128)}, f32[4,512,256]{2,1,0:T(8,128)}) custom-call(s32[4,4]{1,0:T(4,128)} %col_ref.3, s32[1,2,2]{2,1,0:T(2,128)} %recv_ref.7, bf16[4,512,256]{2,1,0:T(8,128)(2,1)} %get-tuple-element.17.h_ref, bf16[4,2,128,256]{3,2,1,0:T(8,128)(2,1)} %copy-done.4, f32[2,256]{1,0:T(2,128)} %emb_ref.3, ...), custom_call_target="tpu_custom_call" | custom-call | tf_op jit(solution)/shard_map/near/pallas_call | solution.py:72
  12.2 5.9 %collective-permute-done.in_ref = bf16[4,2,128,256]{3,2,1,0:T(8,128)(2,1)S(1)} collective-permute-done((bf16[4,2,128,256]{3,2,1,0:T(8,128)(2,1)}, bf16[4,2,128,256]{3,2,1,0:T(8,128)(2,1)S(1)}, u32[]{:S(2)}, u32[]{:S(2)}) %collective-permute-start) | collective-permute-done | bytes 524320 | tf_op jit(solution)/shard_map/ppermute | solution.py:197
  18.2 0.8 copy-done.6
  19.0 6.1 %far.1 = (bf16[4,512,256]{2,1,0:T(8,128)(2,1)}, bf16[4,2,128,256]{3,2,1,0:T(8,128)(2,1)}, bf16[4,2,128,256]{3,2,1,0:T(8,128)(2,1)}) custom-call(s32[1,2,2]{2,1,0:T(2,128)} %recv_ref.7, s32[1,2,2]{2,1,0:T(2,128)} %blocks_ref.3, bf16[4,512,256]{2,1,0:T(8,128)(2,1)} %get-tuple-element.17.h_ref, bf16[4,2,128,256]{3,2,1,0:T(8,128)(2,1)} %copy-done.6, ...), custom_call_target="tpu_custom_call" | custom-call | tf_op jit(solution)/shard_map/far/pallas_call | solution.py:104
  25.1 1.8 %collective-permute-start.2 = (bf16[4,2,128,256]{3,2,1,0:T(8,128)(2,1)}, bf16[4,2,128,256]{3,2,1,0:T(8,128)(2,1)S(1)}, u32[]{:S(2)}, u32[]{:S(2)}) collective-permute-start(bf16[4,2,128,256]{3,2,1,0:T(8,128)(2,1)} %get-tuple-element.23), channel_id=1, source_target_pairs={{0,2},{1,3},{2,0},{3,1},{4,6},{5,7},{6,4},{7,5},{8,10},{9,11},{10,... | collective-permute-start | bytes 1572872 | tf_op jit(solution)/shard_map/ppermute | solution.py:197
  27.0 1.6 %fusion.3 = f32[2,2,512,256]{3,2,1,0:T(8,128)} fusion(bf16[2,2,512,256]{3,2,1,0:T(8,128)(2,1)S(1)} %copy-done.2, f32[2,512,256]{2,1,0:T(8,128)S(1)} %multiply_bitcast_fusion, f32[2]{0:T(128)S(1)} %copy-done.13), kind=kOutput, calls=%fused_computation.3 | output fusion | flops 2097152 | bytes 4194312 | tf_op jit(solution)/shard_map/jit(cumsum)/reduce_window_sum | solution.py:191
  29.0 0.8 copy-done.5
  29.8 4.5 %near.3 = (f32[4,512,256]{2,1,0:T(8,128)}, f32[4,512,256]{2,1,0:T(8,128)}) custom-call(s32[4,4]{1,0:T(4,128)} %col_ref.3, s32[1,2,2]{2,1,0:T(2,128)} %recv_ref.7, bf16[4,512,256]{2,1,0:T(8,128)(2,1)} %get-tuple-element.22.h_ref, bf16[4,2,128,256]{3,2,1,0:T(8,128)(2,1)} %copy-done.5, f32[2,256]{1,0:T(2,128)} %emb_ref.3, ...), custom_call_target="tpu_custom_call" | custom-call | tf_op jit(solution)/shard_map/near/pallas_call | solution.py:72
  34.3 4.8 %collective-permute-done.2.in_ref = bf16[4,2,128,256]{3,2,1,0:T(8,128)(2,1)S(1)} collective-permute-done((bf16[4,2,128,256]{3,2,1,0:T(8,128)(2,1)}, bf16[4,2,128,256]{3,2,1,0:T(8,128)(2,1)S(1)}, u32[]{:S(2)}, u32[]{:S(2)}) %collective-permute-start.2) | collective-permute-done | bytes 524320 | tf_op jit(solution)/shard_map/ppermute | solution.py:197
  39.1 0.8 copy-done.3
  40.0 7.2 %finish.1 = (f32[4,512,256]{2,1,0:T(8,128)}, bf16[2,512,256]{2,1,0:T(8,128)(2,1)}) custom-call(s32[1,2,2]{2,1,0:T(2,128)} %recv_ref.7, f32[2]{0:T(128)} %scale_ref.1, bf16[4,512,256]{2,1,0:T(8,128)(2,1)} %get-tuple-element.22.h_ref, bf16[4,2,128,256]{3,2,1,0:T(8,128)(2,1)} %copy-done.3, f32[4,512,256]{2,1,0:T(8,128)} %get-tuple-element.25.agg_ref, ...), custom_call_target="tpu_custom_call" | custom-call | tf_op jit(solution)/shard_map/finish/pallas_call | solution.py:134
  47.1 24.3 %all_to_all.10.p_ref = bf16[8,128,256]{2,1,0:T(8,128)(2,1)} all-to-all(bf16[8,128,256]{2,1,0:T(8,128)(2,1)} %bitcast.24), channel_id=1, replica_groups={{0,8,16,24,32,40,48,56},{64,72,80,88,96,104,112,120},{128,136,144,152,1..., dimensions={0} | all-to-all | bytes 1048576 | tf_op jit(solution)/shard_map/all_to_all | solution.py:210
  71.5 1.9 %row_total.1 = bf16[128,256]{1,0:T(8,128)(2,1)} custom-call(bf16[8,128,256]{2,1,0:T(8,128)(2,1)} %all_to_all.10.p_ref), custom_call_target="tpu_custom_call" | custom-call | tf_op jit(solution)/shard_map/row_total/pallas_call | solution.py:151
  73.4 4.9 %collective-permute-start.6 = (bf16[128,256]{1,0:T(8,128)(2,1)}, bf16[128,256]{1,0:T(8,128)(2,1)S(1)}, u32[]{:S(2)}, u32[]{:S(2)}) collective-permute-start(bf16[128,256]{1,0:T(8,128)(2,1)} %row_total.1), channel_id=1, source_target_pairs={{0,192},{8,200},{16,208},{24,216},{32,224},{40,232},{48,240},{56,2... | collective-permute-start | bytes 196616 | tf_op jit(solution)/shard_map/ppermute | solution.py:213
  78.3 1.3 %collective-permute-start.5 = (bf16[128,256]{1,0:T(8,128)(2,1)}, bf16[128,256]{1,0:T(8,128)(2,1)S(1)}, u32[]{:S(2)}, u32[]{:S(2)}) collective-permute-start(bf16[128,256]{1,0:T(8,128)(2,1)} %row_total.1), channel_id=1, source_target_pairs={{0,128},{8,136},{16,144},{24,152},{32,160},{40,168},{48,176},{56,1... | collective-permute-start | bytes 196616 | tf_op jit(solution)/shard_map/ppermute | solution.py:213
  79.6 2.8 %collective-permute-start.4 = (bf16[128,256]{1,0:T(8,128)(2,1)}, bf16[128,256]{1,0:T(8,128)(2,1)S(1)}, u32[]{:S(2)}, u32[]{:S(2)}) collective-permute-start(bf16[128,256]{1,0:T(8,128)(2,1)} %row_total.1), channel_id=1, source_target_pairs={{0,64},{8,72},{16,80},{24,88},{32,96},{40,104},{48,112},{56,120},{... | collective-permute-start | bytes 196616 | tf_op jit(solution)/shard_map/ppermute | solution.py:213
  82.4 2.2 %collective-permute-done.4.b0 = bf16[128,256]{1,0:T(8,128)(2,1)S(1)} collective-permute-done((bf16[128,256]{1,0:T(8,128)(2,1)}, bf16[128,256]{1,0:T(8,128)(2,1)S(1)}, u32[]{:S(2)}, u32[]{:S(2)}) %collective-permute-start.4) | collective-permute-done | bytes 65568 | tf_op jit(solution)/shard_map/ppermute | solution.py:213
  85.2 2.0 %row_prefix.1 = bf16[8,128,256]{2,1,0:T(8,128)(2,1)} custom-call(bf16[8,128,256]{2,1,0:T(8,128)(2,1)} %all_to_all.10.p_ref, bf16[128,256]{1,0:T(8,128)(2,1)} %copy-done.12, bf16[128,256]{1,0:T(8,128)(2,1)} %copy-done.11, bf16[128,256]{1,0:T(8,128)(2,1)} %copy-done.10), custom_call_target="tpu_custom_call" | custom-call | tf_op jit(solution)/shard_map/row_prefix/pallas_call | solution.py:161
  87.2 17.2 %all_to_all.11 = bf16[8,128,256]{2,1,0:T(8,128)(2,1)S(1)} all-to-all(bf16[8,128,256]{2,1,0:T(8,128)(2,1)} %row_prefix.1), channel_id=1, replica_groups={{0,8,16,24,32,40,48,56},{64,72,80,88,96,104,112,120},{128,136,144,152,1..., dimensions={0} | all-to-all | bytes 1048576 | tf_op jit(solution)/shard_map/all_to_all | solution.py:218
  104.5 1.5 %broadcast_add_fusion = f32[2,2,512,256]{3,2,1,0:T(8,128)} fusion(f32[2,2,512,256]{3,2,1,0:T(8,128)S(1)} %bitcast.23, f32[2,512,256]{2,1,0:T(8,128)S(1)} %bitcast_convert_fusion), kind=kLoop, calls=%fused_computation.4 | loop fusion | flops 524288 | bytes 5242880 | tf_op jit(solution)/shard_map/add | solution.py:220
  (33 shorter events, 1.9 us)
Async XLA Ops:
  0.0 5.4 %copy-start.7 = (bf16[2,256,256]{2,1,0:T(8,128)(2,1)S(1)}, bf16[2,256,256]{2,1,0:T(8,128)(2,1)}, u32[]{:S(2)}) copy-start(bf16[2,256,256]{2,1,0:T(8,128)(2,1)} %param.19) | copy-start | bytes 786436
  0.0 6.1 %copy-start.8 = (bf16[2,256,256]{2,1,0:T(8,128)(2,1)S(1)}, bf16[2,256,256]{2,1,0:T(8,128)(2,1)}, u32[]{:S(2)}) copy-start(bf16[2,256,256]{2,1,0:T(8,128)(2,1)} %param.21) | copy-start | bytes 786436
  0.0 6.1 %copy-start.9 = (bf16[2,256,256]{2,1,0:T(8,128)(2,1)S(1)}, bf16[2,256,256]{2,1,0:T(8,128)(2,1)}, u32[]{:S(2)}) copy-start(bf16[2,256,256]{2,1,0:T(8,128)(2,1)} %param.20) | copy-start | bytes 786436
  3.1 3.8 %collective-permute-start.1 = (bf16[4,2,128,256]{3,2,1,0:T(8,128)(2,1)}, bf16[4,2,128,256]{3,2,1,0:T(8,128)(2,1)S(1)}, u32[]{:S(2)}, u32[]{:S(2)}) collective-permute-start(bf16[4,2,128,256]{3,2,1,0:T(8,128)(2,1)} %get-tuple-element.19), channel_id=1, source_target_pairs={{0,1},{1,0},{2,3},{3,2},{4,5},{5,4},{6,7},{7,6},{8,9},{9,8},{10,11... | collective-permute-start | bytes 1572872 | tf_op jit(solution)/shard_map/ppermute | solution.py:196
  3.1 15.1 %collective-permute-start = (bf16[4,2,128,256]{3,2,1,0:T(8,128)(2,1)}, bf16[4,2,128,256]{3,2,1,0:T(8,128)(2,1)S(1)}, u32[]{:S(2)}, u32[]{:S(2)}) collective-permute-start(bf16[4,2,128,256]{3,2,1,0:T(8,128)(2,1)} %get-tuple-element.18), channel_id=1, source_target_pairs={{0,2},{1,3},{2,0},{3,1},{4,6},{5,7},{6,4},{7,5},{8,10},{9,11},{10,... | collective-permute-start | bytes 1572872 | tf_op jit(solution)/shard_map/ppermute | solution.py:197
  6.9 0.8 copy-start.4
  18.2 0.8 copy-start.6
  19.0 7.9 %copy-start = (f32[2,2,512,256]{3,2,1,0:T(8,128)S(1)}, f32[2,2,512,256]{3,2,1,0:T(8,128)}, u32[]{:S(2)}) copy-start(f32[2,2,512,256]{3,2,1,0:T(8,128)} %it_ref.1) | copy-start | bytes 6291460
  25.1 1.9 %copy-start.2 = (bf16[2,2,512,256]{3,2,1,0:T(8,128)(2,1)S(1)}, bf16[2,2,512,256]{3,2,1,0:T(8,128)(2,1)}, u32[]{:S(2)}) copy-start(bf16[2,2,512,256]{3,2,1,0:T(8,128)(2,1)} %param.15) | copy-start | bytes 3145732
  25.1 1.9 %copy-start.13 = (f32[2]{0:T(128)S(1)}, f32[2]{0:T(128)}, u32[]{:S(2)}) copy-start(f32[2]{0:T(128)} %param.17) | copy-start | bytes 28
  25.1 14.1 %collective-permute-start.2 = (bf16[4,2,128,256]{3,2,1,0:T(8,128)(2,1)}, bf16[4,2,128,256]{3,2,1,0:T(8,128)(2,1)S(1)}, u32[]{:S(2)}, u32[]{:S(2)}) collective-permute-start(bf16[4,2,128,256]{3,2,1,0:T(8,128)(2,1)} %get-tuple-element.23), channel_id=1, source_target_pairs={{0,2},{1,3},{2,0},{3,1},{4,6},{5,7},{6,4},{7,5},{8,10},{9,11},{10,... | collective-permute-start | bytes 1572872 | tf_op jit(solution)/shard_map/ppermute | solution.py:197
  26.9 2.1 %collective-permute-start.3 = (bf16[4,2,128,256]{3,2,1,0:T(8,128)(2,1)}, bf16[4,2,128,256]{3,2,1,0:T(8,128)(2,1)S(1)}, u32[]{:S(2)}, u32[]{:S(2)}) collective-permute-start(bf16[4,2,128,256]{3,2,1,0:T(8,128)(2,1)} %get-tuple-element.24), channel_id=1, source_target_pairs={{0,1},{1,0},{2,3},{3,2},{4,5},{5,4},{6,7},{7,6},{8,9},{9,8},{10,11... | collective-permute-start | bytes 1572872 | tf_op jit(solution)/shard_map/ppermute | solution.py:196
  29.0 0.8 copy-start.5
  39.1 0.9 copy-start.3
  71.5 33.0 %copy-start.1 = (f32[4,512,256]{2,1,0:T(8,128)S(1)}, f32[4,512,256]{2,1,0:T(8,128)}, u32[]{:S(2)}) copy-start(f32[4,512,256]{2,1,0:T(8,128)} %get-tuple-element.27) | copy-start | bytes 6291460
  73.4 9.0 %collective-permute-start.6 = (bf16[128,256]{1,0:T(8,128)(2,1)}, bf16[128,256]{1,0:T(8,128)(2,1)S(1)}, u32[]{:S(2)}, u32[]{:S(2)}) collective-permute-start(bf16[128,256]{1,0:T(8,128)(2,1)} %row_total.1), channel_id=1, source_target_pairs={{0,192},{8,200},{16,208},{24,216},{32,224},{40,232},{48,240},{56,2... | collective-permute-start | bytes 196616 | tf_op jit(solution)/shard_map/ppermute | solution.py:213
  78.3 4.1 %collective-permute-start.5 = (bf16[128,256]{1,0:T(8,128)(2,1)}, bf16[128,256]{1,0:T(8,128)(2,1)S(1)}, u32[]{:S(2)}, u32[]{:S(2)}) collective-permute-start(bf16[128,256]{1,0:T(8,128)(2,1)} %row_total.1), channel_id=1, source_target_pairs={{0,128},{8,136},{16,144},{24,152},{32,160},{40,168},{48,176},{56,1... | collective-permute-start | bytes 196616 | tf_op jit(solution)/shard_map/ppermute | solution.py:213
  79.6 5.0 %collective-permute-start.4 = (bf16[128,256]{1,0:T(8,128)(2,1)}, bf16[128,256]{1,0:T(8,128)(2,1)S(1)}, u32[]{:S(2)}, u32[]{:S(2)}) collective-permute-start(bf16[128,256]{1,0:T(8,128)(2,1)} %row_total.1), channel_id=1, source_target_pairs={{0,64},{8,72},{16,80},{24,88},{32,96},{40,104},{48,112},{56,120},{... | collective-permute-start | bytes 196616 | tf_op jit(solution)/shard_map/ppermute | solution.py:213
  82.4 2.2 %copy-start.10 = (bf16[128,256]{1,0:T(8,128)(2,1)}, bf16[128,256]{1,0:T(8,128)(2,1)S(1)}, u32[]{:S(2)}) copy-start(bf16[128,256]{1,0:T(8,128)(2,1)S(1)} %collective-permute-done.6.b2) | copy-start | bytes 196612
  82.4 2.2 %copy-start.11 = (bf16[128,256]{1,0:T(8,128)(2,1)}, bf16[128,256]{1,0:T(8,128)(2,1)S(1)}, u32[]{:S(2)}) copy-start(bf16[128,256]{1,0:T(8,128)(2,1)S(1)} %collective-permute-done.5.b1) | copy-start | bytes 196612
  84.6 0.6 copy-start.12

commit v2 on v0

v2 whole, which is shorter than its diff:
```python
import jax
import jax.numpy as jnp
from jax import lax
from jax.experimental import pallas as pl
from jax.experimental.pallas import tpu as pltpu
from jax.sharding import PartitionSpec as P

F32 = jnp.float32
BF16 = jnp.bfloat16
COLS = 8
ROWS = 4


def dot(a, b):
    return jnp.dot(a, b, preferred_element_type=F32)


def call(body, name, outs, scalars, arrays, far_arrays=(), far_outs=(), after=(), scratch=(), flops=1 << 20):
    pin = lambda a: pltpu.with_memory_space_constraint(a, pltpu.VMEM)
    keep = lambda a: pltpu.with_memory_space_constraint(a, pltpu.HBM)
    count = len(scalars) + len(arrays) + len(far_arrays)
    vmem = pl.BlockSpec(memory_space=pltpu.VMEM)

    def inner(*refs):
        body(*refs[:count], *refs[count + len(after) :])

    return pl.pallas_call(
        inner,
        out_shape=[pltpu.VMEM(*o) for o in outs] + [pltpu.HBM(*o) for o in far_outs],
        in_specs=[pl.BlockSpec(memory_space=pltpu.SMEM)] * len(scalars)
        + [vmem] * len(arrays)
        + [pl.BlockSpec(memory_space=pltpu.HBM)] * len(far_arrays)
        + [vmem] * len(after),
        out_specs=[vmem] * len(outs) + [pl.BlockSpec(memory_space=pltpu.HBM)] * len(far_outs),
        scratch_shapes=list(scratch),
        compiler_params=pltpu.CompilerParams(vmem_limit_bytes=12 << 20),
        cost_estimate=pl.CostEstimate(flops=flops, transcendentals=0, bytes_accessed=1 << 10),
        name=name,
    )(*scalars, *map(pin, arrays), *map(keep, far_arrays), *map(pin, after))


def pack(iterates, send_blocks, block):
    steps, showers, cells, width = iterates.shape
    rounds, sent = send_blocks.shape[1:]

    def body(blocks_ref, it_ref, *send_refs):
        for r in reversed(range(rounds)):
            for k in range(sent):
                at = pl.ds(blocks_ref[0, r, k] * block, block)
                for shower in range(showers):
                    for step in range(steps):
                        send_refs[r * showers + shower][step, k] = it_ref[step, shower, at, :].astype(BF16)

    outs = [((steps, sent, block, width), BF16)] * (rounds * showers)
    sends = call(body, "pack", outs, [send_blocks], [iterates])
    return [sends[r * showers : (r + 1) * showers] for r in range(rounds)]


def near_step(col_ref, h_ref, emb_ref, ws, wn, tile_ref, pre_ref, step):
    parts, per_row, block, _ = tile_ref.shape
    mixed = []
    for b in range(parts):
        wide = jnp.concatenate([tile_ref[b, j] for j in range(per_row)], axis=1)
        tall = jnp.concatenate(
            [h_ref[step, pl.ds(col_ref[b, j] * block, block), :] for j in range(per_row)], axis=0
        )
        mixed.append(dot(wide, tall).astype(BF16))
    pre = dot(h_ref[step], ws) + dot(jnp.concatenate(mixed, axis=0), wn)
    pre_ref[step] = pre + emb_ref[step : step + 1, :]


def near(hidden, layer, embed, weight, neighbor, columns, tiles, after):
    steps, cells, width = hidden.shape

    def body(col_ref, h_ref, emb_ref, ws_ref, wn_ref, tile_ref, pre_ref):
        for step in range(steps):
            near_step(col_ref, h_ref, emb_ref, ws_ref[layer], wn_ref[layer], tile_ref, pre_ref, step)

    return call(
        body, "near", [((steps, cells, width), F32)], [columns], [hidden, embed, weight, neighbor, tiles], after=after
    )[0]


def near_first(iterates, shower, embed, weight, neighbor, columns, tiles, after):
    steps, _, cells, width = iterates.shape

    def body(col_ref, it_ref, emb_ref, ws_ref, wn_ref, tile_ref, pre_ref, h_ref):
        for step in range(steps):
            h_ref[step] = it_ref[step, shower].astype(BF16)
        for step in range(steps):
            near_step(col_ref, h_ref, emb_ref, ws_ref[0], wn_ref[0], tile_ref, pre_ref, step)

    return call(
        body, "near_first", [((steps, cells, width), F32), ((steps, cells, width), BF16)], [columns],
        [iterates, embed, weight, neighbor, tiles], after=after,
    )


def update(recv_ref, h_ref, in_refs, pre_ref, wn, wo, rem_ref, step):
    sent, block = in_refs[0].shape[1:3]
    parts = h_ref.shape[1] // block
    addends = [
        (recv_ref[0, r, k], dot(rem_ref[0, r, k], in_ref[step, k])) for r, in_ref in enumerate(in_refs) for k in range(sent)
    ]
    mixed = []
    for b in range(parts):
        total = None
        for row, addend in addends:
            term = jnp.where(row == b, 1.0, 0.0) * addend
            total = term if total is None else total + term
        mixed.append(total.astype(BF16))
    half = 0.5 * (pre_ref[step] + dot(jnp.concatenate(mixed, axis=0), wn))
    activated = (half + half * jnp.tanh(half)).astype(BF16)
    return (h_ref[step].astype(F32) + dot(activated, wo)).astype(BF16)


def far(hidden, incoming, pre, layer, neighbor, output, remote, receive, send_blocks, after):
    steps, cells, width = hidden.shape
    rounds, sent = send_blocks.shape[1:]
    block = incoming[0].shape[2]

    def body(recv_ref, blocks_ref, h_ref, *refs):
        in_refs, (pre_ref, wn_ref, wo_ref, rem_ref, out_ref, *send_refs) = refs[:rounds], refs[rounds:]
        for step in range(steps):
            out_ref[step] = update(recv_ref, h_ref, in_refs, pre_ref, wn_ref[layer], wo_ref[layer], rem_ref, step)
        for r in range(rounds):
            for k in range(sent):
                at = pl.ds(blocks_ref[0, r, k] * block, block)
                for step in range(steps):
                    send_refs[r][step, k] = out_ref[step, at, :]

    outs = [((steps, cells, width), BF16)] + [((steps, sent, block, width), BF16)] * rounds
    return call(
        body, "far", outs, [receive, send_blocks], [hidden, *incoming, pre, neighbor, output, remote], after=after
    )


def finish(hidden, incoming, pre, layer, shower, neighbor, output, remote, receive, drift_weight, scales, noise, iterates, after):
    steps, cells, width = hidden.shape

    def body(recv_ref, ds_ref, ns_ref, h_ref, *refs):
        in_refs, refs = refs[: len(incoming)], refs[len(incoming) :]
        pre_ref, wn_ref, wo_ref, rem_ref, wd_ref, nz_hbm, it_hbm, tot_ref, run_hbm, nz_ref, it_ref, run_ref, sems = refs
        loads = [pltpu.make_async_copy(it_hbm.at[0, shower], it_ref, sems.at[0])]
        loads += [pltpu.make_async_copy(nz_hbm.at[step, shower], nz_ref.at[step], sems.at[1 + step]) for step in range(steps)]
        stores = [pltpu.make_async_copy(run_ref.at[step], run_hbm.at[step], sems.at[1 + steps + step]) for step in range(steps)]
        for load in loads:
            load.start()
        first = jnp.where(lax.axis_index("tm") == 0, 1.0, 0.0)
        total = None
        for step in range(steps):
            last = update(recv_ref, h_ref, in_refs, pre_ref, wn_ref[layer], wo_ref[layer], rem_ref, step)
            drift = ds_ref[step] * dot(last, wd_ref[...])
            if step == 0:
                loads[0].wait()
            loads[1 + step].wait()
            before = first * it_ref[...] if step == 0 else run_ref[step - 1]
            total = before + drift + ns_ref[step] * nz_ref[step].astype(F32)
            run_ref[step] = total
            stores[step].start()
        tot_ref[...] = total.astype(BF16)
        for store in stores:
            store.wait()

    return call(
        body, "finish", [((cells, width), BF16)], [receive, *scales],
        [hidden, *incoming, pre, neighbor, output, remote, drift_weight], [noise, iterates],
        [((steps, cells, width), F32)], after=after, flops=1 << 35,
        scratch=[
            pltpu.VMEM((steps, cells, width), BF16), pltpu.VMEM((cells, width), F32),
            pltpu.VMEM((steps, cells, width), F32), pltpu.SemaphoreType.DMA((1 + 2 * steps,)),
        ],
    )


def row_total(parts):
    def body(p_ref, o_ref):
        total = p_ref[0].astype(F32)
        for z in range(1, parts.shape[0]):
            total = total + p_ref[z].astype(F32)
        o_ref[...] = total.astype(BF16)

    return call(body, "row_total", [(parts.shape[1:], BF16)], [], [parts])[0]


def row_prefix(parts, below):
    def body(p_ref, *refs):
        o_ref = refs[-1]
        total = refs[0][...].astype(F32)
        for ref in refs[1:-1]:
            total = total + ref[...].astype(F32)
        for z in range(parts.shape[0]):
            o_ref[z] = total.astype(BF16)
            total = total + p_ref[z].astype(F32)

    return call(body, "row_prefix", [(parts.shape, BF16)], [], [parts, *below])[0]


def deliver(out, running, earlier, shower, shape):
    steps, cells, width = running.shape
    args = [running, earlier] + ([] if out is None else [out])

    def body(run_ref, early_ref, *refs):
        refs[-1][0, 0] = run_ref[0] + early_ref[...].astype(F32)

    return pl.pallas_call(
        body,
        grid=(steps,),
        out_shape=jax.ShapeDtypeStruct(shape, F32),
        in_specs=[pl.BlockSpec((1, cells, width), lambda t: (t, 0, 0)), pl.BlockSpec((cells, width), lambda t: (0, 0))]
        + [pl.BlockSpec(memory_space=pl.ANY)] * (len(args) - 2),
        out_specs=pl.BlockSpec((1, 1, cells, width), lambda t: (t, shower, 0, 0)),
        input_output_aliases={} if out is None else {2: 0},
        compiler_params=pltpu.CompilerParams(vmem_limit_bytes=12 << 20),
        name="deliver",
    )(*args)


def local(
    iterates,
    noise_draws,
    drift_scale,
    noise_scale,
    step_embed,
    self_weight,
    neighbor_weight,
    output_weight,
    drift_weight,
    local_columns,
    tile_values,
    send_blocks,
    receive_rows,
    remote_values,
):
    steps, showers, cells, width = iterates.shape
    block = tile_values.shape[2]
    layers = self_weight.shape[0]
    parts = lax.axis_size("dom")
    pairs = [[(i, i ^ (1 << r)) for i in range(parts)] for r in range(2)]
    groups = [[y * COLS + z for z in range(COLS)] for y in range(ROWS)]

    sends = pack(iterates, send_blocks, block)
    incoming = [[lax.ppermute(sends[r][s], "dom", pairs[r]) for r in (0, 1)] for s in range(showers)]
    common = (step_embed, self_weight, neighbor_weight, local_columns, tile_values)
    rest = (neighbor_weight, output_weight, remote_values, receive_rows)
    hidden, pre = [None] * showers, [None] * showers
    token = ()
    for s in range(showers):
        pre[s], hidden[s] = near_first(iterates, s, *common, token)
        token = (pre[s],)
    for layer in range(1, layers):
        for s in range(showers):
            hidden[s], *sends = far(hidden[s], incoming[s], pre[s], layer - 1, *rest, send_blocks, token)
            incoming[s] = [lax.ppermute(sends[r], "dom", pairs[r]) for r in (0, 1)]
            pre[s] = near(hidden[s], layer, *common, ())
            token = (pre[s],)
    running, pieces, totals = [None] * showers, [None] * showers, [None] * showers
    for s in range(showers):
        totals[s], running[s] = finish(
            hidden[s], incoming[s], pre[s], layers - 1, s, *rest, drift_weight, (drift_scale, noise_scale),
            noise_draws, iterates, token,
        )
        token = (totals[s],)
        pieces[s] = lax.all_to_all(totals[s].reshape(COLS, -1, width), "tm", 0, 0, axis_index_groups=groups)
    out = None
    for s in range(showers):
        whole = row_total(pieces[s])
        below = [
            lax.ppermute(
                whole, "tm", [(y * COLS + z, (y + up) * COLS + z) for y in range(ROWS - up) for z in range(COLS)]
            )
            for up in range(1, ROWS)
        ]
        earlier = lax.all_to_all(row_prefix(pieces[s], below), "tm", 0, 0, axis_index_groups=groups)
        out = deliver(out, running[s], earlier.reshape(cells, width), s, iterates.shape)
    return out


def solution(mesh):
    return jax.shard_map(
        local,
        mesh=mesh,
        in_specs=(
            P("tm", None, "dom", None),
            P("tm", None, "dom", None),
            P("tm"),
            P("tm"),
            P("tm", None),
            P(),
            P(),
            P(),
            P(),
            P("dom", None),
            P("dom", None, None, None),
            P("dom", None, None),
            P("dom", None, None),
            P("dom", None, None, None, None),
        ),
        out_specs=P("tm", None, "dom", None),
        check_vma=False,
    )
```

time: 481 us -> 100 us (0.21)
  the two profiles are of different devices: /device:TPU:2 before, /device:TPU:8 now
where the time goes in v2:
time: 100 us; the launch traced here: 99.1 us
  starting transfers between devices  43.1 us (43%)
  waiting for transfers between devices  25.1 us (25%)
  Pallas kernels  24.5 us (24%)
  local copies, waits for them, and re-layouts  6.17 us (6%)
    pallas_call x13, Pallas kernels, call(): pl.pallas_call(inner, out_shape=[pltpu.VMEM(*o) for o in outs] + [pltpu.H...  22.4 us
    all_to_all x2, starting transfers between devices, local(): lax.all_to_all(row_prefix(pieces[s], below), 'tm', 0, 0, axis_index_group...  13.4 us
    ppermute x6, starting transfers between devices, local(): lax.ppermute(whole, 'tm', [(y * COLS + z, (y + up) * COLS + z) for y in r...  12.1 us
    all_to_all x2, starting transfers between devices, local(): lax.all_to_all(totals[s].reshape(COLS, -1, width), 'tm', 0, 0, axis_index...  11.9 us
    all_to_all x2, waiting for transfers between devices, local(): lax.all_to_all(row_prefix(pieces[s], below), 'tm', 0, 0, axis_index_group...  10.5 us
    ppermute x6, waiting for transfers between devices, local(): lax.ppermute(whole, 'tm', [(y * COLS + z, (y + up) * COLS + z) for y in r...  7.73 us
    unnamed x40, local copies, waits for them, and re-layouts  6.17 us
    all_to_all x2, waiting for transfers between devices, local(): lax.all_to_all(totals[s].reshape(COLS, -1, width), 'tm', 0, 0, axis_index...  5.88 us
  transfers between devices with their start and end apart: 18, of which 7 were waited for; matrix products, arithmetic and copies ran while one was open for 0% of the time, Pallas kernels for 23%

profile of v2, /device:TPU:8, one launch (start us, length us, event | category | flops | bytes accessed | tf_op | source)
XLA Modules:
  0.0 99.1 jit_solution(8496530872617674809)
XLA Ops:
  0.0 1.6 %copy-done = f32[2,2,512,256]{3,2,1,0:T(8,128)S(1)} copy-done((f32[2,2,512,256]{3,2,1,0:T(8,128)S(1)}, f32[2,2,512,256]{3,2,1,0:T(8,128)}, u32[]{:S(2)}) %copy-start) | copy-done | bytes 2097176
  3.0 1.6 %collective-permute-start.3 = (bf16[2,2,128,256]{3,2,1,0:T(8,128)(2,1)S(1)}, bf16[2,2,128,256]{3,2,1,0:T(8,128)(2,1)S(1)}, u32[]{:S(2)}, u32[]{:S(2)}) collective-permute-start(bf16[2,2,128,256]{3,2,1,0:T(8,128)(2,1)S(1)} %get-tuple-element.30), channel_id=1, source_target_pairs={{0,2},{1,3},{2,0},{3,1},{4,6},{5,7},{6,4},{7,5},{8,10},{9,11},{10,... | collective-permute-start | bytes 786440 | tf_op jit(solution)/shard_map/ppermute | solution.py:243
  8.3 1.6 %near_first.2 = (f32[2,512,256]{2,1,0:T(8,128)S(1)}, bf16[2,512,256]{2,1,0:T(8,128)(2,1)S(1)}) custom-call(s32[4,4]{1,0:T(4,128)S(1)} %copy-done.12, f32[2,2,512,256]{3,2,1,0:T(8,128)S(1)} %copy-done.1, f32[2,256]{1,0:T(2,128)S(1)} %copy-done.13, bf16[2,256,256]{2,1,0:T(8,128)(2,1)S(1)} %copy-done.6, bf16[2,256,256]{2,1,0:T(8,128)(2,1)S(1)} %copy-done.2, ...), custom_call_target="tpu_custom_call" | custom-call | flops 1048576 | bytes 1024 | tf_op jit(solution)/shard_map/near_first/pallas_call | solution.py:27
  10.0 1.6 %near_first.3 = (f32[2,512,256]{2,1,0:T(8,128)S(1)}, bf16[2,512,256]{2,1,0:T(8,128)(2,1)S(1)}) custom-call(s32[4,4]{1,0:T(4,128)S(1)} %copy-done.12, f32[2,2,512,256]{3,2,1,0:T(8,128)S(1)} %copy-done.1, f32[2,256]{1,0:T(2,128)S(1)} %copy-done.13, bf16[2,256,256]{2,1,0:T(8,128)(2,1)S(1)} %copy-done.6, bf16[2,256,256]{2,1,0:T(8,128)(2,1)S(1)} %copy-done.2, ...), custom_call_target="tpu_custom_call" | custom-call | flops 1048576 | bytes 1024 | tf_op jit(solution)/shard_map/near_first/pallas_call | solution.py:27
  12.3 1.7 %far.2 = (bf16[2,512,256]{2,1,0:T(8,128)(2,1)S(1)}, bf16[2,2,128,256]{3,2,1,0:T(8,128)(2,1)S(1)}, bf16[2,2,128,256]{3,2,1,0:T(8,128)(2,1)S(1)}) custom-call(s32[1,2,2]{2,1,0:T(2,128)S(1)} %copy-done.15, s32[1,2,2]{2,1,0:T(2,128)S(1)} %copy-done.14, bf16[2,512,256]{2,1,0:T(8,128)(2,1)S(1)} %get-tuple-element.28.refs_2_, ...), custom_call_target="tpu_custom_call" | custom-call | flops 1048576 | bytes 1024 | tf_op jit(solution)/shard_map/far/pallas_call | solution.py:27
  14.0 1.6 %collective-permute-start.7 = (bf16[2,2,128,256]{3,2,1,0:T(8,128)(2,1)S(1)}, bf16[2,2,128,256]{3,2,1,0:T(8,128)(2,1)S(1)}, u32[]{:S(2)}, u32[]{:S(2)}) collective-permute-start(bf16[2,2,128,256]{3,2,1,0:T(8,128)(2,1)S(1)} %get-tuple-element.36), channel_id=1, source_target_pairs={{0,2},{1,3},{2,0},{3,1},{4,6},{5,7},{6,4},{7,5},{8,10},{9,11},{10,... | collective-permute-start | bytes 786440 | tf_op jit(solution)/shard_map/ppermute | solution.py:254
  15.6 1.6 %near.2.refs_9_.refs_6_ = f32[2,512,256]{2,1,0:T(8,128)S(1)} custom-call(s32[4,4]{1,0:T(4,128)S(1)} %copy-done.12, bf16[2,512,256]{2,1,0:T(8,128)(2,1)S(1)} %get-tuple-element.31.refs_1_.refs_3_, f32[2,256]{1,0:T(2,128)S(1)} %copy-done.13, bf16[2,256,256]{2,1,0:T(8,128)(2,1)S(1)} %copy-done.6, bf16[2,256,256]{2,1,0:T(8,128)(2,1)S(1)} %copy-done.3, ...), custom_call_target="tpu_custom_call" | custom-call | flops 1048576 | bytes 1024 | tf_op jit(solution)/shard_map/near/pallas_call | solution.py:27
  17.6 2.4 %far.3 = (bf16[2,512,256]{2,1,0:T(8,128)(2,1)S(1)}, bf16[2,2,128,256]{3,2,1,0:T(8,128)(2,1)}, bf16[2,2,128,256]{3,2,1,0:T(8,128)(2,1)S(1)}) custom-call(s32[1,2,2]{2,1,0:T(2,128)S(1)} %copy-done.15, s32[1,2,2]{2,1,0:T(2,128)S(1)} %copy-done.14, bf16[2,512,256]{2,1,0:T(8,128)(2,1)S(1)} %get-tuple-element.24.refs_2_, ...), custom_call_target="tpu_custom_call" | custom-call | flops 1048576 | bytes 1024 | tf_op jit(solution)/shard_map/far/pallas_call | solution.py:27
  19.9 1.6 %collective-permute-start.5 = (bf16[2,2,128,256]{3,2,1,0:T(8,128)(2,1)S(1)}, bf16[2,2,128,256]{3,2,1,0:T(8,128)(2,1)}, u32[]{:S(2)}, u32[]{:S(2)}) collective-permute-start(bf16[2,2,128,256]{3,2,1,0:T(8,128)(2,1)S(1)} %get-tuple-element.34), channel_id=1, source_target_pairs={{0,2},{1,3},{2,0},{3,1},{4,6},{5,7},{6,4},{7,5},{8,10},{9,11},{10,... | collective-permute-start | bytes 786440 | tf_op jit(solution)/shard_map/ppermute | solution.py:254
  21.5 1.6 %near.3.refs_13_.refs_6_ = f32[2,512,256]{2,1,0:T(8,128)S(1)} custom-call(s32[4,4]{1,0:T(4,128)S(1)} %copy-done.12, bf16[2,512,256]{2,1,0:T(8,128)(2,1)S(1)} %get-tuple-element.32.refs_1_.refs_3_, f32[2,256]{1,0:T(2,128)S(1)} %copy-done.13, bf16[2,256,256]{2,1,0:T(8,128)(2,1)S(1)} %copy-done.7, bf16[2,256,256]{2,1,0:T(8,128)(2,1)S(1)} %copy-done.3, ...), custom_call_target="tpu_custom_call" | custom-call | flops 1048576 | bytes 1024 | tf_op jit(solution)/shard_map/near/pallas_call | solution.py:27
  23.2 4.3 %finish.2 = (bf16[512,256]{1,0:T(8,128)(2,1)}, f32[2,512,256]{2,1,0:T(8,128)}) custom-call(s32[1,2,2]{2,1,0:T(2,128)S(1)} %copy-done.15, f32[2]{0:T(128)S(1)} %copy-done.18, f32[2]{0:T(128)S(1)} %copy-done.19, bf16[2,512,256]{2,1,0:T(8,128)(2,1)S(1)} %get-tuple-element.31.refs_1_.refs_3_, bf16[2,2,128,256]{3,2,1,0:T(8,128)(2,1)S(1)} %collective-permute-done.6.refs_4_, ...), custom_call_target="tpu_custom_call" | custom-call | flops 34359738368 | bytes 1024 | tf_op jit(solution)/shard_map/finish/pallas_call | solution.py:27
  27.5 8.5 %all-to-all-start.2 = ((bf16[8,64,256]{2,1,0:T(8,128)(2,1)}), bf16[8,64,256]{2,1,0:T(8,128)(2,1)S(1)}, u32[]{:S(2)}, u32[]{:S(2)}) async-start(bf16[8,64,256]{2,1,0:T(8,128)(2,1)} %bitcast.2), calls=%async_computation.2 | async-start | bytes 524288 | tf_op jit(solution)/shard_map/all_to_all | solution.py:264
  36.9 5.4 %finish.3 = (bf16[512,256]{1,0:T(8,128)(2,1)}, f32[2,512,256]{2,1,0:T(8,128)}) custom-call(s32[1,2,2]{2,1,0:T(2,128)S(1)} %copy-done.15, f32[2]{0:T(128)S(1)} %copy-done.18, f32[2]{0:T(128)S(1)} %copy-done.19, bf16[2,512,256]{2,1,0:T(8,128)(2,1)S(1)} %get-tuple-element.32.refs_1_.refs_3_, bf16[2,2,128,256]{3,2,1,0:T(8,128)(2,1)S(1)} %collective-permute-done.4.refs_4_, ...), custom_call_target="tpu_custom_call" | custom-call | flops 34359738368 | bytes 1024 | tf_op jit(solution)/shard_map/finish/pallas_call | solution.py:27
  42.3 5.9 %all-to-all-done.2.refs_0_ = bf16[8,64,256]{2,1,0:T(8,128)(2,1)S(1)} async-done(((bf16[8,64,256]{2,1,0:T(8,128)(2,1)}), bf16[8,64,256]{2,1,0:T(8,128)(2,1)S(1)}, u32[]{:S(2)}, u32[]{:S(2)}) %all-to-all-start.2) | async-done | bytes 262176 | tf_op jit(solution)/shard_map/all_to_all | solution.py:264
  48.2 3.4 %all-to-all-start = ((bf16[8,64,256]{2,1,0:T(8,128)(2,1)}), bf16[8,64,256]{2,1,0:T(8,128)(2,1)S(1)}, u32[]{:S(2)}, u32[]{:S(2)}) async-start(bf16[8,64,256]{2,1,0:T(8,128)(2,1)} %bitcast), calls=%async_computation | async-start | bytes 524288 | tf_op jit(solution)/shard_map/all_to_all | solution.py:264
  52.3 4.8 %collective-permute-start.12 = (bf16[64,256]{1,0:T(8,128)(2,1)S(1)}, bf16[64,256]{1,0:T(8,128)(2,1)S(1)}, u32[]{:S(2)}, u32[]{:S(2)}) collective-permute-start(bf16[64,256]{1,0:T(8,128)(2,1)S(1)} %row_total.3), channel_id=1, source_target_pairs={{0,128},{8,136},{16,144},{24,152},{32,160},{40,168},{48,176},{56,1... | collective-permute-start | bytes 98312 | tf_op jit(solution)/shard_map/ppermute | solution.py:269
  57.2 1.9 %collective-permute-start.11 = (bf16[64,256]{1,0:T(8,128)(2,1)S(1)}, bf16[64,256]{1,0:T(8,128)(2,1)S(1)}, u32[]{:S(2)}, u32[]{:S(2)}) collective-permute-start(bf16[64,256]{1,0:T(8,128)(2,1)S(1)} %row_total.3), channel_id=1, source_target_pairs={{0,64},{8,72},{16,80},{24,88},{32,96},{40,104},{48,112},{56,120},{... | collective-permute-start | bytes 98312 | tf_op jit(solution)/shard_map/ppermute | solution.py:269
  59.1 3.9 %collective-permute-done.11.refs_1_ = bf16[64,256]{1,0:T(8,128)(2,1)S(1)} collective-permute-done((bf16[64,256]{1,0:T(8,128)(2,1)S(1)}, bf16[64,256]{1,0:T(8,128)(2,1)S(1)}, u32[]{:S(2)}, u32[]{:S(2)}) %collective-permute-start.11) | collective-permute-done | bytes 32800 | tf_op jit(solution)/shard_map/ppermute | solution.py:269
  63.7 7.1 %all-to-all-start.3 = ((bf16[8,64,256]{2,1,0:T(8,128)(2,1)}), bf16[8,64,256]{2,1,0:T(8,128)(2,1)S(1)}, u32[]{:S(2)}, u32[]{:S(2)}) async-start(bf16[8,64,256]{2,1,0:T(8,128)(2,1)} %row_prefix.3), calls=%async_computation.3 | async-start | bytes 524288 | tf_op jit(solution)/shard_map/all_to_all | solution.py:274
  71.6 2.1 %collective-permute-start.9 = (bf16[64,256]{1,0:T(8,128)(2,1)S(1)}, bf16[64,256]{1,0:T(8,128)(2,1)S(1)}, u32[]{:S(2)}, u32[]{:S(2)}) collective-permute-start(bf16[64,256]{1,0:T(8,128)(2,1)S(1)} %row_total.2), channel_id=1, source_target_pairs={{0,128},{8,136},{16,144},{24,152},{32,160},{40,168},{48,176},{56,1... | collective-permute-start | bytes 98312 | tf_op jit(solution)/shard_map/ppermute | solution.py:269
  73.7 1.9 %collective-permute-start.8 = (bf16[64,256]{1,0:T(8,128)(2,1)S(1)}, bf16[64,256]{1,0:T(8,128)(2,1)S(1)}, u32[]{:S(2)}, u32[]{:S(2)}) collective-permute-start(bf16[64,256]{1,0:T(8,128)(2,1)S(1)} %row_total.2), channel_id=1, source_target_pairs={{0,64},{8,72},{16,80},{24,88},{32,96},{40,104},{48,112},{56,120},{... | collective-permute-start | bytes 98312 | tf_op jit(solution)/shard_map/ppermute | solution.py:269
  75.7 3.9 %collective-permute-done.8.refs_1_ = bf16[64,256]{1,0:T(8,128)(2,1)S(1)} collective-permute-done((bf16[64,256]{1,0:T(8,128)(2,1)S(1)}, bf16[64,256]{1,0:T(8,128)(2,1)S(1)}, u32[]{:S(2)}, u32[]{:S(2)}) %collective-permute-start.8) | collective-permute-done | bytes 32800 | tf_op jit(solution)/shard_map/ppermute | solution.py:269
  81.3 6.3 %all-to-all-start.1 = ((bf16[8,64,256]{2,1,0:T(8,128)(2,1)}), bf16[8,64,256]{2,1,0:T(8,128)(2,1)S(1)}, u32[]{:S(2)}, u32[]{:S(2)}) async-start(bf16[8,64,256]{2,1,0:T(8,128)(2,1)} %row_prefix.2), calls=%async_computation.1 | async-start | bytes 524288 | tf_op jit(solution)/shard_map/all_to_all | solution.py:274
  88.7 9.4 %all-to-all-done.1 = bf16[8,64,256]{2,1,0:T(8,128)(2,1)S(1)} async-done(((bf16[8,64,256]{2,1,0:T(8,128)(2,1)}), bf16[8,64,256]{2,1,0:T(8,128)(2,1)S(1)}, u32[]{:S(2)}, u32[]{:S(2)}) %all-to-all-start.1) | async-done | bytes 262176 | tf_op jit(solution)/shard_map/all_to_all | solution.py:274
  (67 shorter events, 13.2 us)
Async XLA Ops:
  2.9 8.7 %collective-permute-start.2 = (bf16[2,2,128,256]{3,2,1,0:T(8,128)(2,1)S(1)}, bf16[2,2,128,256]{3,2,1,0:T(8,128)(2,1)S(1)}, u32[]{:S(2)}, u32[]{:S(2)}) collective-permute-start(bf16[2,2,128,256]{3,2,1,0:T(8,128)(2,1)S(1)} %get-tuple-element.29), channel_id=1, source_target_pairs={{0,1},{1,0},{2,3},{3,2},{4,5},{5,4},{6,7},{7,6},{8,9},{9,8},{10,11... | collective-permute-start | bytes 786440 | tf_op jit(solution)/shard_map/ppermute | solution.py:243
  3.0 9.2 %collective-permute-start.3 = (bf16[2,2,128,256]{3,2,1,0:T(8,128)(2,1)S(1)}, bf16[2,2,128,256]{3,2,1,0:T(8,128)(2,1)S(1)}, u32[]{:S(2)}, u32[]{:S(2)}) collective-permute-start(bf16[2,2,128,256]{3,2,1,0:T(8,128)(2,1)S(1)} %get-tuple-element.30), channel_id=1, source_target_pairs={{0,2},{1,3},{2,0},{3,1},{4,6},{5,7},{6,4},{7,5},{8,10},{9,11},{10,... | collective-permute-start | bytes 786440 | tf_op jit(solution)/shard_map/ppermute | solution.py:243
  4.6 12.6 %collective-permute-start = (bf16[2,2,128,256]{3,2,1,0:T(8,128)(2,1)S(1)}, bf16[2,2,128,256]{3,2,1,0:T(8,128)(2,1)S(1)}, u32[]{:S(2)}, u32[]{:S(2)}) collective-permute-start(bf16[2,2,128,256]{3,2,1,0:T(8,128)(2,1)S(1)} %get-tuple-element.25), channel_id=1, source_target_pairs={{0,1},{1,0},{2,3},{3,2},{4,5},{5,4},{6,7},{7,6},{8,9},{9,8},{10,11... | collective-permute-start | bytes 786440 | tf_op jit(solution)/shard_map/ppermute | solution.py:243
  4.8 12.8 %collective-permute-start.1 = (bf16[2,2,128,256]{3,2,1,0:T(8,128)(2,1)S(1)}, bf16[2,2,128,256]{3,2,1,0:T(8,128)(2,1)S(1)}, u32[]{:S(2)}, u32[]{:S(2)}) collective-permute-start(bf16[2,2,128,256]{3,2,1,0:T(8,128)(2,1)S(1)} %get-tuple-element.26), channel_id=1, source_target_pairs={{0,2},{1,3},{2,0},{3,1},{4,6},{5,7},{6,4},{7,5},{8,10},{9,11},{10,... | collective-permute-start | bytes 786440 | tf_op jit(solution)/shard_map/ppermute | solution.py:243
  11.6 4.0 %copy-start.5 = (bf16[4,4,128,128]{3,2,1,0:T(8,128)(2,1)S(1)}, bf16[4,4,128,128]{3,2,1,0:T(8,128)(2,1)}, u32[]{:S(2)}) copy-start(bf16[4,4,128,128]{3,2,1,0:T(8,128)(2,1)} %refs_5_.7) | copy-start | bytes 1572868
  13.9 9.2 %collective-permute-start.6 = (bf16[2,2,128,256]{3,2,1,0:T(8,128)(2,1)S(1)}, bf16[2,2,128,256]{3,2,1,0:T(8,128)(2,1)S(1)}, u32[]{:S(2)}, u32[]{:S(2)}) collective-permute-start(bf16[2,2,128,256]{3,2,1,0:T(8,128)(2,1)S(1)} %get-tuple-element.35), channel_id=1, source_target_pairs={{0,1},{1,0},{2,3},{3,2},{4,5},{5,4},{6,7},{7,6},{8,9},{9,8},{10,11... | collective-permute-start | bytes 786440 | tf_op jit(solution)/shard_map/ppermute | solution.py:254
  14.0 9.1 %collective-permute-start.7 = (bf16[2,2,128,256]{3,2,1,0:T(8,128)(2,1)S(1)}, bf16[2,2,128,256]{3,2,1,0:T(8,128)(2,1)S(1)}, u32[]{:S(2)}, u32[]{:S(2)}) collective-permute-start(bf16[2,2,128,256]{3,2,1,0:T(8,128)(2,1)S(1)} %get-tuple-element.36), channel_id=1, source_target_pairs={{0,2},{1,3},{2,0},{3,1},{4,6},{5,7},{6,4},{7,5},{8,10},{9,11},{10,... | collective-permute-start | bytes 786440 | tf_op jit(solution)/shard_map/ppermute | solution.py:254
  17.2 4.3 %copy-start.7 = (bf16[2,256,256]{2,1,0:T(8,128)(2,1)S(1)}, bf16[2,256,256]{2,1,0:T(8,128)(2,1)}, u32[]{:S(2)}) copy-start(bf16[2,256,256]{2,1,0:T(8,128)(2,1)} %refs_3_.7) | copy-start | bytes 786436
  19.9 3.2 %copy-start.18 = (f32[2]{0:T(128)S(1)}, f32[2]{0:T(128)}, u32[]{:S(2)}) copy-start(f32[2]{0:T(128)} %refs_1_.13) | copy-start | bytes 28
  19.9 3.2 %copy-start.19 = (f32[2]{0:T(128)S(1)}, f32[2]{0:T(128)}, u32[]{:S(2)}) copy-start(f32[2]{0:T(128)} %refs_2_.11) | copy-start | bytes 28
  19.9 16.1 %collective-permute-start.4 = (bf16[2,2,128,256]{3,2,1,0:T(8,128)(2,1)}, bf16[2,2,128,256]{3,2,1,0:T(8,128)(2,1)S(1)}, u32[]{:S(2)}, u32[]{:S(2)}) collective-permute-start(bf16[2,2,128,256]{3,2,1,0:T(8,128)(2,1)} %get-tuple-element.33), channel_id=1, source_target_pairs={{0,1},{1,0},{2,3},{3,2},{4,5},{5,4},{6,7},{7,6},{8,9},{9,8},{10,11... | collective-permute-start | bytes 786440 | tf_op jit(solution)/shard_map/ppermute | solution.py:254
  19.9 16.1 %collective-permute-start.5 = (bf16[2,2,128,256]{3,2,1,0:T(8,128)(2,1)S(1)}, bf16[2,2,128,256]{3,2,1,0:T(8,128)(2,1)}, u32[]{:S(2)}, u32[]{:S(2)}) collective-permute-start(bf16[2,2,128,256]{3,2,1,0:T(8,128)(2,1)S(1)} %get-tuple-element.34), channel_id=1, source_target_pairs={{0,2},{1,3},{2,0},{3,1},{4,6},{5,7},{6,4},{7,5},{8,10},{9,11},{10,... | collective-permute-start | bytes 786440 | tf_op jit(solution)/shard_map/ppermute | solution.py:254
  27.5 20.7 %all-to-all-start.2 = ((bf16[8,64,256]{2,1,0:T(8,128)(2,1)}), bf16[8,64,256]{2,1,0:T(8,128)(2,1)S(1)}, u32[]{:S(2)}, u32[]{:S(2)}) async-start(bf16[8,64,256]{2,1,0:T(8,128)(2,1)} %bitcast.2), calls=%async_computation.2 | async-start | bytes 524288 | tf_op jit(solution)/shard_map/all_to_all | solution.py:264
  42.3 45.4 %copy-start.9 = (f32[2,512,256]{2,1,0:T(8,128)S(1)}, f32[2,512,256]{2,1,0:T(8,128)}, u32[]{:S(2)}) copy-start(f32[2,512,256]{2,1,0:T(8,128)} %get-tuple-element.40.run_ref) | copy-start | bytes 3145732
  48.2 15.5 %all-to-all-start = ((bf16[8,64,256]{2,1,0:T(8,128)(2,1)}), bf16[8,64,256]{2,1,0:T(8,128)(2,1)S(1)}, u32[]{:S(2)}, u32[]{:S(2)}) async-start(bf16[8,64,256]{2,1,0:T(8,128)(2,1)} %bitcast), calls=%async_computation | async-start | bytes 524288 | tf_op jit(solution)/shard_map/all_to_all | solution.py:264
  51.7 7.4 %collective-permute-start.13 = (bf16[64,256]{1,0:T(8,128)(2,1)S(1)}, bf16[64,256]{1,0:T(8,128)(2,1)S(1)}, u32[]{:S(2)}, u32[]{:S(2)}) collective-permute-start(bf16[64,256]{1,0:T(8,128)(2,1)S(1)} %row_total.3), channel_id=1, source_target_pairs={{0,192},{8,200},{16,208},{24,216},{32,224},{40,232},{48,240},{56,2... | collective-permute-start | bytes 98312 | tf_op jit(solution)/shard_map/ppermute | solution.py:269
  52.3 6.8 %collective-permute-start.12 = (bf16[64,256]{1,0:T(8,128)(2,1)S(1)}, bf16[64,256]{1,0:T(8,128)(2,1)S(1)}, u32[]{:S(2)}, u32[]{:S(2)}) collective-permute-start(bf16[64,256]{1,0:T(8,128)(2,1)S(1)} %row_total.3), channel_id=1, source_target_pairs={{0,128},{8,136},{16,144},{24,152},{32,160},{40,168},{48,176},{56,1... | collective-permute-start | bytes 98312 | tf_op jit(solution)/shard_map/ppermute | solution.py:269
  57.2 5.8 %collective-permute-start.11 = (bf16[64,256]{1,0:T(8,128)(2,1)S(1)}, bf16[64,256]{1,0:T(8,128)(2,1)S(1)}, u32[]{:S(2)}, u32[]{:S(2)}) collective-permute-start(bf16[64,256]{1,0:T(8,128)(2,1)S(1)} %row_total.3), channel_id=1, source_target_pairs={{0,64},{8,72},{16,80},{24,88},{32,96},{40,104},{48,112},{56,120},{... | collective-permute-start | bytes 98312 | tf_op jit(solution)/shard_map/ppermute | solution.py:269
  63.7 17.6 %all-to-all-start.3 = ((bf16[8,64,256]{2,1,0:T(8,128)(2,1)}), bf16[8,64,256]{2,1,0:T(8,128)(2,1)S(1)}, u32[]{:S(2)}, u32[]{:S(2)}) async-start(bf16[8,64,256]{2,1,0:T(8,128)(2,1)} %row_prefix.3), calls=%async_computation.3 | async-start | bytes 524288 | tf_op jit(solution)/shard_map/all_to_all | solution.py:274
  70.9 4.7 %collective-permute-start.10 = (bf16[64,256]{1,0:T(8,128)(2,1)S(1)}, bf16[64,256]{1,0:T(8,128)(2,1)S(1)}, u32[]{:S(2)}, u32[]{:S(2)}) collective-permute-start(bf16[64,256]{1,0:T(8,128)(2,1)S(1)} %row_total.2), channel_id=1, source_target_pairs={{0,192},{8,200},{16,208},{24,216},{32,224},{40,232},{48,240},{56,2... | collective-permute-start | bytes 98312 | tf_op jit(solution)/shard_map/ppermute | solution.py:269
  71.6 4.1 %collective-permute-start.9 = (bf16[64,256]{1,0:T(8,128)(2,1)S(1)}, bf16[64,256]{1,0:T(8,128)(2,1)S(1)}, u32[]{:S(2)}, u32[]{:S(2)}) collective-permute-start(bf16[64,256]{1,0:T(8,128)(2,1)S(1)} %row_total.2), channel_id=1, source_target_pairs={{0,128},{8,136},{16,144},{24,152},{32,160},{40,168},{48,176},{56,1... | collective-permute-start | bytes 98312 | tf_op jit(solution)/shard_map/ppermute | solution.py:269
  73.7 5.8 %collective-permute-start.8 = (bf16[64,256]{1,0:T(8,128)(2,1)S(1)}, bf16[64,256]{1,0:T(8,128)(2,1)S(1)}, u32[]{:S(2)}, u32[]{:S(2)}) collective-permute-start(bf16[64,256]{1,0:T(8,128)(2,1)S(1)} %row_total.2), channel_id=1, source_target_pairs={{0,64},{8,72},{16,80},{24,88},{32,96},{40,104},{48,112},{56,120},{... | collective-permute-start | bytes 98312 | tf_op jit(solution)/shard_map/ppermute | solution.py:269
  80.3 17.8 %copy-start.10 = (f32[2,512,256]{2,1,0:T(8,128)S(1)}, f32[2,512,256]{2,1,0:T(8,128)}, u32[]{:S(2)}) copy-start(f32[2,512,256]{2,1,0:T(8,128)} %get-tuple-element.38.run_ref) | copy-start | bytes 3145732
  81.3 16.8 %all-to-all-start.1 = ((bf16[8,64,256]{2,1,0:T(8,128)(2,1)}), bf16[8,64,256]{2,1,0:T(8,128)(2,1)S(1)}, u32[]{:S(2)}, u32[]{:S(2)}) async-start(bf16[8,64,256]{2,1,0:T(8,128)(2,1)} %row_prefix.2), calls=%async_computation.1 | async-start | bytes 524288 | tf_op jit(solution)/shard_map/all_to_all | solution.py:274
  (14 other events, 27.8 us)

commit v3 on v2

v3 whole, which is shorter than its diff:
```python
import jax
import jax.numpy as jnp
from jax import lax
from jax.experimental import pallas as pl
from jax.experimental.pallas import tpu as pltpu
from jax.sharding import PartitionSpec as P

F32 = jnp.float32
BF16 = jnp.bfloat16


def dot(a, b):
    return jnp.dot(a, b, preferred_element_type=F32)


def call(body, name, outs, scalars, arrays, far_arrays=(), far_outs=(), after=(), scratch=(), aliases=None):
    pin = lambda a: pltpu.with_memory_space_constraint(a, pltpu.VMEM)
    keep = lambda a: pltpu.with_memory_space_constraint(a, pltpu.HBM)
    count = len(scalars) + len(arrays) + len(far_arrays)
    vmem = pl.BlockSpec(memory_space=pltpu.VMEM)

    def inner(*refs):
        body(*refs[:count], *refs[count + len(after) :])

    return pl.pallas_call(
        inner,
        out_shape=[pltpu.VMEM(*o) for o in outs] + [pltpu.HBM(*o) for o in far_outs],
        in_specs=[pl.BlockSpec(memory_space=pltpu.SMEM)] * len(scalars)
        + [vmem] * len(arrays)
        + [pl.BlockSpec(memory_space=pltpu.HBM)] * len(far_arrays)
        + [vmem] * len(after),
        out_specs=[vmem] * len(outs) + [pl.BlockSpec(memory_space=pltpu.HBM)] * len(far_outs),
        scratch_shapes=list(scratch),
        input_output_aliases=aliases or {},
        compiler_params=pltpu.CompilerParams(vmem_limit_bytes=12 << 20),
        cost_estimate=pl.CostEstimate(flops=1 << 20, transcendentals=0, bytes_accessed=1 << 10),
        name=name,
    )(*scalars, *map(pin, arrays), *map(keep, far_arrays), *map(pin, after))


def pack(iterates, shower, send_blocks, block):
    steps, _, cells, width = iterates.shape
    rounds, sent = send_blocks.shape[1:]

    def body(blocks_hbm, it_hbm, *refs):
        send_refs, (blocks_ref, it_ref, sems) = refs[:rounds], refs[rounds:]
        index = pltpu.make_async_copy(blocks_hbm, blocks_ref, sems.at[steps])
        index.start()
        loads = [pltpu.make_async_copy(it_hbm.at[step, shower], it_ref.at[step], sems.at[step]) for step in range(steps)]
        for load in loads:
            load.start()
        index.wait()
        for step in range(steps):
            loads[step].wait()
            for r in range(rounds):
                for k in range(sent):
                    at = pl.ds(blocks_ref[0, r, k] * block, block)
                    send_refs[r][step, k] = it_ref[step, at, :].astype(BF16)

    return call(
        body, "pack", [((steps, sent, block, width), BF16)] * rounds, [], [], [send_blocks, iterates],
        scratch=[
            pltpu.SMEM(send_blocks.shape, jnp.int32), pltpu.VMEM((steps, cells, width), F32),
            pltpu.SemaphoreType.DMA((steps + 1,)),
        ],
    )


def near_step(col_ref, h_ref, emb_ref, ws, wn, tile_ref, pre_ref, step):
    parts, per_row, block, _ = tile_ref.shape
    mixed = []
    for b in range(parts):
        wide = jnp.concatenate([tile_ref[b, j] for j in range(per_row)], axis=1)
        tall = jnp.concatenate(
            [h_ref[step, pl.ds(col_ref[b, j] * block, block), :] for j in range(per_row)], axis=0
        )
        mixed.append(dot(wide, tall).astype(BF16))
    pre = dot(h_ref[step], ws) + dot(jnp.concatenate(mixed, axis=0), wn)
    pre_ref[step] = pre + emb_ref[step : step + 1, :]


def near(hidden, layer, embed, weight, neighbor, columns, tiles, after):
    steps, cells, width = hidden.shape

    def body(col_ref, h_ref, emb_ref, ws_ref, wn_ref, tile_ref, pre_ref):
        for step in range(steps):
            near_step(col_ref, h_ref, emb_ref, ws_ref[layer], wn_ref[layer], tile_ref, pre_ref, step)

    return call(
        body, "near", [((steps, cells, width), F32)], [columns], [hidden, embed, weight, neighbor, tiles], after=after
    )[0]


def near_first(iterates, shower, embed, weight, neighbor, columns, tiles, after):
    steps, _, cells, width = iterates.shape

    def body(col_ref, it_ref, emb_ref, ws_ref, wn_ref, tile_ref, pre_ref, h_ref):
        for step in range(steps):
            h_ref[step] = it_ref[step, shower].astype(BF16)
        for step in range(steps):
            near_step(col_ref, h_ref, emb_ref, ws_ref[0], wn_ref[0], tile_ref, pre_ref, step)

    return call(
        body, "near_first", [((steps, cells, width), F32), ((steps, cells, width), BF16)], [columns],
        [iterates, embed, weight, neighbor, tiles], after=after,
    )


def update(recv_ref, h_ref, in_refs, pre_ref, wn, wo, rem_ref, step):
    sent, block = in_refs[0].shape[1:3]
    parts = h_ref.shape[1] // block
    addends = [
        (recv_ref[0, r, k], dot(rem_ref[0, r, k], in_ref[step, k])) for r, in_ref in enumerate(in_refs) for k in range(sent)
    ]
    mixed = []
    for b in range(parts):
        total = None
        for row, addend in addends:
            term = jnp.where(row == b, 1.0, 0.0) * addend
            total = term if total is None else total + term
        mixed.append(total.astype(BF16))
    half = 0.5 * (pre_ref[step] + dot(jnp.concatenate(mixed, axis=0), wn))
    activated = (half + half * jnp.tanh(half)).astype(BF16)
    return (h_ref[step].astype(F32) + dot(activated, wo)).astype(BF16)


def far(hidden, incoming, pre, layer, neighbor, output, remote, receive, send_blocks, after):
    steps, cells, width = hidden.shape
    rounds, sent = send_blocks.shape[1:]
    block = incoming[0].shape[2]

    def body(recv_ref, blocks_ref, h_ref, *refs):
        in_refs, (pre_ref, wn_ref, wo_ref, rem_ref, out_ref, *send_refs) = refs[:rounds], refs[rounds:]
        for step in range(steps):
            out_ref[step] = update(recv_ref, h_ref, in_refs, pre_ref, wn_ref[layer], wo_ref[layer], rem_ref, step)
        for r in range(rounds):
            for k in range(sent):
                at = pl.ds(blocks_ref[0, r, k] * block, block)
                for step in range(steps):
                    send_refs[r][step, k] = out_ref[step, at, :]

    outs = [((steps, cells, width), BF16)] + [((steps, sent, block, width), BF16)] * rounds
    return call(
        body, "far", outs, [receive, send_blocks], [hidden, *incoming, pre, neighbor, output, remote], after=after
    )


def noise_sums(noise, scale, iterates, after):
    steps, showers, cells, width = noise.shape

    def body(scale_ref, nz_hbm, it_hbm, *refs):
        out_refs, (nz_ref, it_ref, sems) = refs[:showers], refs[showers:]
        loads = [pltpu.make_async_copy(it_hbm.at[0], it_ref, sems.at[0]), pltpu.make_async_copy(nz_hbm, nz_ref, sems.at[1])]
        for load in loads:
            load.start()
        for load in loads:
            load.wait()
        first = jnp.where(lax.axis_index("tm") == 0, 1.0, 0.0)
        for shower in range(showers):
            total = first * it_ref[shower]
            for step in range(steps):
                total = total + scale_ref[step] * nz_ref[step, shower].astype(F32)
                out_refs[shower][step] = total

    return call(
        body, "noise_sums", [((steps, cells, width), F32)] * showers, [scale], [], [noise, iterates], after=after,
        scratch=[
            pltpu.VMEM(noise.shape, BF16), pltpu.VMEM(iterates.shape[1:], F32), pltpu.SemaphoreType.DMA((2,)),
        ],
    )


def finish(hidden, incoming, pre, layer, shower, showers, neighbor, output, remote, receive, drift_weight, scale, noise_sum, totals, after):
    steps, cells, width = hidden.shape
    rounds = len(incoming)

    def body(recv_ref, scale_ref, h_ref, *refs):
        in_refs, (pre_ref, wn_ref, wo_ref, rem_ref, wd_ref, nz_ref, *_, tot_ref, run_ref) = refs[:rounds], refs[rounds:]
        drift = None
        for step in range(steps):
            last = update(recv_ref, h_ref, in_refs, pre_ref, wn_ref[layer], wo_ref[layer], rem_ref, step)
            term = scale_ref[step] * dot(last, wd_ref[...])
            drift = term if drift is None else drift + term
            run = drift + nz_ref[step]
            run_ref[step] = run
        tot_ref[shower] = run.astype(BF16)

    arrays = [hidden, *incoming, pre, neighbor, output, remote, drift_weight, noise_sum, *totals]
    return call(
        body, "finish", [((showers, cells, width), BF16), ((steps, cells, width), F32)], [receive, scale], arrays,
        after=after, aliases={len(arrays) + 1: 0} if totals else None,
    )


def exclusive_prefix(parts):
    def body(p_ref, o_ref):
        total = jnp.zeros(parts.shape[1:], F32)
        for k in range(parts.shape[0]):
            o_ref[k] = total.astype(BF16)
            total = total + p_ref[k].astype(F32)

    return call(body, "exclusive_prefix", [(parts.shape, BF16)], [], [parts])[0]


def deliver(running, earlier):
    showers = len(running)
    steps, cells, width = running[0].shape
    every = [(step, shower) for step in range(steps) for shower in range(showers)]

    def body(*refs):
        run_refs, (early_ref, out_hbm, out_ref, sems) = refs[:showers], refs[showers:]
        stores = [
            pltpu.make_async_copy(out_ref.at[step, shower], out_hbm.at[step, shower], sems.at[i])
            for i, (step, shower) in enumerate(every)
        ]
        for i, (step, shower) in enumerate(every):
            out_ref[step, shower] = run_refs[shower][step] + early_ref[shower].astype(F32)
            stores[i].start()
        for store in stores:
            store.wait()

    shape = (steps, showers, cells, width)
    return call(
        body, "deliver", [], [], [*running, earlier], [], [(shape, F32)],
        scratch=[pltpu.VMEM(shape, F32), pltpu.SemaphoreType.DMA((len(every),))],
    )[0]


def local(
    iterates,
    noise_draws,
    drift_scale,
    noise_scale,
    step_embed,
    self_weight,
    neighbor_weight,
    output_weight,
    drift_weight,
    local_columns,
    tile_values,
    send_blocks,
    receive_rows,
    remote_values,
):
    steps, showers, cells, width = iterates.shape
    block = tile_values.shape[2]
    layers = self_weight.shape[0]
    parts = lax.axis_size("dom")
    pairs = [[(i, i ^ (1 << r)) for i in range(parts)] for r in range(2)]
    incoming = []
    for s in range(showers):
        sends = pack(iterates, s, send_blocks, block)
        incoming.append([lax.ppermute(sends[r], "dom", pairs[r]) for r in (0, 1)])
    common = (step_embed, self_weight, neighbor_weight, local_columns, tile_values)
    rest = (neighbor_weight, output_weight, remote_values, receive_rows)
    hidden, pre = [None] * showers, [None] * showers
    token = ()
    for s in range(showers):
        pre[s], hidden[s] = near_first(iterates, s, *common, token)
        token = (pre[s],)
    noise_sum = noise_sums(noise_draws, noise_scale, iterates, token)
    token = (noise_sum[0],)
    for layer in range(1, layers):
        for s in range(showers):
            hidden[s], *sends = far(hidden[s], incoming[s], pre[s], layer - 1, *rest, send_blocks, token)
            incoming[s] = [lax.ppermute(sends[r], "dom", pairs[r]) for r in (0, 1)]
            pre[s] = near(hidden[s], layer, *common, ())
            token = (pre[s],)
    totals, running = (), [None] * showers
    for s in range(showers):
        total, running[s] = finish(
            hidden[s], incoming[s], pre[s], layers - 1, s, showers, *rest, drift_weight, drift_scale, noise_sum[s],
            totals, token,
        )
        totals, token = (total,), ()
    pieces = lax.all_to_all(total.reshape(lax.axis_size("tm"), -1, width), "tm", 0, 0)
    earlier = lax.all_to_all(exclusive_prefix(pieces), "tm", 0, 0)
    return deliver(running, earlier.reshape(showers, cells, width))


def solution(mesh):
    return jax.shard_map(
        local,
        mesh=mesh,
        in_specs=(
            P("tm", None, "dom", None),
            P("tm", None, "dom", None),
            P("tm"),
            P("tm"),
            P("tm", None),
            P(),
            P(),
            P(),
            P(),
            P("dom", None),
            P("dom", None, None, None),
            P("dom", None, None),
            P("dom", None, None),
            P("dom", None, None, None, None),
        ),
        out_specs=P("tm", None, "dom", None),
        check_vma=False,
    )
```

time: 100 us -> 81.1 us (0.81)
  the two profiles are of different devices: /device:TPU:8 before, /device:TPU:2 now
where the time goes in v3:
time: 81.1 us; the launch traced here: 80.6 us
  blocking collectives  49.5 us (61%)
  Pallas kernels  19.9 us (25%)
  starting transfers between devices  6.77 us (8%)
  waiting for transfers between devices  3.94 us (5%)
    all_to_all x1, blocking collectives, local(): lax.all_to_all(total.reshape(lax.axis_size('tm'), -1, width), 'tm', 0, 0)  27.7 us
    all_to_all x1, blocking collectives, local(): earlier = lax.all_to_all(exclusive_prefix(pieces), 'tm', 0, 0)  21.8 us
    pallas_call x13, Pallas kernels, call(): pl.pallas_call(inner, out_shape=[pltpu.VMEM(*o) for o in outs] + [pltpu.H...  19.9 us
    ppermute x4, waiting for transfers between devices, local(): incoming[s] = [lax.ppermute(sends[r], 'dom', pairs[r]) for r in (0, 1)]  3.93 us
    ppermute x4, starting transfers between devices, local(): incoming[s] = [lax.ppermute(sends[r], 'dom', pairs[r]) for r in (0, 1)]  3.84 us
    ppermute x4, starting transfers between devices, local(): incoming.append([lax.ppermute(sends[r], 'dom', pairs[r]) for r in (0, 1)])  2.93 us
  transfers between devices with their start and end apart: 8, of which 2 were waited for; matrix products, arithmetic and copies ran while one was open for 0% of the time, Pallas kernels for 19%

profile of v3, /device:TPU:2, one launch (start us, length us, event | category | flops | bytes accessed | tf_op | source)
XLA Modules:
  0.0 80.6 jit_solution(1502592868350321675)
XLA Ops:
  0.0 1.4 %pack.2 = (bf16[2,2,128,256]{3,2,1,0:T(8,128)(2,1)S(1)}, bf16[2,2,128,256]{3,2,1,0:T(8,128)(2,1)S(1)}) custom-call(s32[1,2,2]{2,1,0:T(2,128)} %refs_1_.15, f32[2,2,512,256]{3,2,1,0:T(8,128)} %refs_1_.14), custom_call_target="tpu_custom_call" | custom-call | flops 1048576 | bytes 1024 | tf_op jit(solution)/shard_map/pack/pallas_call | solution.py:25
  1.5 0.1 collective-permute-start
  1.6 2.3 %collective-permute-start.1 = (bf16[2,2,128,256]{3,2,1,0:T(8,128)(2,1)S(1)}, bf16[2,2,128,256]{3,2,1,0:T(8,128)(2,1)S(1)}, u32[]{:S(2)}, u32[]{:S(2)}) collective-permute-start(bf16[2,2,128,256]{3,2,1,0:T(8,128)(2,1)S(1)} %get-tuple-element.27), channel_id=1, source_target_pairs={{0,2},{1,3},{2,0},{3,1},{4,6},{5,7},{6,4},{7,5},{8,10},{9,11},{10,... | collective-permute-start | bytes 786440 | tf_op jit(solution)/shard_map/ppermute | solution.py:253
  3.9 1.3 %pack.3 = (bf16[2,2,128,256]{3,2,1,0:T(8,128)(2,1)S(1)}, bf16[2,2,128,256]{3,2,1,0:T(8,128)(2,1)S(1)}) custom-call(s32[1,2,2]{2,1,0:T(2,128)} %refs_1_.15, f32[2,2,512,256]{3,2,1,0:T(8,128)} %refs_1_.14), custom_call_target="tpu_custom_call" | custom-call | flops 1048576 | bytes 1024 | tf_op jit(solution)/shard_map/pack/pallas_call | solution.py:25
  5.2 0.2 collective-permute-start.4
  5.4 0.3 collective-permute-start.5
  5.7 1.6 %near_first.2 = (f32[2,512,256]{2,1,0:T(8,128)S(1)}, bf16[2,512,256]{2,1,0:T(8,128)(2,1)S(1)}) custom-call(s32[4,4]{1,0:T(4,128)S(1)} %copy-done.7, f32[2,2,512,256]{3,2,1,0:T(8,128)S(1)} %copy-done, f32[2,256]{1,0:T(2,128)S(1)} %copy-done.8, bf16[2,256,256]{2,1,0:T(8,128)(2,1)S(1)} %copy-done.3, bf16[2,256,256]{2,1,0:T(8,128)(2,1)S(1)} %copy-done.1, ...), custom_call_target="tpu_custom_call" | custom-call | flops 1048576 | bytes 1024 | tf_op jit(solution)/shard_map/near_first/pallas_call | solution.py:25
  7.3 1.6 %near_first.3 = (f32[2,512,256]{2,1,0:T(8,128)S(1)}, bf16[2,512,256]{2,1,0:T(8,128)(2,1)S(1)}) custom-call(s32[4,4]{1,0:T(4,128)S(1)} %copy-done.7, f32[2,2,512,256]{3,2,1,0:T(8,128)S(1)} %copy-done, f32[2,256]{1,0:T(2,128)S(1)} %copy-done.8, bf16[2,256,256]{2,1,0:T(8,128)(2,1)S(1)} %copy-done.3, bf16[2,256,256]{2,1,0:T(8,128)(2,1)S(1)} %copy-done.1, ...), custom_call_target="tpu_custom_call" | custom-call | flops 1048576 | bytes 1024 | tf_op jit(solution)/shard_map/near_first/pallas_call | solution.py:25
  9.0 2.4 %noise_sums.1 = (f32[2,512,256]{2,1,0:T(8,128)S(1)}, f32[2,512,256]{2,1,0:T(8,128)S(1)}) custom-call(f32[2]{0:T(128)S(1)} %copy-done.12, bf16[2,2,512,256]{3,2,1,0:T(8,128)(2,1)} %refs_1_.12, f32[2,2,512,256]{3,2,1,0:T(8,128)} %refs_1_.14, f32[2,512,256]{2,1,0:T(8,128)S(1)} %get-tuple-element.29.refs_3_.refs_5_), custom_call_target="tpu_custom_call" | custom-call | flops 1048576 | bytes 1024 | tf_op jit(solution)/shard_map/noise_sums/pallas_call | solution.py:25
  11.4 1.7 %far.2 = (bf16[2,512,256]{2,1,0:T(8,128)(2,1)S(1)}, bf16[2,2,128,256]{3,2,1,0:T(8,128)(2,1)S(1)}, bf16[2,2,128,256]{3,2,1,0:T(8,128)(2,1)S(1)}) custom-call(s32[1,2,2]{2,1,0:T(2,128)S(1)} %copy-done.10, s32[1,2,2]{2,1,0:T(2,128)S(1)} %copy-done.9, bf16[2,512,256]{2,1,0:T(8,128)(2,1)S(1)} %get-tuple-element.25.refs_2_, ...), custom_call_target="tpu_custom_call" | custom-call | flops 1048576 | bytes 1024 | tf_op jit(solution)/shard_map/far/pallas_call | solution.py:25
  13.1 0.2 collective-permute-start.2
  13.3 1.8 %collective-permute-start.3 = (bf16[2,2,128,256]{3,2,1,0:T(8,128)(2,1)S(1)}, bf16[2,2,128,256]{3,2,1,0:T(8,128)(2,1)S(1)}, u32[]{:S(2)}, u32[]{:S(2)}) collective-permute-start(bf16[2,2,128,256]{3,2,1,0:T(8,128)(2,1)S(1)} %get-tuple-element.33), channel_id=1, source_target_pairs={{0,2},{1,3},{2,0},{3,1},{4,6},{5,7},{6,4},{7,5},{8,10},{9,11},{10,... | collective-permute-start | bytes 786440 | tf_op jit(solution)/shard_map/ppermute | solution.py:266
  15.1 1.6 %near.2.refs_9_.refs_5_ = f32[2,512,256]{2,1,0:T(8,128)S(1)} custom-call(s32[4,4]{1,0:T(4,128)S(1)} %copy-done.7, bf16[2,512,256]{2,1,0:T(8,128)(2,1)S(1)} %get-tuple-element.31.refs_1_.refs_2_, f32[2,256]{1,0:T(2,128)S(1)} %copy-done.8, bf16[2,256,256]{2,1,0:T(8,128)(2,1)S(1)} %copy-done.3, bf16[2,256,256]{2,1,0:T(8,128)(2,1)S(1)} %copy-done.1, ...), custom_call_target="tpu_custom_call" | custom-call | flops 1048576 | bytes 1024 | tf_op jit(solution)/shard_map/near/pallas_call | solution.py:25
  16.6 1.7 %far.3 = (bf16[2,512,256]{2,1,0:T(8,128)(2,1)S(1)}, bf16[2,2,128,256]{3,2,1,0:T(8,128)(2,1)S(1)}, bf16[2,2,128,256]{3,2,1,0:T(8,128)(2,1)S(1)}) custom-call(s32[1,2,2]{2,1,0:T(2,128)S(1)} %copy-done.10, s32[1,2,2]{2,1,0:T(2,128)S(1)} %copy-done.9, bf16[2,512,256]{2,1,0:T(8,128)(2,1)S(1)} %get-tuple-element.34.refs_2_, ...), custom_call_target="tpu_custom_call" | custom-call | flops 1048576 | bytes 1024 | tf_op jit(solution)/shard_map/far/pallas_call | solution.py:25
  18.3 0.2 collective-permute-start.6
  18.6 1.6 %collective-permute-start.7 = (bf16[2,2,128,256]{3,2,1,0:T(8,128)(2,1)S(1)}, bf16[2,2,128,256]{3,2,1,0:T(8,128)(2,1)S(1)}, u32[]{:S(2)}, u32[]{:S(2)}) collective-permute-start(bf16[2,2,128,256]{3,2,1,0:T(8,128)(2,1)S(1)} %get-tuple-element.40), channel_id=1, source_target_pairs={{0,2},{1,3},{2,0},{3,1},{4,6},{5,7},{6,4},{7,5},{8,10},{9,11},{10,... | collective-permute-start | bytes 786440 | tf_op jit(solution)/shard_map/ppermute | solution.py:266
  20.2 1.6 %near.3.refs_11_.refs_5_ = f32[2,512,256]{2,1,0:T(8,128)S(1)} custom-call(s32[4,4]{1,0:T(4,128)S(1)} %copy-done.7, bf16[2,512,256]{2,1,0:T(8,128)(2,1)S(1)} %get-tuple-element.37.refs_1_.refs_2_, f32[2,256]{1,0:T(2,128)S(1)} %copy-done.8, bf16[2,256,256]{2,1,0:T(8,128)(2,1)S(1)} %copy-done.3, bf16[2,256,256]{2,1,0:T(8,128)(2,1)S(1)} %copy-done.1, ...), custom_call_target="tpu_custom_call" | custom-call | flops 1048576 | bytes 1024 | tf_op jit(solution)/shard_map/near/pallas_call | solution.py:25
  21.8 0.6 collective-permute-done.3.refs_4_
  22.4 1.9 %finish.2 = (bf16[2,512,256]{2,1,0:T(8,128)(2,1)S(1)}, f32[2,512,256]{2,1,0:T(8,128)S(1)}) custom-call(s32[1,2,2]{2,1,0:T(2,128)S(1)} %copy-done.10, f32[2]{0:T(128)S(1)} %copy-done.11, bf16[2,512,256]{2,1,0:T(8,128)(2,1)S(1)} %get-tuple-element.31.refs_1_.refs_2_, bf16[2,2,128,256]{3,2,1,0:T(8,128)(2,1)S(1)} %collective-permute-done.2.refs_3_, ...), custom_call_target="tpu_custom_call" | custom-call | flops 1048576 | bytes 1024 | tf_op jit(solution)/shard_map/finish/pallas_call | solution.py:25
  24.3 3.3 %collective-permute-done.7.refs_4_ = bf16[2,2,128,256]{3,2,1,0:T(8,128)(2,1)S(1)} collective-permute-done((bf16[2,2,128,256]{3,2,1,0:T(8,128)(2,1)S(1)}, bf16[2,2,128,256]{3,2,1,0:T(8,128)(2,1)S(1)}, u32[]{:S(2)}, u32[]{:S(2)}) %collective-permute-start.7) | collective-permute-done | bytes 262176 | tf_op jit(solution)/shard_map/ppermute | solution.py:266
  27.6 1.9 %finish.3 = (bf16[2,512,256]{2,1,0:T(8,128)(2,1)S(1)}, f32[2,512,256]{2,1,0:T(8,128)S(1)}) custom-call(s32[1,2,2]{2,1,0:T(2,128)S(1)} %copy-done.10, f32[2]{0:T(128)S(1)} %copy-done.11, bf16[2,512,256]{2,1,0:T(8,128)(2,1)S(1)} %get-tuple-element.37.refs_1_.refs_2_, ...), custom_call_target="tpu_custom_call", output_to_operand_aliasing={{0}: (11, {})} | custom-call | flops 1048576 | bytes 1024 | tf_op jit(solution)/shard_map/finish/pallas_call | solution.py:25
  29.5 27.7 %all_to_all.10.refs_0_ = bf16[32,32,256]{2,1,0:T(8,128)(2,1)S(1)} all-to-all(bf16[32,32,256]{2,1,0:T(8,128)(2,1)S(1)} %bitcast.3), channel_id=1, replica_groups=mesh['tm'=32,'dom'=8] {'tm'}, dimensions={0} | all-to-all | bytes 1048576 | tf_op jit(solution)/shard_map/all_to_all | solution.py:276
  57.3 21.8 %all_to_all.11 = bf16[32,32,256]{2,1,0:T(8,128)(2,1)S(1)} all-to-all(bf16[32,32,256]{2,1,0:T(8,128)(2,1)S(1)} %exclusive_prefix.1), channel_id=1, replica_groups=mesh['tm'=32,'dom'=8] {'tm'}, dimensions={0} | all-to-all | bytes 1048576 | tf_op jit(solution)/shard_map/all_to_all | solution.py:277
  79.1 1.4 %deliver.1 = f32[2,2,512,256]{3,2,1,0:T(8,128)} custom-call(f32[2,512,256]{2,1,0:T(8,128)S(1)} %get-tuple-element.38.refs_0_, f32[2,512,256]{2,1,0:T(8,128)S(1)} %get-tuple-element.43.refs_1_, bf16[2,512,256]{2,1,0:T(8,128)(2,1)S(1)} %bitcast.2), custom_call_target="tpu_custom_call" | custom-call | flops 1048576 | bytes 1024 | tf_op jit(solution)/shard_map/deliver/pallas_call | solution.py:25
  (33 shorter events, 0.2 us)
Async XLA Ops:
  0.0 5.7 %copy-start = (f32[2,2,512,256]{3,2,1,0:T(8,128)S(1)}, f32[2,2,512,256]{3,2,1,0:T(8,128)}, u32[]{:S(2)}) copy-start(f32[2,2,512,256]{3,2,1,0:T(8,128)} %refs_1_.14) | copy-start | bytes 6291460
  0.0 5.7 %copy-start.1 = (bf16[2,256,256]{2,1,0:T(8,128)(2,1)S(1)}, bf16[2,256,256]{2,1,0:T(8,128)(2,1)}, u32[]{:S(2)}) copy-start(bf16[2,256,256]{2,1,0:T(8,128)(2,1)} %refs_6_.7) | copy-start | bytes 786436
  0.0 5.7 %copy-start.2 = (bf16[4,4,128,128]{3,2,1,0:T(8,128)(2,1)S(1)}, bf16[4,4,128,128]{3,2,1,0:T(8,128)(2,1)}, u32[]{:S(2)}) copy-start(bf16[4,4,128,128]{3,2,1,0:T(8,128)(2,1)} %refs_5_.7) | copy-start | bytes 1572868
  0.0 5.7 %copy-start.7 = (s32[4,4]{1,0:T(4,128)S(1)}, s32[4,4]{1,0:T(4,128)}, u32[]{:S(2)}) copy-start(s32[4,4]{1,0:T(4,128)} %refs_0_.19) | copy-start | bytes 196
  0.0 5.7 %copy-start.3 = (bf16[2,256,256]{2,1,0:T(8,128)(2,1)S(1)}, bf16[2,256,256]{2,1,0:T(8,128)(2,1)}, u32[]{:S(2)}) copy-start(bf16[2,256,256]{2,1,0:T(8,128)(2,1)} %refs_3_.7) | copy-start | bytes 786436
  0.0 5.7 %copy-start.8 = (f32[2,256]{1,0:T(2,128)S(1)}, f32[2,256]{1,0:T(2,128)}, u32[]{:S(2)}) copy-start(f32[2,256]{1,0:T(2,128)} %refs_2_.9) | copy-start | bytes 6148
  1.5 9.9 %collective-permute-start = (bf16[2,2,128,256]{3,2,1,0:T(8,128)(2,1)S(1)}, bf16[2,2,128,256]{3,2,1,0:T(8,128)(2,1)S(1)}, u32[]{:S(2)}, u32[]{:S(2)}) collective-permute-start(bf16[2,2,128,256]{3,2,1,0:T(8,128)(2,1)S(1)} %get-tuple-element.26), channel_id=1, source_target_pairs={{0,1},{1,0},{2,3},{3,2},{4,5},{5,4},{6,7},{7,6},{8,9},{9,8},{10,11... | collective-permute-start | bytes 786440 | tf_op jit(solution)/shard_map/ppermute | solution.py:253
  1.6 9.8 %collective-permute-start.1 = (bf16[2,2,128,256]{3,2,1,0:T(8,128)(2,1)S(1)}, bf16[2,2,128,256]{3,2,1,0:T(8,128)(2,1)S(1)}, u32[]{:S(2)}, u32[]{:S(2)}) collective-permute-start(bf16[2,2,128,256]{3,2,1,0:T(8,128)(2,1)S(1)} %get-tuple-element.27), channel_id=1, source_target_pairs={{0,2},{1,3},{2,0},{3,1},{4,6},{5,7},{6,4},{7,5},{8,10},{9,11},{10,... | collective-permute-start | bytes 786440 | tf_op jit(solution)/shard_map/ppermute | solution.py:253
  5.2 11.5 %collective-permute-start.4 = (bf16[2,2,128,256]{3,2,1,0:T(8,128)(2,1)S(1)}, bf16[2,2,128,256]{3,2,1,0:T(8,128)(2,1)S(1)}, u32[]{:S(2)}, u32[]{:S(2)}) collective-permute-start(bf16[2,2,128,256]{3,2,1,0:T(8,128)(2,1)S(1)} %get-tuple-element.35), channel_id=1, source_target_pairs={{0,1},{1,0},{2,3},{3,2},{4,5},{5,4},{6,7},{7,6},{8,9},{9,8},{10,11... | collective-permute-start | bytes 786440 | tf_op jit(solution)/shard_map/ppermute | solution.py:253
  5.4 11.2 %collective-permute-start.5 = (bf16[2,2,128,256]{3,2,1,0:T(8,128)(2,1)S(1)}, bf16[2,2,128,256]{3,2,1,0:T(8,128)(2,1)S(1)}, u32[]{:S(2)}, u32[]{:S(2)}) collective-permute-start(bf16[2,2,128,256]{3,2,1,0:T(8,128)(2,1)S(1)} %get-tuple-element.36), channel_id=1, source_target_pairs={{0,2},{1,3},{2,0},{3,1},{4,6},{5,7},{6,4},{7,5},{8,10},{9,11},{10,... | collective-permute-start | bytes 786440 | tf_op jit(solution)/shard_map/ppermute | solution.py:253
  7.3 1.6 %copy-start.12 = (f32[2]{0:T(128)S(1)}, f32[2]{0:T(128)}, u32[]{:S(2)}) copy-start(f32[2]{0:T(128)} %refs_0_.14) | copy-start | bytes 28
  8.9 2.4 %copy-start.4 = (bf16[2,256,256]{2,1,0:T(8,128)(2,1)S(1)}, bf16[2,256,256]{2,1,0:T(8,128)(2,1)}, u32[]{:S(2)}) copy-start(bf16[2,256,256]{2,1,0:T(8,128)(2,1)} %refs_7_.7) | copy-start | bytes 786436
  9.0 2.4 %copy-start.5 = (bf16[1,2,2,128,128]{4,3,2,1,0:T(8,128)(2,1)S(1)}, bf16[1,2,2,128,128]{4,3,2,1,0:T(8,128)(2,1)}, u32[]{:S(2)}) copy-start(bf16[1,2,2,128,128]{4,3,2,1,0:T(8,128)(2,1)} %refs_8_.7) | copy-start | bytes 393220
  9.0 2.4 %copy-start.9 = (s32[1,2,2]{2,1,0:T(2,128)S(1)}, s32[1,2,2]{2,1,0:T(2,128)}, u32[]{:S(2)}) copy-start(s32[1,2,2]{2,1,0:T(2,128)} %refs_1_.15) | copy-start | bytes 52
  9.0 2.4 %copy-start.10 = (s32[1,2,2]{2,1,0:T(2,128)S(1)}, s32[1,2,2]{2,1,0:T(2,128)}, u32[]{:S(2)}) copy-start(s32[1,2,2]{2,1,0:T(2,128)} %refs_0_.21) | copy-start | bytes 52
  13.1 8.7 %collective-permute-start.2 = (bf16[2,2,128,256]{3,2,1,0:T(8,128)(2,1)S(1)}, bf16[2,2,128,256]{3,2,1,0:T(8,128)(2,1)S(1)}, u32[]{:S(2)}, u32[]{:S(2)}) collective-permute-start(bf16[2,2,128,256]{3,2,1,0:T(8,128)(2,1)S(1)} %get-tuple-element.32), channel_id=1, source_target_pairs={{0,1},{1,0},{2,3},{3,2},{4,5},{5,4},{6,7},{7,6},{8,9},{9,8},{10,11... | collective-permute-start | bytes 786440 | tf_op jit(solution)/shard_map/ppermute | solution.py:266
  13.3 9.1 %collective-permute-start.3 = (bf16[2,2,128,256]{3,2,1,0:T(8,128)(2,1)S(1)}, bf16[2,2,128,256]{3,2,1,0:T(8,128)(2,1)S(1)}, u32[]{:S(2)}, u32[]{:S(2)}) collective-permute-start(bf16[2,2,128,256]{3,2,1,0:T(8,128)(2,1)S(1)} %get-tuple-element.33), channel_id=1, source_target_pairs={{0,2},{1,3},{2,0},{3,1},{4,6},{5,7},{6,4},{7,5},{8,10},{9,11},{10,... | collective-permute-start | bytes 786440 | tf_op jit(solution)/shard_map/ppermute | solution.py:266
  18.3 4.1 %copy-start.6 = (bf16[256,256]{1,0:T(8,128)(2,1)S(1)}, bf16[256,256]{1,0:T(8,128)(2,1)}, u32[]{:S(2)}) copy-start(bf16[256,256]{1,0:T(8,128)(2,1)} %refs_9_.3) | copy-start | bytes 393220
  18.3 4.1 %copy-start.11 = (f32[2]{0:T(128)S(1)}, f32[2]{0:T(128)}, u32[]{:S(2)}) copy-start(f32[2]{0:T(128)} %refs_1_.17) | copy-start | bytes 28
  18.3 6.0 %collective-permute-start.6 = (bf16[2,2,128,256]{3,2,1,0:T(8,128)(2,1)S(1)}, bf16[2,2,128,256]{3,2,1,0:T(8,128)(2,1)S(1)}, u32[]{:S(2)}, u32[]{:S(2)}) collective-permute-start(bf16[2,2,128,256]{3,2,1,0:T(8,128)(2,1)S(1)} %get-tuple-element.39), channel_id=1, source_target_pairs={{0,1},{1,0},{2,3},{3,2},{4,5},{5,4},{6,7},{7,6},{8,9},{9,8},{10,11... | collective-permute-start | bytes 786440 | tf_op jit(solution)/shard_map/ppermute | solution.py:266
  18.6 9.0 %collective-permute-start.7 = (bf16[2,2,128,256]{3,2,1,0:T(8,128)(2,1)S(1)}, bf16[2,2,128,256]{3,2,1,0:T(8,128)(2,1)S(1)}, u32[]{:S(2)}, u32[]{:S(2)}) collective-permute-start(bf16[2,2,128,256]{3,2,1,0:T(8,128)(2,1)S(1)} %get-tuple-element.40), channel_id=1, source_target_pairs={{0,2},{1,3},{2,0},{3,1},{4,6},{5,7},{6,4},{7,5},{8,10},{9,11},{10,... | collective-permute-start | bytes 786440 | tf_op jit(solution)/shard_map/ppermute | solution.py:266

commit v4 on v3

--- a/solution.py
+++ b/solution.py
@@ -38,7 +38,7 @@
     )(*scalars, *map(pin, arrays), *map(keep, far_arrays), *map(pin, after))
 
 
-def pack(iterates, shower, send_blocks, block):
+def pack(iterates, shower, send_blocks, block, after):
     steps, _, cells, width = iterates.shape
     rounds, sent = send_blocks.shape[1:]
 
@@ -58,7 +58,7 @@
                     send_refs[r][step, k] = it_ref[step, at, :].astype(BF16)
 
     return call(
-        body, "pack", [((steps, sent, block, width), BF16)] * rounds, [], [], [send_blocks, iterates],
+        body, "pack", [((steps, sent, block, width), BF16)] * rounds, [], [], [send_blocks, iterates], after=after,
         scratch=[
             pltpu.SMEM(send_blocks.shape, jnp.int32), pltpu.VMEM((steps, cells, width), F32),
             pltpu.SemaphoreType.DMA((steps + 1,)),
@@ -109,9 +109,14 @@
 def update(recv_ref, h_ref, in_refs, pre_ref, wn, wo, rem_ref, step):
     sent, block = in_refs[0].shape[1:3]
     parts = h_ref.shape[1] // block
-    addends = [
-        (recv_ref[0, r, k], dot(rem_ref[0, r, k], in_ref[step, k])) for r, in_ref in enumerate(in_refs) for k in range(sent)
-    ]
+    even = lax.rem(lax.axis_index("dom"), 2) == 0
+    addends = []
+    for r in range(2):
+        for k in range(sent):
+            chosen = in_refs[r][step, k]
+            if r == 1 and len(in_refs) > 2:
+                chosen = jnp.where(even, chosen, in_refs[2 + step][0, k])
+            addends.append((recv_ref[0, r, k], dot(rem_ref[0, r, k], chosen)))
     mixed = []
     for b in range(parts):
         total = None
@@ -124,25 +129,43 @@
     return (h_ref[step].astype(F32) + dot(activated, wo)).astype(BF16)
 
 
-def far(hidden, incoming, pre, layer, neighbor, output, remote, receive, send_blocks, after):
+def far(hidden, incoming, pre, layer, neighbor, output, remote, receive, send_blocks, by_step, after):
     steps, cells, width = hidden.shape
     rounds, sent = send_blocks.shape[1:]
     block = incoming[0].shape[2]
+    count = len(incoming)
 
     def body(recv_ref, blocks_ref, h_ref, *refs):
-        in_refs, (pre_ref, wn_ref, wo_ref, rem_ref, out_ref, *send_refs) = refs[:rounds], refs[rounds:]
+        in_refs, (pre_ref, wn_ref, wo_ref, rem_ref, out_ref, *send_refs) = refs[:count], refs[count:]
         for step in range(steps):
             out_ref[step] = update(recv_ref, h_ref, in_refs, pre_ref, wn_ref[layer], wo_ref[layer], rem_ref, step)
         for r in range(rounds):
             for k in range(sent):
                 at = pl.ds(blocks_ref[0, r, k] * block, block)
                 for step in range(steps):
-                    send_refs[r][step, k] = out_ref[step, at, :]
+                    rows = out_ref[step, at, :]
+                    send_refs[r][step, k] = rows
+                    if by_step and r == 1:
+                        send_refs[rounds + step][0, k] = rows
 
     outs = [((steps, cells, width), BF16)] + [((steps, sent, block, width), BF16)] * rounds
+    if by_step:
+        outs += [((1, sent, block, width), BF16)] * steps
     return call(
         body, "far", outs, [receive, send_blocks], [hidden, *incoming, pre, neighbor, output, remote], after=after
     )
+
+
+def ready(after):
+    def body(o_ref):
+        o_ref[...] = jnp.zeros_like(o_ref)
+
+    return call(body, "ready", [((16, 128), BF16)], [], [], after=after)[0]
+
+
+def hold(arrays, after):
+    outs = [(a.shape, a.dtype) for a in arrays]
+    return call(lambda *refs: None, "hold", outs, [], arrays, after=after, aliases={i: i for i in range(len(arrays))})
 
 
 def noise_sums(noise, scale, iterates, after):
@@ -247,25 +270,38 @@
     layers = self_weight.shape[0]
     parts = lax.axis_size("dom")
     pairs = [[(i, i ^ (1 << r)) for i in range(parts)] for r in range(2)]
-    incoming = []
+    incoming, token = [], ()
     for s in range(showers):
-        sends = pack(iterates, s, send_blocks, block)
+        sends = pack(iterates, s, send_blocks, block, token)
+        token = (sends[1],)
         incoming.append([lax.ppermute(sends[r], "dom", pairs[r]) for r in (0, 1)])
     common = (step_embed, self_weight, neighbor_weight, local_columns, tile_values)
     rest = (neighbor_weight, output_weight, remote_values, receive_rows)
     hidden, pre = [None] * showers, [None] * showers
-    token = ()
     for s in range(showers):
         pre[s], hidden[s] = near_first(iterates, s, *common, token)
         token = (pre[s],)
-    noise_sum = noise_sums(noise_draws, noise_scale, iterates, token)
-    token = (noise_sum[0],)
+    evens, odds = ([(i, j) for i, j in pairs[1] if i % 2 == odd] for odd in (0, 1))
+    hand_over = [(i, i + 1) for i in range(0, parts, 2)]
+    noise_sum = None
     for layer in range(1, layers):
+        last = layer + 1 == layers
+        held = []
         for s in range(showers):
-            hidden[s], *sends = far(hidden[s], incoming[s], pre[s], layer - 1, *rest, send_blocks, token)
-            incoming[s] = [lax.ppermute(sends[r], "dom", pairs[r]) for r in (0, 1)]
+            hidden[s], send0, send1, *again = far(
+                hidden[s], incoming[s], pre[s], layer - 1, *rest, send_blocks, last, token
+            )
+            held += again
+            incoming[s] = [lax.ppermute(send0, "dom", pairs[0]), lax.ppermute(send1, "dom", evens if last else pairs[1])]
             pre[s] = near(hidden[s], layer, *common, ())
             token = (pre[s],)
+            if noise_sum is None:
+                noise_sum = noise_sums(noise_draws, noise_scale, iterates, token)
+                token = (noise_sum[0],)
+        if last:
+            turn = lax.ppermute(ready((*incoming[0], incoming[-1][0], pre[-1])), "dom", hand_over)
+            for i, sends in enumerate(hold(held, (turn,))):
+                incoming[i // steps].append(lax.ppermute(sends, "dom", odds))
     totals, running = (), [None] * showers
     for s in range(showers):
         total, running[s] = finish(

time: 81.1 us -> 86.7 us (1.069)
  the two profiles are of different devices: /device:TPU:2 before, /device:TPU:1 now
where the time goes in v4:
time: 86.7 us; the launch traced here: 86.4 us
  blocking collectives  38.9 us (45%)
  starting transfers between devices  21.5 us (25%)
  Pallas kernels  20.1 us (23%)
  waiting for transfers between devices  5.38 us (6%)
    all_to_all x1, blocking collectives, local(): lax.all_to_all(total.reshape(lax.axis_size('tm'), -1, width), 'tm', 0, 0)  21.9 us
    pallas_call x15, Pallas kernels, call(): pl.pallas_call(inner, out_shape=[pltpu.VMEM(*o) for o in outs] + [pltpu.H...  20.1 us
    all_to_all x1, blocking collectives, local(): earlier = lax.all_to_all(exclusive_prefix(pieces), 'tm', 0, 0)  17 us
    ppermute x4, starting transfers between devices, local(): incoming[i // steps].append(lax.ppermute(sends, 'dom', odds))  10.7 us
    ppermute x4, starting transfers between devices, local(): incoming.append([lax.ppermute(sends[r], 'dom', pairs[r]) for r in (0, 1)])  5.24 us
    ppermute x1, waiting for transfers between devices, local(): lax.ppermute(ready((*incoming[0], incoming[-1][0], pre[-1])), 'dom', hand...  3.85 us
    ppermute x2, starting transfers between devices, local(): lax.ppermute(send0, 'dom', pairs[0])  2.85 us
  transfers between devices with their start and end apart: 13, of which 3 were waited for; matrix products, arithmetic and copies ran while one was open for 0% of the time, Pallas kernels for 18%

profile of v4, /device:TPU:1, one launch (start us, length us, event | category | flops | bytes accessed | tf_op | source)
XLA Modules:
  0.0 86.4 jit_solution(6382433414116102581)
XLA Ops:
  0.0 1.4 %pack.2 = (bf16[2,2,128,256]{3,2,1,0:T(8,128)(2,1)S(1)}, bf16[2,2,128,256]{3,2,1,0:T(8,128)(2,1)S(1)}) custom-call(s32[1,2,2]{2,1,0:T(2,128)} %refs_1_.15, f32[2,2,512,256]{3,2,1,0:T(8,128)} %refs_2_.8), custom_call_target="tpu_custom_call" | custom-call | flops 1048576 | bytes 1024 | tf_op jit(solution)/shard_map/pack/pallas_call | solution.py:25
  1.5 3.3 %collective-permute-start = (bf16[2,2,128,256]{3,2,1,0:T(8,128)(2,1)S(1)}, bf16[2,2,128,256]{3,2,1,0:T(8,128)(2,1)S(1)}, u32[]{:S(2)}, u32[]{:S(2)}) collective-permute-start(bf16[2,2,128,256]{3,2,1,0:T(8,128)(2,1)S(1)} %get-tuple-element.36), channel_id=1, source_target_pairs={{0,1},{1,0},{2,3},{3,2},{4,5},{5,4},{6,7},{7,6},{8,9},{9,8},{10,11... | collective-permute-start | bytes 786440 | tf_op jit(solution)/shard_map/ppermute | solution.py:277
  6.2 1.7 %collective-permute-start.5 = (bf16[2,2,128,256]{3,2,1,0:T(8,128)(2,1)S(1)}, bf16[2,2,128,256]{3,2,1,0:T(8,128)(2,1)S(1)}, u32[]{:S(2)}, u32[]{:S(2)}) collective-permute-start(bf16[2,2,128,256]{3,2,1,0:T(8,128)(2,1)S(1)} %get-tuple-element.34.refs_6_), channel_id=1, source_target_pairs={{0,2},{1,3},{2,0},{3,1},{4,6},{5,7},{6,4},{7,5},{8,10},{9,11},{10,... | collective-permute-start | bytes 786440 | tf_op jit(solution)/shard_map/ppermute | solution.py:277
  8.0 1.6 %near_first.2 = (f32[2,512,256]{2,1,0:T(8,128)S(1)}, bf16[2,512,256]{2,1,0:T(8,128)(2,1)S(1)}) custom-call(s32[4,4]{1,0:T(4,128)S(1)} %copy-done.7, f32[2,2,512,256]{3,2,1,0:T(8,128)S(1)} %copy-done, f32[2,256]{1,0:T(2,128)S(1)} %copy-done.8, bf16[2,256,256]{2,1,0:T(8,128)(2,1)S(1)} %copy-done.4, bf16[2,256,256]{2,1,0:T(8,128)(2,1)S(1)} %copy-done.1, ...), custom_call_target="tpu_custom_call" | custom-call | flops 1048576 | bytes 1024 | tf_op jit(solution)/shard_map/near_first/pallas_call | solution.py:25
  9.7 1.6 %near_first.3 = (f32[2,512,256]{2,1,0:T(8,128)S(1)}, bf16[2,512,256]{2,1,0:T(8,128)(2,1)S(1)}) custom-call(s32[4,4]{1,0:T(4,128)S(1)} %copy-done.7, f32[2,2,512,256]{3,2,1,0:T(8,128)S(1)} %copy-done, f32[2,256]{1,0:T(2,128)S(1)} %copy-done.8, bf16[2,256,256]{2,1,0:T(8,128)(2,1)S(1)} %copy-done.4, bf16[2,256,256]{2,1,0:T(8,128)(2,1)S(1)} %copy-done.1, ...), custom_call_target="tpu_custom_call" | custom-call | flops 1048576 | bytes 1024 | tf_op jit(solution)/shard_map/near_first/pallas_call | solution.py:25
  11.3 1.3 %collective-permute-done.1.refs_4_ = bf16[2,2,128,256]{3,2,1,0:T(8,128)(2,1)S(1)} collective-permute-done((bf16[2,2,128,256]{3,2,1,0:T(8,128)(2,1)S(1)}, bf16[2,2,128,256]{3,2,1,0:T(8,128)(2,1)S(1)}, u32[]{:S(2)}, u32[]{:S(2)}) %collective-permute-start.1) | collective-permute-done | bytes 262176 | tf_op jit(solution)/shard_map/ppermute | solution.py:277
  12.7 1.7 %far.2 = (bf16[2,512,256]{2,1,0:T(8,128)(2,1)S(1)}, bf16[2,2,128,256]{3,2,1,0:T(8,128)(2,1)S(1)}, bf16[2,2,128,256]{3,2,1,0:T(8,128)(2,1)S(1)}, bf16[1,2,128,256...) custom-call(s32[1,2,2]{2,1,0:T(2,128)S(1)} %copy-done.10, s32[1,2,2]{2,1,0:T(2,128)S(1)} %copy-done.9, ...), custom_call_target="tpu_custom_call" | custom-call | flops 1048576 | bytes 1024 | tf_op jit(solution)/shard_map/far/pallas_call | solution.py:25
  14.4 1.4 %collective-permute-start.2 = (bf16[2,2,128,256]{3,2,1,0:T(8,128)(2,1)S(1)}, bf16[2,2,128,256]{3,2,1,0:T(8,128)(2,1)S(1)}, u32[]{:S(2)}, u32[]{:S(2)}) collective-permute-start(bf16[2,2,128,256]{3,2,1,0:T(8,128)(2,1)S(1)} %get-tuple-element.40), channel_id=1, source_target_pairs={{0,1},{1,0},{2,3},{3,2},{4,5},{5,4},{6,7},{7,6},{8,9},{9,8},{10,11... | collective-permute-start | bytes 786440 | tf_op jit(solution)/shard_map/ppermute | solution.py:295
  16.5 1.6 %near.2.refs_3_.refs_7_ = f32[2,512,256]{2,1,0:T(8,128)S(1)} custom-call(s32[4,4]{1,0:T(4,128)S(1)} %copy-done.7, bf16[2,512,256]{2,1,0:T(8,128)(2,1)S(1)} %get-tuple-element.39.refs_1_.refs_2_, f32[2,256]{1,0:T(2,128)S(1)} %copy-done.8, bf16[2,256,256]{2,1,0:T(8,128)(2,1)S(1)} %copy-done.4, bf16[2,256,256]{2,1,0:T(8,128)(2,1)S(1)} %copy-done.1, ...), custom_call_target="tpu_custom_call" | custom-call | flops 1048576 | bytes 1024 | tf_op jit(solution)/shard_map/near/pallas_call | solution.py:25
  18.0 2.4 %noise_sums.1 = (f32[2,512,256]{2,1,0:T(8,128)S(1)}, f32[2,512,256]{2,1,0:T(8,128)S(1)}) custom-call(f32[2]{0:T(128)S(1)} %copy-done.12, bf16[2,2,512,256]{3,2,1,0:T(8,128)(2,1)} %refs_1_.14, f32[2,2,512,256]{3,2,1,0:T(8,128)} %refs_2_.8, f32[2,512,256]{2,1,0:T(8,128)S(1)} %near.2.refs_3_.refs_7_), custom_call_target="tpu_custom_call" | custom-call | flops 1048576 | bytes 1024 | tf_op jit(solution)/shard_map/noise_sums/pallas_call | solution.py:25
  20.4 1.7 %far.3 = (bf16[2,512,256]{2,1,0:T(8,128)(2,1)S(1)}, bf16[2,2,128,256]{3,2,1,0:T(8,128)(2,1)S(1)}, bf16[2,2,128,256]{3,2,1,0:T(8,128)(2,1)S(1)}, bf16[1,2,128,256...) custom-call(s32[1,2,2]{2,1,0:T(2,128)S(1)} %copy-done.10, s32[1,2,2]{2,1,0:T(2,128)S(1)} %copy-done.9, ...), custom_call_target="tpu_custom_call" | custom-call | flops 1048576 | bytes 1024 | tf_op jit(solution)/shard_map/far/pallas_call | solution.py:25
  22.1 1.4 %collective-permute-start.6 = (bf16[2,2,128,256]{3,2,1,0:T(8,128)(2,1)S(1)}, bf16[2,2,128,256]{3,2,1,0:T(8,128)(2,1)S(1)}, u32[]{:S(2)}, u32[]{:S(2)}) collective-permute-start(bf16[2,2,128,256]{3,2,1,0:T(8,128)(2,1)S(1)} %get-tuple-element.49), channel_id=1, source_target_pairs={{0,1},{1,0},{2,3},{3,2},{4,5},{5,4},{6,7},{7,6},{8,9},{9,8},{10,11... | collective-permute-start | bytes 786440 | tf_op jit(solution)/shard_map/ppermute | solution.py:295
  24.2 1.6 %near.3.refs_3_.refs_13_.refs_7_ = f32[2,512,256]{2,1,0:T(8,128)S(1)} custom-call(s32[4,4]{1,0:T(4,128)S(1)} %copy-done.7, bf16[2,512,256]{2,1,0:T(8,128)(2,1)S(1)} %get-tuple-element.50.refs_1_.refs_2_, f32[2,256]{1,0:T(2,128)S(1)} %copy-done.8, bf16[2,256,256]{2,1,0:T(8,128)(2,1)S(1)} %copy-done.4, bf16[2,256,256]{2,1,0:T(8,128)(2,1)S(1)} %copy-done.1, ...), custom_call_target="tpu_custom_call" | custom-call | flops 1048576 | bytes 1024 | tf_op jit(solution)/shard_map/near/pallas_call | solution.py:25
  25.9 1.3 %collective-permute-start.7 = (bf16[16,128]{1,0:T(8,128)(2,1)S(1)}, bf16[16,128]{1,0:T(8,128)(2,1)S(1)}, u32[]{:S(2)}, u32[]{:S(2)}) collective-permute-start(bf16[16,128]{1,0:T(8,128)(2,1)S(1)} %ready.1), channel_id=1, source_target_pairs={{0,1},{2,3},{4,5},{6,7},{8,9},{10,11},{12,13},{14,15},{16,17},{18,... | collective-permute-start | bytes 12296 | tf_op jit(solution)/shard_map/ppermute | solution.py:302
  27.2 3.8 %collective-permute-done.7.refs_4_ = bf16[16,128]{1,0:T(8,128)(2,1)S(1)} collective-permute-done((bf16[16,128]{1,0:T(8,128)(2,1)S(1)}, bf16[16,128]{1,0:T(8,128)(2,1)S(1)}, u32[]{:S(2)}, u32[]{:S(2)}) %collective-permute-start.7) | collective-permute-done | bytes 4128 | tf_op jit(solution)/shard_map/ppermute | solution.py:302
  31.0 1.9 %collective-permute-start.8 = (bf16[1,2,128,256]{3,2,1,0:T(8,128)(2,1)S(1)}, bf16[1,2,128,256]{3,2,1,0:T(8,128)(2,1)S(1)}, u32[]{:S(2)}, u32[]{:S(2)}) collective-permute-start(bf16[1,2,128,256]{3,2,1,0:T(8,128)(2,1)S(1)} %get-tuple-element.51), channel_id=1, source_target_pairs={{1,3},{3,1},{5,7},{7,5},{9,11},{11,9},{13,15},{15,13},{17,19},{19,... | collective-permute-start | bytes 393224 | tf_op jit(solution)/shard_map/ppermute | solution.py:304
  32.9 3.4 %collective-permute-start.9 = (bf16[1,2,128,256]{3,2,1,0:T(8,128)(2,1)S(1)}, bf16[1,2,128,256]{3,2,1,0:T(8,128)(2,1)S(1)}, u32[]{:S(2)}, u32[]{:S(2)}) collective-permute-start(bf16[1,2,128,256]{3,2,1,0:T(8,128)(2,1)S(1)} %get-tuple-element.52), channel_id=1, source_target_pairs={{1,3},{3,1},{5,7},{7,5},{9,11},{11,9},{13,15},{15,13},{17,19},{19,... | collective-permute-start | bytes 393224 | tf_op jit(solution)/shard_map/ppermute | solution.py:304
  36.3 1.9 %collective-permute-start.11 = (bf16[1,2,128,256]{3,2,1,0:T(8,128)(2,1)S(1)}, bf16[1,2,128,256]{3,2,1,0:T(8,128)(2,1)S(1)}, u32[]{:S(2)}, u32[]{:S(2)}) collective-permute-start(bf16[1,2,128,256]{3,2,1,0:T(8,128)(2,1)S(1)} %get-tuple-element.55), channel_id=1, source_target_pairs={{1,3},{3,1},{5,7},{7,5},{9,11},{11,9},{13,15},{15,13},{17,19},{19,... | collective-permute-start | bytes 393224 | tf_op jit(solution)/shard_map/ppermute | solution.py:304
  38.2 3.5 %collective-permute-start.12 = (bf16[1,2,128,256]{3,2,1,0:T(8,128)(2,1)S(1)}, bf16[1,2,128,256]{3,2,1,0:T(8,128)(2,1)S(1)}, u32[]{:S(2)}, u32[]{:S(2)}) collective-permute-start(bf16[1,2,128,256]{3,2,1,0:T(8,128)(2,1)S(1)} %get-tuple-element.56), channel_id=1, source_target_pairs={{1,3},{3,1},{5,7},{7,5},{9,11},{11,9},{13,15},{15,13},{17,19},{19,... | collective-permute-start | bytes 393224 | tf_op jit(solution)/shard_map/ppermute | solution.py:304
  41.8 1.9 %finish.2 = (bf16[2,512,256]{2,1,0:T(8,128)(2,1)S(1)}, f32[2,512,256]{2,1,0:T(8,128)S(1)}) custom-call(s32[1,2,2]{2,1,0:T(2,128)S(1)} %copy-done.10, f32[2]{0:T(128)S(1)} %copy-done.11, bf16[2,512,256]{2,1,0:T(8,128)(2,1)S(1)} %get-tuple-element.39.refs_1_.refs_2_, bf16[2,2,128,256]{3,2,1,0:T(8,128)(2,1)S(1)} %collective-permute-done.2.refs_0_.refs_3_, ...), custom_call_target="tpu_custom_call" | custom-call | flops 1048576 | bytes 1024 | tf_op jit(solution)/shard_map/finish/pallas_call | solution.py:25
  44.0 1.9 %finish.3 = (bf16[2,512,256]{2,1,0:T(8,128)(2,1)S(1)}, f32[2,512,256]{2,1,0:T(8,128)S(1)}) custom-call(s32[1,2,2]{2,1,0:T(2,128)S(1)} %copy-done.10, f32[2]{0:T(128)S(1)} %copy-done.11, bf16[2,512,256]{2,1,0:T(8,128)(2,1)S(1)} %get-tuple-element.50.refs_1_.refs_2_, ...), custom_call_target="tpu_custom_call", output_to_operand_aliasing={{0}: (13, {})} | custom-call | flops 1048576 | bytes 1024 | tf_op jit(solution)/shard_map/finish/pallas_call | solution.py:25
  45.9 21.9 %all_to_all.10.refs_0_ = bf16[32,32,256]{2,1,0:T(8,128)(2,1)S(1)} all-to-all(bf16[32,32,256]{2,1,0:T(8,128)(2,1)S(1)} %bitcast.3), channel_id=1, replica_groups=mesh['tm'=32,'dom'=8] {'tm'}, dimensions={0} | all-to-all | bytes 1048576 | tf_op jit(solution)/shard_map/all_to_all | solution.py:312
  67.8 17.0 %all_to_all.11 = bf16[32,32,256]{2,1,0:T(8,128)(2,1)S(1)} all-to-all(bf16[32,32,256]{2,1,0:T(8,128)(2,1)S(1)} %exclusive_prefix.1), channel_id=1, replica_groups=mesh['tm'=32,'dom'=8] {'tm'}, dimensions={0} | all-to-all | bytes 1048576 | tf_op jit(solution)/shard_map/all_to_all | solution.py:313
  84.8 1.4 %deliver.1 = f32[2,2,512,256]{3,2,1,0:T(8,128)} custom-call(f32[2,512,256]{2,1,0:T(8,128)S(1)} %get-tuple-element.53.refs_0_, f32[2,512,256]{2,1,0:T(8,128)S(1)} %get-tuple-element.59.refs_1_, bf16[2,512,256]{2,1,0:T(8,128)(2,1)S(1)} %bitcast.2), custom_call_target="tpu_custom_call" | custom-call | flops 1048576 | bytes 1024 | tf_op jit(solution)/shard_map/deliver/pallas_call | solution.py:25
  (45 shorter events, 3.2 us)
Async XLA Ops:
  0.0 8.0 %copy-start = (f32[2,2,512,256]{3,2,1,0:T(8,128)S(1)}, f32[2,2,512,256]{3,2,1,0:T(8,128)}, u32[]{:S(2)}) copy-start(f32[2,2,512,256]{3,2,1,0:T(8,128)} %refs_2_.8) | copy-start | bytes 6291460
  0.0 8.0 %copy-start.1 = (bf16[2,256,256]{2,1,0:T(8,128)(2,1)S(1)}, bf16[2,256,256]{2,1,0:T(8,128)(2,1)}, u32[]{:S(2)}) copy-start(bf16[2,256,256]{2,1,0:T(8,128)(2,1)} %refs_8_.7) | copy-start | bytes 786436
  0.0 8.0 %copy-start.2 = (bf16[4,4,128,128]{3,2,1,0:T(8,128)(2,1)S(1)}, bf16[4,4,128,128]{3,2,1,0:T(8,128)(2,1)}, u32[]{:S(2)}) copy-start(bf16[4,4,128,128]{3,2,1,0:T(8,128)(2,1)} %refs_5_.7) | copy-start | bytes 1572868
  0.0 8.0 %copy-start.7 = (s32[4,4]{1,0:T(4,128)S(1)}, s32[4,4]{1,0:T(4,128)}, u32[]{:S(2)}) copy-start(s32[4,4]{1,0:T(4,128)} %refs_0_.19) | copy-start | bytes 196
  0.0 8.0 %copy-start.4 = (bf16[2,256,256]{2,1,0:T(8,128)(2,1)S(1)}, bf16[2,256,256]{2,1,0:T(8,128)(2,1)}, u32[]{:S(2)}) copy-start(bf16[2,256,256]{2,1,0:T(8,128)(2,1)} %refs_3_.7) | copy-start | bytes 786436
  0.0 8.0 %copy-start.8 = (f32[2,256]{1,0:T(2,128)S(1)}, f32[2,256]{1,0:T(2,128)}, u32[]{:S(2)}) copy-start(f32[2,256]{1,0:T(2,128)} %refs_2_.9) | copy-start | bytes 6148
  1.5 9.9 %collective-permute-start = (bf16[2,2,128,256]{3,2,1,0:T(8,128)(2,1)S(1)}, bf16[2,2,128,256]{3,2,1,0:T(8,128)(2,1)S(1)}, u32[]{:S(2)}, u32[]{:S(2)}) collective-permute-start(bf16[2,2,128,256]{3,2,1,0:T(8,128)(2,1)S(1)} %get-tuple-element.36), channel_id=1, source_target_pairs={{0,1},{1,0},{2,3},{3,2},{4,5},{5,4},{6,7},{7,6},{8,9},{9,8},{10,11... | collective-permute-start | bytes 786440 | tf_op jit(solution)/shard_map/ppermute | solution.py:277
  4.8 7.9 %collective-permute-start.1 = (bf16[2,2,128,256]{3,2,1,0:T(8,128)(2,1)S(1)}, bf16[2,2,128,256]{3,2,1,0:T(8,128)(2,1)S(1)}, u32[]{:S(2)}, u32[]{:S(2)}) collective-permute-start(bf16[2,2,128,256]{3,2,1,0:T(8,128)(2,1)S(1)} %get-tuple-element.33.refs_2_), channel_id=1, source_target_pairs={{0,2},{1,3},{2,0},{3,1},{4,6},{5,7},{6,4},{7,5},{8,10},{9,11},{10,... | collective-permute-start | bytes 786440 | tf_op jit(solution)/shard_map/ppermute | solution.py:277
  6.0 14.4 %collective-permute-start.4 = (bf16[2,2,128,256]{3,2,1,0:T(8,128)(2,1)S(1)}, bf16[2,2,128,256]{3,2,1,0:T(8,128)(2,1)S(1)}, u32[]{:S(2)}, u32[]{:S(2)}) collective-permute-start(bf16[2,2,128,256]{3,2,1,0:T(8,128)(2,1)S(1)} %get-tuple-element.45), channel_id=1, source_target_pairs={{0,1},{1,0},{2,3},{3,2},{4,5},{5,4},{6,7},{7,6},{8,9},{9,8},{10,11... | collective-permute-start | bytes 786440 | tf_op jit(solution)/shard_map/ppermute | solution.py:277
  6.2 14.2 %collective-permute-start.5 = (bf16[2,2,128,256]{3,2,1,0:T(8,128)(2,1)S(1)}, bf16[2,2,128,256]{3,2,1,0:T(8,128)(2,1)S(1)}, u32[]{:S(2)}, u32[]{:S(2)}) collective-permute-start(bf16[2,2,128,256]{3,2,1,0:T(8,128)(2,1)S(1)} %get-tuple-element.34.refs_6_), channel_id=1, source_target_pairs={{0,2},{1,3},{2,0},{3,1},{4,6},{5,7},{6,4},{7,5},{8,10},{9,11},{10,... | collective-permute-start | bytes 786440 | tf_op jit(solution)/shard_map/ppermute | solution.py:277
  9.6 3.0 %copy-start.3 = (bf16[2,256,256]{2,1,0:T(8,128)(2,1)S(1)}, bf16[2,256,256]{2,1,0:T(8,128)(2,1)}, u32[]{:S(2)}) copy-start(bf16[2,256,256]{2,1,0:T(8,128)(2,1)} %refs_9_.3) | copy-start | bytes 786436
  9.6 3.0 %copy-start.5 = (bf16[1,2,2,128,128]{4,3,2,1,0:T(8,128)(2,1)S(1)}, bf16[1,2,2,128,128]{4,3,2,1,0:T(8,128)(2,1)}, u32[]{:S(2)}) copy-start(bf16[1,2,2,128,128]{4,3,2,1,0:T(8,128)(2,1)} %refs_10_.3) | copy-start | bytes 393220
  14.3 3.7 %copy-start.12 = (f32[2]{0:T(128)S(1)}, f32[2]{0:T(128)}, u32[]{:S(2)}) copy-start(f32[2]{0:T(128)} %refs_0_.17) | copy-start | bytes 28
  14.4 11.5 %collective-permute-start.2 = (bf16[2,2,128,256]{3,2,1,0:T(8,128)(2,1)S(1)}, bf16[2,2,128,256]{3,2,1,0:T(8,128)(2,1)S(1)}, u32[]{:S(2)}, u32[]{:S(2)}) collective-permute-start(bf16[2,2,128,256]{3,2,1,0:T(8,128)(2,1)S(1)} %get-tuple-element.40), channel_id=1, source_target_pairs={{0,1},{1,0},{2,3},{3,2},{4,5},{5,4},{6,7},{7,6},{8,9},{9,8},{10,11... | collective-permute-start | bytes 786440 | tf_op jit(solution)/shard_map/ppermute | solution.py:295
  15.8 10.1 %collective-permute-start.3 = (bf16[2,2,128,256]{3,2,1,0:T(8,128)(2,1)S(1)}, bf16[2,2,128,256]{3,2,1,0:T(8,128)(2,1)S(1)}, u32[]{:S(2)}, u32[]{:S(2)}) collective-permute-start(bf16[2,2,128,256]{3,2,1,0:T(8,128)(2,1)S(1)} %get-tuple-element.41), channel_id=1, source_target_pairs={{0,2},{2,0},{4,6},{6,4},{8,10},{10,8},{12,14},{14,12},{16,18},{18,... | collective-permute-start | bytes 786440 | tf_op jit(solution)/shard_map/ppermute | solution.py:295
  22.1 3.7 %collective-permute-start.6 = (bf16[2,2,128,256]{3,2,1,0:T(8,128)(2,1)S(1)}, bf16[2,2,128,256]{3,2,1,0:T(8,128)(2,1)S(1)}, u32[]{:S(2)}, u32[]{:S(2)}) collective-permute-start(bf16[2,2,128,256]{3,2,1,0:T(8,128)(2,1)S(1)} %get-tuple-element.49), channel_id=1, source_target_pairs={{0,1},{1,0},{2,3},{3,2},{4,5},{5,4},{6,7},{7,6},{8,9},{9,8},{10,11... | collective-permute-start | bytes 786440 | tf_op jit(solution)/shard_map/ppermute | solution.py:295
  23.5 20.2 %collective-permute-start.10 = (bf16[2,2,128,256]{3,2,1,0:T(8,128)(2,1)S(1)}, bf16[2,2,128,256]{3,2,1,0:T(8,128)(2,1)S(1)}, u32[]{:S(2)}, u32[]{:S(2)}) collective-permute-start(bf16[2,2,128,256]{3,2,1,0:T(8,128)(2,1)S(1)} %get-tuple-element.54), channel_id=1, source_target_pairs={{0,2},{2,0},{4,6},{6,4},{8,10},{10,8},{12,14},{14,12},{16,18},{18,... | collective-permute-start | bytes 786440 | tf_op jit(solution)/shard_map/ppermute | solution.py:295
  24.2 17.6 %copy-start.6 = (bf16[256,256]{1,0:T(8,128)(2,1)S(1)}, bf16[256,256]{1,0:T(8,128)(2,1)}, u32[]{:S(2)}) copy-start(bf16[256,256]{1,0:T(8,128)(2,1)} %refs_11_.3) | copy-start | bytes 393220
  24.2 17.6 %copy-start.11 = (f32[2]{0:T(128)S(1)}, f32[2]{0:T(128)}, u32[]{:S(2)}) copy-start(f32[2]{0:T(128)} %refs_1_.17) | copy-start | bytes 28
  25.9 5.1 %collective-permute-start.7 = (bf16[16,128]{1,0:T(8,128)(2,1)S(1)}, bf16[16,128]{1,0:T(8,128)(2,1)S(1)}, u32[]{:S(2)}, u32[]{:S(2)}) collective-permute-start(bf16[16,128]{1,0:T(8,128)(2,1)S(1)} %ready.1), channel_id=1, source_target_pairs={{0,1},{2,3},{4,5},{6,7},{8,9},{10,11},{12,13},{14,15},{16,17},{18,... | collective-permute-start | bytes 12296 | tf_op jit(solution)/shard_map/ppermute | solution.py:302
  31.0 10.8 %collective-permute-start.8 = (bf16[1,2,128,256]{3,2,1,0:T(8,128)(2,1)S(1)}, bf16[1,2,128,256]{3,2,1,0:T(8,128)(2,1)S(1)}, u32[]{:S(2)}, u32[]{:S(2)}) collective-permute-start(bf16[1,2,128,256]{3,2,1,0:T(8,128)(2,1)S(1)} %get-tuple-element.51), channel_id=1, source_target_pairs={{1,3},{3,1},{5,7},{7,5},{9,11},{11,9},{13,15},{15,13},{17,19},{19,... | collective-permute-start | bytes 393224 | tf_op jit(solution)/shard_map/ppermute | solution.py:304
  32.9 8.9 %collective-permute-start.9 = (bf16[1,2,128,256]{3,2,1,0:T(8,128)(2,1)S(1)}, bf16[1,2,128,256]{3,2,1,0:T(8,128)(2,1)S(1)}, u32[]{:S(2)}, u32[]{:S(2)}) collective-permute-start(bf16[1,2,128,256]{3,2,1,0:T(8,128)(2,1)S(1)} %get-tuple-element.52), channel_id=1, source_target_pairs={{1,3},{3,1},{5,7},{7,5},{9,11},{11,9},{13,15},{15,13},{17,19},{19,... | collective-permute-start | bytes 393224 | tf_op jit(solution)/shard_map/ppermute | solution.py:304
  36.3 7.4 %collective-permute-start.11 = (bf16[1,2,128,256]{3,2,1,0:T(8,128)(2,1)S(1)}, bf16[1,2,128,256]{3,2,1,0:T(8,128)(2,1)S(1)}, u32[]{:S(2)}, u32[]{:S(2)}) collective-permute-start(bf16[1,2,128,256]{3,2,1,0:T(8,128)(2,1)S(1)} %get-tuple-element.55), channel_id=1, source_target_pairs={{1,3},{3,1},{5,7},{7,5},{9,11},{11,9},{13,15},{15,13},{17,19},{19,... | collective-permute-start | bytes 393224 | tf_op jit(solution)/shard_map/ppermute | solution.py:304
  38.2 5.7 %collective-permute-start.12 = (bf16[1,2,128,256]{3,2,1,0:T(8,128)(2,1)S(1)}, bf16[1,2,128,256]{3,2,1,0:T(8,128)(2,1)S(1)}, u32[]{:S(2)}, u32[]{:S(2)}) collective-permute-start(bf16[1,2,128,256]{3,2,1,0:T(8,128)(2,1)S(1)} %get-tuple-element.56), channel_id=1, source_target_pairs={{1,3},{3,1},{5,7},{7,5},{9,11},{11,9},{13,15},{15,13},{17,19},{19,... | collective-permute-start | bytes 393224 | tf_op jit(solution)/shard_map/ppermute | solution.py:304
  (2 other events, 6.0 us)

commit v5 on v3

--- a/solution.py
+++ b/solution.py
@@ -106,22 +106,36 @@
     )
 
 
-def update(recv_ref, h_ref, in_refs, pre_ref, wn, wo, rem_ref, step):
-    sent, block = in_refs[0].shape[1:3]
-    parts = h_ref.shape[1] // block
-    addends = [
-        (recv_ref[0, r, k], dot(rem_ref[0, r, k], in_ref[step, k])) for r, in_ref in enumerate(in_refs) for k in range(sent)
-    ]
+def received(recv_ref, rem_ref, rounds, cells):
+    steps, sent, block, _ = next(iter(rounds.values())).shape
     mixed = []
-    for b in range(parts):
-        total = None
-        for row, addend in addends:
-            term = jnp.where(row == b, 1.0, 0.0) * addend
-            total = term if total is None else total + term
-        mixed.append(total.astype(BF16))
-    half = 0.5 * (pre_ref[step] + dot(jnp.concatenate(mixed, axis=0), wn))
+    for step in range(steps):
+        addends = [(recv_ref[0, r, k], dot(rem_ref[0, r, k], in_ref[step, k])) for r, in_ref in rounds.items() for k in range(sent)]
+        for b in range(cells // block):
+            total = None
+            for row, addend in addends:
+                term = jnp.where(row == b, 1.0, 0.0) * addend
+                total = term if total is None else total + term
+            mixed.append(total.astype(BF16))
+    return jnp.concatenate(mixed, axis=0)
+
+
+def middle(incoming, pre, layer, neighbor, remote, receive, after):
+    shape = pre.shape
+
+    def body(recv_ref, in_ref, pre_ref, wn_ref, rem_ref, out_ref):
+        mixed = received(recv_ref, rem_ref, {0: in_ref}, shape[1])
+        out_ref[...] = pre_ref[...] + dot(mixed, wn_ref[layer]).reshape(shape)
+
+    return call(body, "middle", [(shape, F32)], [receive], [incoming, pre, neighbor, remote], after=after)[0]
+
+
+def update(recv_ref, h_ref, rounds, pre_ref, wn, wo, rem_ref):
+    steps, cells, width = h_ref.shape
+    half = 0.5 * (pre_ref[...].reshape(steps * cells, width) + dot(received(recv_ref, rem_ref, rounds, cells), wn))
     activated = (half + half * jnp.tanh(half)).astype(BF16)
-    return (h_ref[step].astype(F32) + dot(activated, wo)).astype(BF16)
+    before = h_ref[...].reshape(steps * cells, width).astype(F32)
+    return (before + dot(activated, wo)).astype(BF16)
 
 
 def far(hidden, incoming, pre, layer, neighbor, output, remote, receive, send_blocks, after):
@@ -131,8 +145,8 @@
 
     def body(recv_ref, blocks_ref, h_ref, *refs):
         in_refs, (pre_ref, wn_ref, wo_ref, rem_ref, out_ref, *send_refs) = refs[:rounds], refs[rounds:]
-        for step in range(steps):
-            out_ref[step] = update(recv_ref, h_ref, in_refs, pre_ref, wn_ref[layer], wo_ref[layer], rem_ref, step)
+        rows = update(recv_ref, h_ref, dict(enumerate(in_refs)), pre_ref, wn_ref[layer], wo_ref[layer], rem_ref)
+        out_ref[...] = rows.reshape(steps, cells, width)
         for r in range(rounds):
             for k in range(sent):
                 at = pl.ds(blocks_ref[0, r, k] * block, block)
@@ -172,20 +186,23 @@
 
 def finish(hidden, incoming, pre, layer, shower, showers, neighbor, output, remote, receive, drift_weight, scale, noise_sum, totals, after):
     steps, cells, width = hidden.shape
-    rounds = len(incoming)
+
+    count = len(incoming)
 
     def body(recv_ref, scale_ref, h_ref, *refs):
-        in_refs, (pre_ref, wn_ref, wo_ref, rem_ref, wd_ref, nz_ref, *_, tot_ref, run_ref) = refs[:rounds], refs[rounds:]
+        rounds = dict(zip(incoming, refs[:count]))
+        pre_ref, wn_ref, wo_ref, rem_ref, wd_ref, nz_ref, *_, tot_ref, run_ref = refs[count:]
+        last = update(recv_ref, h_ref, rounds, pre_ref, wn_ref[layer], wo_ref[layer], rem_ref)
+        terms = dot(last, wd_ref[...])
         drift = None
         for step in range(steps):
-            last = update(recv_ref, h_ref, in_refs, pre_ref, wn_ref[layer], wo_ref[layer], rem_ref, step)
-            term = scale_ref[step] * dot(last, wd_ref[...])
+            term = scale_ref[step] * terms[step * cells : (step + 1) * cells]
             drift = term if drift is None else drift + term
             run = drift + nz_ref[step]
             run_ref[step] = run
         tot_ref[shower] = run.astype(BF16)
 
-    arrays = [hidden, *incoming, pre, neighbor, output, remote, drift_weight, noise_sum, *totals]
+    arrays = [hidden, *incoming.values(), pre, neighbor, output, remote, drift_weight, noise_sum, *totals]
     return call(
         body, "finish", [((showers, cells, width), BF16), ((steps, cells, width), F32)], [receive, scale], arrays,
         after=after, aliases={len(arrays) + 1: 0} if totals else None,
@@ -268,8 +285,11 @@
             token = (pre[s],)
     totals, running = (), [None] * showers
     for s in range(showers):
+        rounds = dict(enumerate(incoming[s]))
+        if s > 0:
+            pre[s] = middle(rounds.pop(0), pre[s], layers - 1, neighbor_weight, remote_values, receive_rows, totals)
         total, running[s] = finish(
-            hidden[s], incoming[s], pre[s], layers - 1, s, showers, *rest, drift_weight, drift_scale, noise_sum[s],
+            hidden[s], rounds, pre[s], layers - 1, s, showers, *rest, drift_weight, drift_scale, noise_sum[s],
             totals, token,
         )
         totals, token = (total,), ()

time: 81.1 us -> 80.9 us (level)
    ppermute x4, waiting for transfers between devices: 3.93 us -> 3.06 us  [local(): incoming[s] = [lax.ppermute(sends[r], 'dom', pairs[r]) for r in (0, 1)]]
    pallas_call x13 -> x14, Pallas kernels: 19.9 us -> 20 us  [call(): pl.pallas_call(inner, out_shape=[pltpu.VMEM(*o) for o in outs] + [pltpu.H...]
  transfers between devices with their start and end apart: 8 -> 8, of which waited for: 2 -> 3; matrix products, arithmetic and copies ran while one was open for 0% -> 0% of each run, Pallas kernels for 19% -> 19%
where the time goes in v5:
time: 80.9 us; the launch traced here: 80.4 us
  blocking collectives  49.6 us (61%)
  Pallas kernels  20 us (25%)
  starting transfers between devices  7.03 us (9%)
  waiting for transfers between devices  3.19 us (4%)
    all_to_all x1, blocking collectives, local(): lax.all_to_all(total.reshape(lax.axis_size('tm'), -1, width), 'tm', 0, 0)  27.7 us
    all_to_all x1, blocking collectives, local(): earlier = lax.all_to_all(exclusive_prefix(pieces), 'tm', 0, 0)  22 us
    pallas_call x14, Pallas kernels, call(): pl.pallas_call(inner, out_shape=[pltpu.VMEM(*o) for o in outs] + [pltpu.H...  20 us
    ppermute x4, starting transfers between devices, local(): incoming[s] = [lax.ppermute(sends[r], 'dom', pairs[r]) for r in (0, 1)]  4.09 us
    ppermute x4, waiting for transfers between devices, local(): incoming[s] = [lax.ppermute(sends[r], 'dom', pairs[r]) for r in (0, 1)]  3.06 us
    ppermute x4, starting transfers between devices, local(): incoming.append([lax.ppermute(sends[r], 'dom', pairs[r]) for r in (0, 1)])  2.93 us
  transfers between devices with their start and end apart: 8, of which 3 were waited for; matrix products, arithmetic and copies ran while one was open for 0% of the time, Pallas kernels for 19%

profile of v5, /device:TPU:2, one launch (start us, length us, event | category | flops | bytes accessed | tf_op | source)
XLA Modules:
  0.0 80.4 jit_solution(16888339168212888592)
XLA Ops:
  0.0 1.4 %pack.2 = (bf16[2,2,128,256]{3,2,1,0:T(8,128)(2,1)S(1)}, bf16[2,2,128,256]{3,2,1,0:T(8,128)(2,1)S(1)}) custom-call(s32[1,2,2]{2,1,0:T(2,128)} %refs_1_.15, f32[2,2,512,256]{3,2,1,0:T(8,128)} %refs_1_.14), custom_call_target="tpu_custom_call" | custom-call | flops 1048576 | bytes 1024 | tf_op jit(solution)/shard_map/pack/pallas_call | solution.py:25
  1.6 2.3 %collective-permute-start.1 = (bf16[2,2,128,256]{3,2,1,0:T(8,128)(2,1)S(1)}, bf16[2,2,128,256]{3,2,1,0:T(8,128)(2,1)S(1)}, u32[]{:S(2)}, u32[]{:S(2)}) collective-permute-start(bf16[2,2,128,256]{3,2,1,0:T(8,128)(2,1)S(1)} %get-tuple-element.27), channel_id=1, source_target_pairs={{0,2},{1,3},{2,0},{3,1},{4,6},{5,7},{6,4},{7,5},{8,10},{9,11},{10,... | collective-permute-start | bytes 786440 | tf_op jit(solution)/shard_map/ppermute | solution.py:270
  3.9 1.3 %pack.3 = (bf16[2,2,128,256]{3,2,1,0:T(8,128)(2,1)S(1)}, bf16[2,2,128,256]{3,2,1,0:T(8,128)(2,1)S(1)}) custom-call(s32[1,2,2]{2,1,0:T(2,128)} %refs_1_.15, f32[2,2,512,256]{3,2,1,0:T(8,128)} %refs_1_.14), custom_call_target="tpu_custom_call" | custom-call | flops 1048576 | bytes 1024 | tf_op jit(solution)/shard_map/pack/pallas_call | solution.py:25
  5.2 0.2 collective-permute-start.4
  5.4 0.3 collective-permute-start.5
  5.7 1.6 %near_first.2 = (f32[2,512,256]{2,1,0:T(8,128)S(1)}, bf16[2,512,256]{2,1,0:T(8,128)(2,1)S(1)}) custom-call(s32[4,4]{1,0:T(4,128)S(1)} %copy-done.7, f32[2,2,512,256]{3,2,1,0:T(8,128)S(1)} %copy-done, f32[2,256]{1,0:T(2,128)S(1)} %copy-done.8, bf16[2,256,256]{2,1,0:T(8,128)(2,1)S(1)} %copy-done.3, bf16[2,256,256]{2,1,0:T(8,128)(2,1)S(1)} %copy-done.1, ...), custom_call_target="tpu_custom_call" | custom-call | flops 1048576 | bytes 1024 | tf_op jit(solution)/shard_map/near_first/pallas_call | solution.py:25
  7.3 1.6 %near_first.3 = (f32[2,512,256]{2,1,0:T(8,128)S(1)}, bf16[2,512,256]{2,1,0:T(8,128)(2,1)S(1)}) custom-call(s32[4,4]{1,0:T(4,128)S(1)} %copy-done.7, f32[2,2,512,256]{3,2,1,0:T(8,128)S(1)} %copy-done, f32[2,256]{1,0:T(2,128)S(1)} %copy-done.8, bf16[2,256,256]{2,1,0:T(8,128)(2,1)S(1)} %copy-done.3, bf16[2,256,256]{2,1,0:T(8,128)(2,1)S(1)} %copy-done.1, ...), custom_call_target="tpu_custom_call" | custom-call | flops 1048576 | bytes 1024 | tf_op jit(solution)/shard_map/near_first/pallas_call | solution.py:25
  9.0 2.4 %noise_sums.1 = (f32[2,512,256]{2,1,0:T(8,128)S(1)}, f32[2,512,256]{2,1,0:T(8,128)S(1)}) custom-call(f32[2]{0:T(128)S(1)} %copy-done.12, bf16[2,2,512,256]{3,2,1,0:T(8,128)(2,1)} %refs_1_.12, f32[2,2,512,256]{3,2,1,0:T(8,128)} %refs_1_.14, f32[2,512,256]{2,1,0:T(8,128)S(1)} %get-tuple-element.29.refs_3_.refs_5_), custom_call_target="tpu_custom_call" | custom-call | flops 1048576 | bytes 1024 | tf_op jit(solution)/shard_map/noise_sums/pallas_call | solution.py:25
  11.4 1.5 %far.2 = (bf16[2,512,256]{2,1,0:T(8,128)(2,1)S(1)}, bf16[2,2,128,256]{3,2,1,0:T(8,128)(2,1)S(1)}, bf16[2,2,128,256]{3,2,1,0:T(8,128)(2,1)S(1)}) custom-call(s32[1,2,2]{2,1,0:T(2,128)S(1)} %copy-done.9, s32[1,2,2]{2,1,0:T(2,128)S(1)} %copy-done.10, bf16[2,512,256]{2,1,0:T(8,128)(2,1)S(1)} %get-tuple-element.25.refs_2_, ...), custom_call_target="tpu_custom_call" | custom-call | flops 1048576 | bytes 1024 | tf_op jit(solution)/shard_map/far/pallas_call | solution.py:25
  12.9 0.2 collective-permute-start.2
  13.1 1.8 %collective-permute-start.3 = (bf16[2,2,128,256]{3,2,1,0:T(8,128)(2,1)S(1)}, bf16[2,2,128,256]{3,2,1,0:T(8,128)(2,1)S(1)}, u32[]{:S(2)}, u32[]{:S(2)}) collective-permute-start(bf16[2,2,128,256]{3,2,1,0:T(8,128)(2,1)S(1)} %get-tuple-element.33), channel_id=1, source_target_pairs={{0,2},{1,3},{2,0},{3,1},{4,6},{5,7},{6,4},{7,5},{8,10},{9,11},{10,... | collective-permute-start | bytes 786440 | tf_op jit(solution)/shard_map/ppermute | solution.py:283
  14.9 1.6 %near.2.refs_9_.refs_5_ = f32[2,512,256]{2,1,0:T(8,128)S(1)} custom-call(s32[4,4]{1,0:T(4,128)S(1)} %copy-done.7, bf16[2,512,256]{2,1,0:T(8,128)(2,1)S(1)} %get-tuple-element.31.refs_1_.refs_2_, f32[2,256]{1,0:T(2,128)S(1)} %copy-done.8, bf16[2,256,256]{2,1,0:T(8,128)(2,1)S(1)} %copy-done.3, bf16[2,256,256]{2,1,0:T(8,128)(2,1)S(1)} %copy-done.1, ...), custom_call_target="tpu_custom_call" | custom-call | flops 1048576 | bytes 1024 | tf_op jit(solution)/shard_map/near/pallas_call | solution.py:25
  16.6 1.4 %far.3 = (bf16[2,512,256]{2,1,0:T(8,128)(2,1)S(1)}, bf16[2,2,128,256]{3,2,1,0:T(8,128)(2,1)S(1)}, bf16[2,2,128,256]{3,2,1,0:T(8,128)(2,1)S(1)}) custom-call(s32[1,2,2]{2,1,0:T(2,128)S(1)} %copy-done.9, s32[1,2,2]{2,1,0:T(2,128)S(1)} %copy-done.10, bf16[2,512,256]{2,1,0:T(8,128)(2,1)S(1)} %get-tuple-element.34.refs_2_, ...), custom_call_target="tpu_custom_call" | custom-call | flops 1048576 | bytes 1024 | tf_op jit(solution)/shard_map/far/pallas_call | solution.py:25
  18.1 0.1 collective-permute-start.7
  18.2 2.0 %collective-permute-start.6 = (bf16[2,2,128,256]{3,2,1,0:T(8,128)(2,1)S(1)}, bf16[2,2,128,256]{3,2,1,0:T(8,128)(2,1)S(1)}, u32[]{:S(2)}, u32[]{:S(2)}) collective-permute-start(bf16[2,2,128,256]{3,2,1,0:T(8,128)(2,1)S(1)} %get-tuple-element.39), channel_id=1, source_target_pairs={{0,2},{1,3},{2,0},{3,1},{4,6},{5,7},{6,4},{7,5},{8,10},{9,11},{10,... | collective-permute-start | bytes 786440 | tf_op jit(solution)/shard_map/ppermute | solution.py:283
  20.2 1.6 %near.3.refs_11_.refs_2_ = f32[2,512,256]{2,1,0:T(8,128)S(1)} custom-call(s32[4,4]{1,0:T(4,128)S(1)} %copy-done.7, bf16[2,512,256]{2,1,0:T(8,128)(2,1)S(1)} %get-tuple-element.37.refs_1_.refs_2_, f32[2,256]{1,0:T(2,128)S(1)} %copy-done.8, bf16[2,256,256]{2,1,0:T(8,128)(2,1)S(1)} %copy-done.3, bf16[2,256,256]{2,1,0:T(8,128)(2,1)S(1)} %copy-done.1, ...), custom_call_target="tpu_custom_call" | custom-call | flops 1048576 | bytes 1024 | tf_op jit(solution)/shard_map/near/pallas_call | solution.py:25
  21.8 0.5 collective-permute-done.3.refs_4_
  22.3 1.7 %finish.2 = (bf16[2,512,256]{2,1,0:T(8,128)(2,1)S(1)}, f32[2,512,256]{2,1,0:T(8,128)S(1)}) custom-call(s32[1,2,2]{2,1,0:T(2,128)S(1)} %copy-done.9, f32[2]{0:T(128)S(1)} %copy-done.11, bf16[2,512,256]{2,1,0:T(8,128)(2,1)S(1)} %get-tuple-element.31.refs_1_.refs_2_, bf16[2,2,128,256]{3,2,1,0:T(8,128)(2,1)S(1)} %collective-permute-done.2.refs_3_, ...), custom_call_target="tpu_custom_call" | custom-call | flops 1048576 | bytes 1024 | tf_op jit(solution)/shard_map/finish/pallas_call | solution.py:25
  24.0 1.0 %middle.1.refs_4_ = f32[2,512,256]{2,1,0:T(8,128)S(1)} custom-call(s32[1,2,2]{2,1,0:T(2,128)S(1)} %copy-done.9, bf16[2,2,128,256]{3,2,1,0:T(8,128)(2,1)S(1)} %collective-permute-done.7.refs_1_, f32[2,512,256]{2,1,0:T(8,128)S(1)} %near.3.refs_11_.refs_2_, bf16[2,256,256]{2,1,0:T(8,128)(2,1)S(1)} %copy-done.1, bf16[1,2,2,128,128]{4,3,2,1,0:T(8,128)(2,1)S(1)} %copy-done.5, ...), custom_call_target="tpu_custom_call" | custom-call | flops 1048576 | bytes 1024 | tf_op jit(solution)/shard_map/middle/pallas_call | solution.py:25
  25.1 2.6 %collective-permute-done.6.refs_3_ = bf16[2,2,128,256]{3,2,1,0:T(8,128)(2,1)S(1)} collective-permute-done((bf16[2,2,128,256]{3,2,1,0:T(8,128)(2,1)S(1)}, bf16[2,2,128,256]{3,2,1,0:T(8,128)(2,1)S(1)}, u32[]{:S(2)}, u32[]{:S(2)}) %collective-permute-start.6) | collective-permute-done | bytes 262176 | tf_op jit(solution)/shard_map/ppermute | solution.py:283
  27.6 1.5 %finish.3 = (bf16[2,512,256]{2,1,0:T(8,128)(2,1)S(1)}, f32[2,512,256]{2,1,0:T(8,128)S(1)}) custom-call(s32[1,2,2]{2,1,0:T(2,128)S(1)} %copy-done.9, f32[2]{0:T(128)S(1)} %copy-done.11, bf16[2,512,256]{2,1,0:T(8,128)(2,1)S(1)} %get-tuple-element.37.refs_1_.refs_2_, ...), custom_call_target="tpu_custom_call", output_to_operand_aliasing={{0}: (10, {})} | custom-call | flops 1048576 | bytes 1024 | tf_op jit(solution)/shard_map/finish/pallas_call | solution.py:25
  29.1 27.7 %all_to_all.10.refs_0_ = bf16[32,32,256]{2,1,0:T(8,128)(2,1)S(1)} all-to-all(bf16[32,32,256]{2,1,0:T(8,128)(2,1)S(1)} %bitcast.2), channel_id=1, replica_groups=mesh['tm'=32,'dom'=8] {'tm'}, dimensions={0} | all-to-all | bytes 1048576 | tf_op jit(solution)/shard_map/all_to_all | solution.py:296
  56.9 22.0 %all_to_all.11 = bf16[32,32,256]{2,1,0:T(8,128)(2,1)S(1)} all-to-all(bf16[32,32,256]{2,1,0:T(8,128)(2,1)S(1)} %exclusive_prefix.1), channel_id=1, replica_groups=mesh['tm'=32,'dom'=8] {'tm'}, dimensions={0} | all-to-all | bytes 1048576 | tf_op jit(solution)/shard_map/all_to_all | solution.py:297
  78.8 1.4 %deliver.1 = f32[2,2,512,256]{3,2,1,0:T(8,128)} custom-call(f32[2,512,256]{2,1,0:T(8,128)S(1)} %get-tuple-element.38.refs_0_, f32[2,512,256]{2,1,0:T(8,128)S(1)} %get-tuple-element.43.refs_1_, bf16[2,512,256]{2,1,0:T(8,128)(2,1)S(1)} %bitcast.3), custom_call_target="tpu_custom_call" | custom-call | flops 1048576 | bytes 1024 | tf_op jit(solution)/shard_map/deliver/pallas_call | solution.py:25
  (34 shorter events, 0.4 us)
Async XLA Ops:
  0.0 5.7 %copy-start = (f32[2,2,512,256]{3,2,1,0:T(8,128)S(1)}, f32[2,2,512,256]{3,2,1,0:T(8,128)}, u32[]{:S(2)}) copy-start(f32[2,2,512,256]{3,2,1,0:T(8,128)} %refs_1_.14) | copy-start | bytes 6291460
  0.0 5.7 %copy-start.1 = (bf16[2,256,256]{2,1,0:T(8,128)(2,1)S(1)}, bf16[2,256,256]{2,1,0:T(8,128)(2,1)}, u32[]{:S(2)}) copy-start(bf16[2,256,256]{2,1,0:T(8,128)(2,1)} %refs_5_.9) | copy-start | bytes 786436
  0.0 5.7 %copy-start.2 = (bf16[4,4,128,128]{3,2,1,0:T(8,128)(2,1)S(1)}, bf16[4,4,128,128]{3,2,1,0:T(8,128)(2,1)}, u32[]{:S(2)}) copy-start(bf16[4,4,128,128]{3,2,1,0:T(8,128)(2,1)} %refs_5_.8) | copy-start | bytes 1572868
  0.0 5.7 %copy-start.7 = (s32[4,4]{1,0:T(4,128)S(1)}, s32[4,4]{1,0:T(4,128)}, u32[]{:S(2)}) copy-start(s32[4,4]{1,0:T(4,128)} %refs_0_.20) | copy-start | bytes 196
  0.0 5.7 %copy-start.3 = (bf16[2,256,256]{2,1,0:T(8,128)(2,1)S(1)}, bf16[2,256,256]{2,1,0:T(8,128)(2,1)}, u32[]{:S(2)}) copy-start(bf16[2,256,256]{2,1,0:T(8,128)(2,1)} %refs_3_.8) | copy-start | bytes 786436
  0.0 5.7 %copy-start.8 = (f32[2,256]{1,0:T(2,128)S(1)}, f32[2,256]{1,0:T(2,128)}, u32[]{:S(2)}) copy-start(f32[2,256]{1,0:T(2,128)} %refs_2_.9) | copy-start | bytes 6148
  1.5 9.9 %collective-permute-start = (bf16[2,2,128,256]{3,2,1,0:T(8,128)(2,1)S(1)}, bf16[2,2,128,256]{3,2,1,0:T(8,128)(2,1)S(1)}, u32[]{:S(2)}, u32[]{:S(2)}) collective-permute-start(bf16[2,2,128,256]{3,2,1,0:T(8,128)(2,1)S(1)} %get-tuple-element.26), channel_id=1, source_target_pairs={{0,1},{1,0},{2,3},{3,2},{4,5},{5,4},{6,7},{7,6},{8,9},{9,8},{10,11... | collective-permute-start | bytes 786440 | tf_op jit(solution)/shard_map/ppermute | solution.py:270
  1.6 9.8 %collective-permute-start.1 = (bf16[2,2,128,256]{3,2,1,0:T(8,128)(2,1)S(1)}, bf16[2,2,128,256]{3,2,1,0:T(8,128)(2,1)S(1)}, u32[]{:S(2)}, u32[]{:S(2)}) collective-permute-start(bf16[2,2,128,256]{3,2,1,0:T(8,128)(2,1)S(1)} %get-tuple-element.27), channel_id=1, source_target_pairs={{0,2},{1,3},{2,0},{3,1},{4,6},{5,7},{6,4},{7,5},{8,10},{9,11},{10,... | collective-permute-start | bytes 786440 | tf_op jit(solution)/shard_map/ppermute | solution.py:270
  5.2 11.3 %collective-permute-start.4 = (bf16[2,2,128,256]{3,2,1,0:T(8,128)(2,1)S(1)}, bf16[2,2,128,256]{3,2,1,0:T(8,128)(2,1)S(1)}, u32[]{:S(2)}, u32[]{:S(2)}) collective-permute-start(bf16[2,2,128,256]{3,2,1,0:T(8,128)(2,1)S(1)} %get-tuple-element.35), channel_id=1, source_target_pairs={{0,1},{1,0},{2,3},{3,2},{4,5},{5,4},{6,7},{7,6},{8,9},{9,8},{10,11... | collective-permute-start | bytes 786440 | tf_op jit(solution)/shard_map/ppermute | solution.py:270
  5.4 11.2 %collective-permute-start.5 = (bf16[2,2,128,256]{3,2,1,0:T(8,128)(2,1)S(1)}, bf16[2,2,128,256]{3,2,1,0:T(8,128)(2,1)S(1)}, u32[]{:S(2)}, u32[]{:S(2)}) collective-permute-start(bf16[2,2,128,256]{3,2,1,0:T(8,128)(2,1)S(1)} %get-tuple-element.36), channel_id=1, source_target_pairs={{0,2},{1,3},{2,0},{3,1},{4,6},{5,7},{6,4},{7,5},{8,10},{9,11},{10,... | collective-permute-start | bytes 786440 | tf_op jit(solution)/shard_map/ppermute | solution.py:270
  7.3 1.6 %copy-start.12 = (f32[2]{0:T(128)S(1)}, f32[2]{0:T(128)}, u32[]{:S(2)}) copy-start(f32[2]{0:T(128)} %refs_0_.15) | copy-start | bytes 28
  9.0 2.4 %copy-start.4 = (bf16[2,256,256]{2,1,0:T(8,128)(2,1)S(1)}, bf16[2,256,256]{2,1,0:T(8,128)(2,1)}, u32[]{:S(2)}) copy-start(bf16[2,256,256]{2,1,0:T(8,128)(2,1)} %refs_6_.7) | copy-start | bytes 786436
  9.0 2.4 %copy-start.5 = (bf16[1,2,2,128,128]{4,3,2,1,0:T(8,128)(2,1)S(1)}, bf16[1,2,2,128,128]{4,3,2,1,0:T(8,128)(2,1)}, u32[]{:S(2)}) copy-start(bf16[1,2,2,128,128]{4,3,2,1,0:T(8,128)(2,1)} %refs_7_.7) | copy-start | bytes 393220
  9.0 2.4 %copy-start.9 = (s32[1,2,2]{2,1,0:T(2,128)S(1)}, s32[1,2,2]{2,1,0:T(2,128)}, u32[]{:S(2)}) copy-start(s32[1,2,2]{2,1,0:T(2,128)} %refs_0_.23) | copy-start | bytes 52
  9.0 2.4 %copy-start.10 = (s32[1,2,2]{2,1,0:T(2,128)S(1)}, s32[1,2,2]{2,1,0:T(2,128)}, u32[]{:S(2)}) copy-start(s32[1,2,2]{2,1,0:T(2,128)} %refs_1_.15) | copy-start | bytes 52
  12.9 8.9 %collective-permute-start.2 = (bf16[2,2,128,256]{3,2,1,0:T(8,128)(2,1)S(1)}, bf16[2,2,128,256]{3,2,1,0:T(8,128)(2,1)S(1)}, u32[]{:S(2)}, u32[]{:S(2)}) collective-permute-start(bf16[2,2,128,256]{3,2,1,0:T(8,128)(2,1)S(1)} %get-tuple-element.32), channel_id=1, source_target_pairs={{0,1},{1,0},{2,3},{3,2},{4,5},{5,4},{6,7},{7,6},{8,9},{9,8},{10,11... | collective-permute-start | bytes 786440 | tf_op jit(solution)/shard_map/ppermute | solution.py:283
  13.1 9.2 %collective-permute-start.3 = (bf16[2,2,128,256]{3,2,1,0:T(8,128)(2,1)S(1)}, bf16[2,2,128,256]{3,2,1,0:T(8,128)(2,1)S(1)}, u32[]{:S(2)}, u32[]{:S(2)}) collective-permute-start(bf16[2,2,128,256]{3,2,1,0:T(8,128)(2,1)S(1)} %get-tuple-element.33), channel_id=1, source_target_pairs={{0,2},{1,3},{2,0},{3,1},{4,6},{5,7},{6,4},{7,5},{8,10},{9,11},{10,... | collective-permute-start | bytes 786440 | tf_op jit(solution)/shard_map/ppermute | solution.py:283
  18.0 4.2 %copy-start.6 = (bf16[256,256]{1,0:T(8,128)(2,1)S(1)}, bf16[256,256]{1,0:T(8,128)(2,1)}, u32[]{:S(2)}) copy-start(bf16[256,256]{1,0:T(8,128)(2,1)} %refs_8_.7) | copy-start | bytes 393220
  18.1 4.2 %copy-start.11 = (f32[2]{0:T(128)S(1)}, f32[2]{0:T(128)}, u32[]{:S(2)}) copy-start(f32[2]{0:T(128)} %refs_1_.17) | copy-start | bytes 28
  18.1 5.9 %collective-permute-start.7 = (bf16[2,2,128,256]{3,2,1,0:T(8,128)(2,1)S(1)}, bf16[2,2,128,256]{3,2,1,0:T(8,128)(2,1)S(1)}, u32[]{:S(2)}, u32[]{:S(2)}) collective-permute-start(bf16[2,2,128,256]{3,2,1,0:T(8,128)(2,1)S(1)} %get-tuple-element.40), channel_id=1, source_target_pairs={{0,1},{1,0},{2,3},{3,2},{4,5},{5,4},{6,7},{7,6},{8,9},{9,8},{10,11... | collective-permute-start | bytes 786440 | tf_op jit(solution)/shard_map/ppermute | solution.py:283
  18.2 9.4 %collective-permute-start.6 = (bf16[2,2,128,256]{3,2,1,0:T(8,128)(2,1)S(1)}, bf16[2,2,128,256]{3,2,1,0:T(8,128)(2,1)S(1)}, u32[]{:S(2)}, u32[]{:S(2)}) collective-permute-start(bf16[2,2,128,256]{3,2,1,0:T(8,128)(2,1)S(1)} %get-tuple-element.39), channel_id=1, source_target_pairs={{0,2},{1,3},{2,0},{3,1},{4,6},{5,7},{6,4},{7,5},{8,10},{9,11},{10,... | collective-permute-start | bytes 786440 | tf_op jit(solution)/shard_map/ppermute | solution.py:283

commit v6 on v5

--- a/solution.py
+++ b/solution.py
@@ -106,15 +106,35 @@
     )
 
 
-def received(recv_ref, rem_ref, rounds, cells):
+def goes_to(recv_ref):
+    return lambda r, k, b: jnp.where(recv_ref[0, r, k] == b, 1.0, 0.0)
+
+
+def tables(receive, scale, parts, width, after):
+    _, rounds, sent = receive.shape
+    steps = scale.shape[0]
+
+    def body(recv_ref, scale_ref, mask_ref, scales_ref):
+        mask = goes_to(recv_ref)
+        for i in range(rounds * sent * parts):
+            r, k, b = i // (sent * parts), i // parts % sent, i % parts
+            mask_ref[i] = jnp.broadcast_to(mask(r, k, b), (1, width))
+        for step in range(steps):
+            scales_ref[step] = jnp.broadcast_to(scale_ref[step], (1, width))
+
+    outs = [((rounds * sent * parts, 1, width), F32), ((steps, 1, width), F32)]
+    return call(body, "tables", outs, [receive, scale], [], after=after)
+
+
+def received(mask, rem_ref, rounds, cells):
     steps, sent, block, _ = next(iter(rounds.values())).shape
     mixed = []
     for step in range(steps):
-        addends = [(recv_ref[0, r, k], dot(rem_ref[0, r, k], in_ref[step, k])) for r, in_ref in rounds.items() for k in range(sent)]
+        addends = [((r, k), dot(rem_ref[0, r, k], in_ref[step, k])) for r, in_ref in rounds.items() for k in range(sent)]
         for b in range(cells // block):
             total = None
-            for row, addend in addends:
-                term = jnp.where(row == b, 1.0, 0.0) * addend
+            for place, addend in addends:
+                term = mask(*place, b) * addend
                 total = term if total is None else total + term
             mixed.append(total.astype(BF16))
     return jnp.concatenate(mixed, axis=0)
@@ -124,15 +144,15 @@
     shape = pre.shape
 
     def body(recv_ref, in_ref, pre_ref, wn_ref, rem_ref, out_ref):
-        mixed = received(recv_ref, rem_ref, {0: in_ref}, shape[1])
+        mixed = received(goes_to(recv_ref), rem_ref, {0: in_ref}, shape[1])
         out_ref[...] = pre_ref[...] + dot(mixed, wn_ref[layer]).reshape(shape)
 
     return call(body, "middle", [(shape, F32)], [receive], [incoming, pre, neighbor, remote], after=after)[0]
 
 
-def update(recv_ref, h_ref, rounds, pre_ref, wn, wo, rem_ref):
+def update(mask, h_ref, rounds, pre_ref, wn, wo, rem_ref):
     steps, cells, width = h_ref.shape
-    half = 0.5 * (pre_ref[...].reshape(steps * cells, width) + dot(received(recv_ref, rem_ref, rounds, cells), wn))
+    half = 0.5 * (pre_ref[...].reshape(steps * cells, width) + dot(received(mask, rem_ref, rounds, cells), wn))
     activated = (half + half * jnp.tanh(half)).astype(BF16)
     before = h_ref[...].reshape(steps * cells, width).astype(F32)
     return (before + dot(activated, wo)).astype(BF16)
@@ -145,7 +165,7 @@
 
     def body(recv_ref, blocks_ref, h_ref, *refs):
         in_refs, (pre_ref, wn_ref, wo_ref, rem_ref, out_ref, *send_refs) = refs[:rounds], refs[rounds:]
-        rows = update(recv_ref, h_ref, dict(enumerate(in_refs)), pre_ref, wn_ref[layer], wo_ref[layer], rem_ref)
+        rows = update(goes_to(recv_ref), h_ref, dict(enumerate(in_refs)), pre_ref, wn_ref[layer], wo_ref[layer], rem_ref)
         out_ref[...] = rows.reshape(steps, cells, width)
         for r in range(rounds):
             for k in range(sent):
@@ -184,15 +204,17 @@
     )
 
 
-def finish(hidden, incoming, pre, layer, shower, showers, neighbor, output, remote, receive, drift_weight, scale, noise_sum, totals, after):
+def finish(hidden, incoming, pre, layer, shower, showers, neighbor, output, remote, drift_weight, vectors, noise_sum, totals, after):
     steps, cells, width = hidden.shape
 
     count = len(incoming)
-
-    def body(recv_ref, scale_ref, h_ref, *refs):
+    parts, sent = cells // remote.shape[3], remote.shape[2]
+
+    def body(h_ref, *refs):
         rounds = dict(zip(incoming, refs[:count]))
-        pre_ref, wn_ref, wo_ref, rem_ref, wd_ref, nz_ref, *_, tot_ref, run_ref = refs[count:]
-        last = update(recv_ref, h_ref, rounds, pre_ref, wn_ref[layer], wo_ref[layer], rem_ref)
+        pre_ref, wn_ref, wo_ref, rem_ref, wd_ref, mask_ref, scale_ref, nz_ref, *_, tot_ref, run_ref = refs[count:]
+        mask = lambda r, k, b: mask_ref[(r * sent + k) * parts + b]
+        last = update(mask, h_ref, rounds, pre_ref, wn_ref[layer], wo_ref[layer], rem_ref)
         terms = dot(last, wd_ref[...])
         drift = None
         for step in range(steps):
@@ -202,10 +224,10 @@
             run_ref[step] = run
         tot_ref[shower] = run.astype(BF16)
 
-    arrays = [hidden, *incoming.values(), pre, neighbor, output, remote, drift_weight, noise_sum, *totals]
-    return call(
-        body, "finish", [((showers, cells, width), BF16), ((steps, cells, width), F32)], [receive, scale], arrays,
-        after=after, aliases={len(arrays) + 1: 0} if totals else None,
+    arrays = [hidden, *incoming.values(), pre, neighbor, output, remote, drift_weight, *vectors, noise_sum, *totals]
+    return call(
+        body, "finish", [((showers, cells, width), BF16), ((steps, cells, width), F32)], [], arrays,
+        after=after, aliases={len(arrays) - 1: 0} if totals else None,
     )
 
 
@@ -277,6 +299,7 @@
         token = (pre[s],)
     noise_sum = noise_sums(noise_draws, noise_scale, iterates, token)
     token = (noise_sum[0],)
+    vectors = tables(receive_rows, drift_scale, cells // block, width, token)
     for layer in range(1, layers):
         for s in range(showers):
             hidden[s], *sends = far(hidden[s], incoming[s], pre[s], layer - 1, *rest, send_blocks, token)
@@ -289,7 +312,7 @@
         if s > 0:
             pre[s] = middle(rounds.pop(0), pre[s], layers - 1, neighbor_weight, remote_values, receive_rows, totals)
         total, running[s] = finish(
-            hidden[s], rounds, pre[s], layers - 1, s, showers, *rest, drift_weight, drift_scale, noise_sum[s],
+            hidden[s], rounds, pre[s], layers - 1, s, showers, *rest[:3], drift_weight, vectors, noise_sum[s],
             totals, token,
         )
         totals, token = (total,), ()

time: 80.9 us -> 80.3 us (level)
    pallas_call x14 -> x15, Pallas kernels: 20 us -> 19.6 us  [call(): pl.pallas_call(inner, out_shape=[pltpu.VMEM(*o) for o in outs] + [pltpu.H...]
  transfers between devices with their start and end apart: 8 -> 8, of which waited for: 3 -> 2; matrix products, arithmetic and copies ran while one was open for 0% -> 0% of each run, Pallas kernels for 19% -> 20%
where the time goes in v6:
time: 80.3 us; the launch traced here: 79.9 us
  blocking collectives  49.6 us (62%)
  Pallas kernels  19.6 us (24%)
  starting transfers between devices  7.03 us (9%)
  waiting for transfers between devices  3.1 us (4%)
    all_to_all x1, blocking collectives, local(): lax.all_to_all(total.reshape(lax.axis_size('tm'), -1, width), 'tm', 0, 0)  27.7 us
    all_to_all x1, blocking collectives, local(): earlier = lax.all_to_all(exclusive_prefix(pieces), 'tm', 0, 0)  22 us
    pallas_call x15, Pallas kernels, call(): pl.pallas_call(inner, out_shape=[pltpu.VMEM(*o) for o in outs] + [pltpu.H...  19.6 us
    ppermute x4, starting transfers between devices, local(): incoming[s] = [lax.ppermute(sends[r], 'dom', pairs[r]) for r in (0, 1)]  4.09 us
    ppermute x4, waiting for transfers between devices, local(): incoming[s] = [lax.ppermute(sends[r], 'dom', pairs[r]) for r in (0, 1)]  3 us
    ppermute x4, starting transfers between devices, local(): incoming.append([lax.ppermute(sends[r], 'dom', pairs[r]) for r in (0, 1)])  2.93 us
  transfers between devices with their start and end apart: 8, of which 2 were waited for; matrix products, arithmetic and copies ran while one was open for 0% of the time, Pallas kernels for 20%

profile of v6, /device:TPU:2, one launch (start us, length us, event | category | flops | bytes accessed | tf_op | source)
XLA Modules:
  0.0 79.9 jit_solution(139146666548017691)
XLA Ops:
  0.0 1.4 %pack.2 = (bf16[2,2,128,256]{3,2,1,0:T(8,128)(2,1)S(1)}, bf16[2,2,128,256]{3,2,1,0:T(8,128)(2,1)S(1)}) custom-call(s32[1,2,2]{2,1,0:T(2,128)} %refs_1_.15, f32[2,2,512,256]{3,2,1,0:T(8,128)} %refs_1_.14), custom_call_target="tpu_custom_call" | custom-call | flops 1048576 | bytes 1024 | tf_op jit(solution)/shard_map/pack/pallas_call | solution.py:25
  1.6 2.3 %collective-permute-start.1 = (bf16[2,2,128,256]{3,2,1,0:T(8,128)(2,1)S(1)}, bf16[2,2,128,256]{3,2,1,0:T(8,128)(2,1)S(1)}, u32[]{:S(2)}, u32[]{:S(2)}) collective-permute-start(bf16[2,2,128,256]{3,2,1,0:T(8,128)(2,1)S(1)} %get-tuple-element.29), channel_id=1, source_target_pairs={{0,2},{1,3},{2,0},{3,1},{4,6},{5,7},{6,4},{7,5},{8,10},{9,11},{10,... | collective-permute-start | bytes 786440 | tf_op jit(solution)/shard_map/ppermute | solution.py:292
  3.9 1.3 %pack.3 = (bf16[2,2,128,256]{3,2,1,0:T(8,128)(2,1)S(1)}, bf16[2,2,128,256]{3,2,1,0:T(8,128)(2,1)S(1)}) custom-call(s32[1,2,2]{2,1,0:T(2,128)} %refs_1_.15, f32[2,2,512,256]{3,2,1,0:T(8,128)} %refs_1_.14), custom_call_target="tpu_custom_call" | custom-call | flops 1048576 | bytes 1024 | tf_op jit(solution)/shard_map/pack/pallas_call | solution.py:25
  5.2 0.2 collective-permute-start.4
  5.4 0.3 collective-permute-start.5
  5.7 1.6 %near_first.2 = (f32[2,512,256]{2,1,0:T(8,128)S(1)}, bf16[2,512,256]{2,1,0:T(8,128)(2,1)S(1)}) custom-call(s32[4,4]{1,0:T(4,128)S(1)} %copy-done.7, f32[2,2,512,256]{3,2,1,0:T(8,128)S(1)} %copy-done, f32[2,256]{1,0:T(2,128)S(1)} %copy-done.8, bf16[2,256,256]{2,1,0:T(8,128)(2,1)S(1)} %copy-done.3, bf16[2,256,256]{2,1,0:T(8,128)(2,1)S(1)} %copy-done.1, ...), custom_call_target="tpu_custom_call" | custom-call | flops 1048576 | bytes 1024 | tf_op jit(solution)/shard_map/near_first/pallas_call | solution.py:25
  7.3 1.6 %near_first.3 = (f32[2,512,256]{2,1,0:T(8,128)S(1)}, bf16[2,512,256]{2,1,0:T(8,128)(2,1)S(1)}) custom-call(s32[4,4]{1,0:T(4,128)S(1)} %copy-done.7, f32[2,2,512,256]{3,2,1,0:T(8,128)S(1)} %copy-done, f32[2,256]{1,0:T(2,128)S(1)} %copy-done.8, bf16[2,256,256]{2,1,0:T(8,128)(2,1)S(1)} %copy-done.3, bf16[2,256,256]{2,1,0:T(8,128)(2,1)S(1)} %copy-done.1, ...), custom_call_target="tpu_custom_call" | custom-call | flops 1048576 | bytes 1024 | tf_op jit(solution)/shard_map/near_first/pallas_call | solution.py:25
  9.0 2.4 %noise_sums.1 = (f32[2,512,256]{2,1,0:T(8,128)S(1)}, f32[2,512,256]{2,1,0:T(8,128)S(1)}) custom-call(f32[2]{0:T(128)S(1)} %copy-done.11, bf16[2,2,512,256]{3,2,1,0:T(8,128)(2,1)} %refs_1_.11, f32[2,2,512,256]{3,2,1,0:T(8,128)} %refs_1_.14, f32[2,512,256]{2,1,0:T(8,128)S(1)} %get-tuple-element.31.refs_3_.refs_5_), custom_call_target="tpu_custom_call" | custom-call | flops 1048576 | bytes 1024 | tf_op jit(solution)/shard_map/noise_sums/pallas_call | solution.py:25
  11.4 1.4 %far.2 = (bf16[2,512,256]{2,1,0:T(8,128)(2,1)S(1)}, bf16[2,2,128,256]{3,2,1,0:T(8,128)(2,1)S(1)}, bf16[2,2,128,256]{3,2,1,0:T(8,128)(2,1)S(1)}) custom-call(s32[1,2,2]{2,1,0:T(2,128)S(1)} %copy-done.10, s32[1,2,2]{2,1,0:T(2,128)S(1)} %copy-done.9, bf16[2,512,256]{2,1,0:T(8,128)(2,1)S(1)} %get-tuple-element.27.refs_2_, ...), custom_call_target="tpu_custom_call" | custom-call | flops 1048576 | bytes 1024 | tf_op jit(solution)/shard_map/far/pallas_call | solution.py:25
  12.9 0.2 collective-permute-start.2
  13.1 1.8 %collective-permute-start.3 = (bf16[2,2,128,256]{3,2,1,0:T(8,128)(2,1)S(1)}, bf16[2,2,128,256]{3,2,1,0:T(8,128)(2,1)S(1)}, u32[]{:S(2)}, u32[]{:S(2)}) collective-permute-start(bf16[2,2,128,256]{3,2,1,0:T(8,128)(2,1)S(1)} %get-tuple-element.35), channel_id=1, source_target_pairs={{0,2},{1,3},{2,0},{3,1},{4,6},{5,7},{6,4},{7,5},{8,10},{9,11},{10,... | collective-permute-start | bytes 786440 | tf_op jit(solution)/shard_map/ppermute | solution.py:306
  14.9 1.6 %near.2.refs_9_.refs_3_ = f32[2,512,256]{2,1,0:T(8,128)S(1)} custom-call(s32[4,4]{1,0:T(4,128)S(1)} %copy-done.7, bf16[2,512,256]{2,1,0:T(8,128)(2,1)S(1)} %get-tuple-element.33.refs_1_.refs_0_, f32[2,256]{1,0:T(2,128)S(1)} %copy-done.8, bf16[2,256,256]{2,1,0:T(8,128)(2,1)S(1)} %copy-done.3, bf16[2,256,256]{2,1,0:T(8,128)(2,1)S(1)} %copy-done.1, ...), custom_call_target="tpu_custom_call" | custom-call | flops 1048576 | bytes 1024 | tf_op jit(solution)/shard_map/near/pallas_call | solution.py:25
  16.6 1.4 %far.3 = (bf16[2,512,256]{2,1,0:T(8,128)(2,1)S(1)}, bf16[2,2,128,256]{3,2,1,0:T(8,128)(2,1)S(1)}, bf16[2,2,128,256]{3,2,1,0:T(8,128)(2,1)S(1)}) custom-call(s32[1,2,2]{2,1,0:T(2,128)S(1)} %copy-done.10, s32[1,2,2]{2,1,0:T(2,128)S(1)} %copy-done.9, bf16[2,512,256]{2,1,0:T(8,128)(2,1)S(1)} %get-tuple-element.38.refs_2_, ...), custom_call_target="tpu_custom_call" | custom-call | flops 1048576 | bytes 1024 | tf_op jit(solution)/shard_map/far/pallas_call | solution.py:25
  18.0 0.2 collective-permute-start.7
  18.2 2.0 %collective-permute-start.6 = (bf16[2,2,128,256]{3,2,1,0:T(8,128)(2,1)S(1)}, bf16[2,2,128,256]{3,2,1,0:T(8,128)(2,1)S(1)}, u32[]{:S(2)}, u32[]{:S(2)}) collective-permute-start(bf16[2,2,128,256]{3,2,1,0:T(8,128)(2,1)S(1)} %get-tuple-element.43), channel_id=1, source_target_pairs={{0,2},{1,3},{2,0},{3,1},{4,6},{5,7},{6,4},{7,5},{8,10},{9,11},{10,... | collective-permute-start | bytes 786440 | tf_op jit(solution)/shard_map/ppermute | solution.py:306
  20.2 0.6 tables.1
  20.8 1.6 %near.3.refs_11_.refs_2_ = f32[2,512,256]{2,1,0:T(8,128)S(1)} custom-call(s32[4,4]{1,0:T(4,128)S(1)} %copy-done.7, bf16[2,512,256]{2,1,0:T(8,128)(2,1)S(1)} %get-tuple-element.41.refs_1_.refs_0_, f32[2,256]{1,0:T(2,128)S(1)} %copy-done.8, bf16[2,256,256]{2,1,0:T(8,128)(2,1)S(1)} %copy-done.3, bf16[2,256,256]{2,1,0:T(8,128)(2,1)S(1)} %copy-done.1, ...), custom_call_target="tpu_custom_call" | custom-call | flops 1048576 | bytes 1024 | tf_op jit(solution)/shard_map/near/pallas_call | solution.py:25
  22.4 1.2 %finish.2 = (bf16[2,512,256]{2,1,0:T(8,128)(2,1)S(1)}, f32[2,512,256]{2,1,0:T(8,128)S(1)}) custom-call(bf16[2,512,256]{2,1,0:T(8,128)(2,1)S(1)} %get-tuple-element.33.refs_1_.refs_0_, bf16[2,2,128,256]{3,2,1,0:T(8,128)(2,1)S(1)} %collective-permute-done.2.refs_1_, bf16[2,2,128,256]{3,2,1,0:T(8,128)(2,1)S(1)} %collective-permute-done.3.refs_2_, ...), custom_call_target="tpu_custom_call" | custom-call | flops 1048576 | bytes 1024 | tf_op jit(solution)/shard_map/finish/pallas_call | solution.py:25
  23.6 1.1 %middle.1.refs_2_ = f32[2,512,256]{2,1,0:T(8,128)S(1)} custom-call(s32[1,2,2]{2,1,0:T(2,128)S(1)} %copy-done.10, bf16[2,2,128,256]{3,2,1,0:T(8,128)(2,1)S(1)} %collective-permute-done.7.refs_1_, f32[2,512,256]{2,1,0:T(8,128)S(1)} %near.3.refs_11_.refs_2_, bf16[2,256,256]{2,1,0:T(8,128)(2,1)S(1)} %copy-done.1, bf16[1,2,2,128,128]{4,3,2,1,0:T(8,128)(2,1)S(1)} %copy-done.5, ...), custom_call_target="tpu_custom_call" | custom-call | flops 1048576 | bytes 1024 | tf_op jit(solution)/shard_map/middle/pallas_call | solution.py:25
  24.6 3.0 %collective-permute-done.6.refs_1_ = bf16[2,2,128,256]{3,2,1,0:T(8,128)(2,1)S(1)} collective-permute-done((bf16[2,2,128,256]{3,2,1,0:T(8,128)(2,1)S(1)}, bf16[2,2,128,256]{3,2,1,0:T(8,128)(2,1)S(1)}, u32[]{:S(2)}, u32[]{:S(2)}) %collective-permute-start.6) | collective-permute-done | bytes 262176 | tf_op jit(solution)/shard_map/ppermute | solution.py:306
  27.6 0.9 %finish.3 = (bf16[2,512,256]{2,1,0:T(8,128)(2,1)S(1)}, f32[2,512,256]{2,1,0:T(8,128)S(1)}) custom-call(bf16[2,512,256]{2,1,0:T(8,128)(2,1)S(1)} %get-tuple-element.41.refs_1_.refs_0_, bf16[2,2,128,256]{3,2,1,0:T(8,128)(2,1)S(1)} %collective-permute-done.6.refs_1_, f32[2,512,256]{2,1,0:T(8,128)S(1)} %middle.1.refs_2_, ...), custom_call_target="tpu_custom_call", output_to_operand_aliasing={{0}: (10, {})} | custom-call | flops 1048576 | bytes 1024 | tf_op jit(solution)/shard_map/finish/pallas_call | solution.py:25
  28.6 27.7 %all_to_all.10.refs_0_ = bf16[32,32,256]{2,1,0:T(8,128)(2,1)S(1)} all-to-all(bf16[32,32,256]{2,1,0:T(8,128)(2,1)S(1)} %bitcast.2), channel_id=1, replica_groups=mesh['tm'=32,'dom'=8] {'tm'}, dimensions={0} | all-to-all | bytes 1048576 | tf_op jit(solution)/shard_map/all_to_all | solution.py:319
  56.3 22.0 %all_to_all.11 = bf16[32,32,256]{2,1,0:T(8,128)(2,1)S(1)} all-to-all(bf16[32,32,256]{2,1,0:T(8,128)(2,1)S(1)} %exclusive_prefix.1), channel_id=1, replica_groups=mesh['tm'=32,'dom'=8] {'tm'}, dimensions={0} | all-to-all | bytes 1048576 | tf_op jit(solution)/shard_map/all_to_all | solution.py:320
  78.3 1.4 %deliver.1 = f32[2,2,512,256]{3,2,1,0:T(8,128)} custom-call(f32[2,512,256]{2,1,0:T(8,128)S(1)} %get-tuple-element.42.refs_0_, f32[2,512,256]{2,1,0:T(8,128)S(1)} %get-tuple-element.47.refs_1_, bf16[2,512,256]{2,1,0:T(8,128)(2,1)S(1)} %bitcast.3), custom_call_target="tpu_custom_call" | custom-call | flops 1048576 | bytes 1024 | tf_op jit(solution)/shard_map/deliver/pallas_call | solution.py:25
  (35 shorter events, 0.4 us)
Async XLA Ops:
  0.0 5.7 %copy-start = (f32[2,2,512,256]{3,2,1,0:T(8,128)S(1)}, f32[2,2,512,256]{3,2,1,0:T(8,128)}, u32[]{:S(2)}) copy-start(f32[2,2,512,256]{3,2,1,0:T(8,128)} %refs_1_.14) | copy-start | bytes 6291460
  0.0 5.7 %copy-start.1 = (bf16[2,256,256]{2,1,0:T(8,128)(2,1)S(1)}, bf16[2,256,256]{2,1,0:T(8,128)(2,1)}, u32[]{:S(2)}) copy-start(bf16[2,256,256]{2,1,0:T(8,128)(2,1)} %refs_3_.11) | copy-start | bytes 786436
  0.0 5.7 %copy-start.2 = (bf16[4,4,128,128]{3,2,1,0:T(8,128)(2,1)S(1)}, bf16[4,4,128,128]{3,2,1,0:T(8,128)(2,1)}, u32[]{:S(2)}) copy-start(bf16[4,4,128,128]{3,2,1,0:T(8,128)(2,1)} %refs_5_.9) | copy-start | bytes 1572868
  0.0 5.7 %copy-start.7 = (s32[4,4]{1,0:T(4,128)S(1)}, s32[4,4]{1,0:T(4,128)}, u32[]{:S(2)}) copy-start(s32[4,4]{1,0:T(4,128)} %refs_0_.20) | copy-start | bytes 196
  0.0 5.7 %copy-start.3 = (bf16[2,256,256]{2,1,0:T(8,128)(2,1)S(1)}, bf16[2,256,256]{2,1,0:T(8,128)(2,1)}, u32[]{:S(2)}) copy-start(bf16[2,256,256]{2,1,0:T(8,128)(2,1)} %refs_3_.9) | copy-start | bytes 786436
  0.0 5.7 %copy-start.8 = (f32[2,256]{1,0:T(2,128)S(1)}, f32[2,256]{1,0:T(2,128)}, u32[]{:S(2)}) copy-start(f32[2,256]{1,0:T(2,128)} %refs_2_.9) | copy-start | bytes 6148
  1.5 9.9 %collective-permute-start = (bf16[2,2,128,256]{3,2,1,0:T(8,128)(2,1)S(1)}, bf16[2,2,128,256]{3,2,1,0:T(8,128)(2,1)S(1)}, u32[]{:S(2)}, u32[]{:S(2)}) collective-permute-start(bf16[2,2,128,256]{3,2,1,0:T(8,128)(2,1)S(1)} %get-tuple-element.28), channel_id=1, source_target_pairs={{0,1},{1,0},{2,3},{3,2},{4,5},{5,4},{6,7},{7,6},{8,9},{9,8},{10,11... | collective-permute-start | bytes 786440 | tf_op jit(solution)/shard_map/ppermute | solution.py:292
  1.6 9.8 %collective-permute-start.1 = (bf16[2,2,128,256]{3,2,1,0:T(8,128)(2,1)S(1)}, bf16[2,2,128,256]{3,2,1,0:T(8,128)(2,1)S(1)}, u32[]{:S(2)}, u32[]{:S(2)}) collective-permute-start(bf16[2,2,128,256]{3,2,1,0:T(8,128)(2,1)S(1)} %get-tuple-element.29), channel_id=1, source_target_pairs={{0,2},{1,3},{2,0},{3,1},{4,6},{5,7},{6,4},{7,5},{8,10},{9,11},{10,... | collective-permute-start | bytes 786440 | tf_op jit(solution)/shard_map/ppermute | solution.py:292
  5.2 11.3 %collective-permute-start.4 = (bf16[2,2,128,256]{3,2,1,0:T(8,128)(2,1)S(1)}, bf16[2,2,128,256]{3,2,1,0:T(8,128)(2,1)S(1)}, u32[]{:S(2)}, u32[]{:S(2)}) collective-permute-start(bf16[2,2,128,256]{3,2,1,0:T(8,128)(2,1)S(1)} %get-tuple-element.39), channel_id=1, source_target_pairs={{0,1},{1,0},{2,3},{3,2},{4,5},{5,4},{6,7},{7,6},{8,9},{9,8},{10,11... | collective-permute-start | bytes 786440 | tf_op jit(solution)/shard_map/ppermute | solution.py:292
  5.4 11.2 %collective-permute-start.5 = (bf16[2,2,128,256]{3,2,1,0:T(8,128)(2,1)S(1)}, bf16[2,2,128,256]{3,2,1,0:T(8,128)(2,1)S(1)}, u32[]{:S(2)}, u32[]{:S(2)}) collective-permute-start(bf16[2,2,128,256]{3,2,1,0:T(8,128)(2,1)S(1)} %get-tuple-element.40), channel_id=1, source_target_pairs={{0,2},{1,3},{2,0},{3,1},{4,6},{5,7},{6,4},{7,5},{8,10},{9,11},{10,... | collective-permute-start | bytes 786440 | tf_op jit(solution)/shard_map/ppermute | solution.py:292
  7.3 1.6 %copy-start.11 = (f32[2]{0:T(128)S(1)}, f32[2]{0:T(128)}, u32[]{:S(2)}) copy-start(f32[2]{0:T(128)} %refs_0_.14) | copy-start | bytes 28
  9.0 2.4 %copy-start.4 = (bf16[2,256,256]{2,1,0:T(8,128)(2,1)S(1)}, bf16[2,256,256]{2,1,0:T(8,128)(2,1)}, u32[]{:S(2)}) copy-start(bf16[2,256,256]{2,1,0:T(8,128)(2,1)} %refs_4_.13) | copy-start | bytes 786436
  9.0 2.4 %copy-start.5 = (bf16[1,2,2,128,128]{4,3,2,1,0:T(8,128)(2,1)S(1)}, bf16[1,2,2,128,128]{4,3,2,1,0:T(8,128)(2,1)}, u32[]{:S(2)}) copy-start(bf16[1,2,2,128,128]{4,3,2,1,0:T(8,128)(2,1)} %refs_5_.11) | copy-start | bytes 393220
  9.0 2.4 %copy-start.9 = (s32[1,2,2]{2,1,0:T(2,128)S(1)}, s32[1,2,2]{2,1,0:T(2,128)}, u32[]{:S(2)}) copy-start(s32[1,2,2]{2,1,0:T(2,128)} %refs_1_.15) | copy-start | bytes 52
  9.0 2.4 %copy-start.10 = (s32[1,2,2]{2,1,0:T(2,128)S(1)}, s32[1,2,2]{2,1,0:T(2,128)}, u32[]{:S(2)}) copy-start(s32[1,2,2]{2,1,0:T(2,128)} %refs_0_.21) | copy-start | bytes 52
  12.9 9.5 %collective-permute-start.2 = (bf16[2,2,128,256]{3,2,1,0:T(8,128)(2,1)S(1)}, bf16[2,2,128,256]{3,2,1,0:T(8,128)(2,1)S(1)}, u32[]{:S(2)}, u32[]{:S(2)}) collective-permute-start(bf16[2,2,128,256]{3,2,1,0:T(8,128)(2,1)S(1)} %get-tuple-element.34), channel_id=1, source_target_pairs={{0,1},{1,0},{2,3},{3,2},{4,5},{5,4},{6,7},{7,6},{8,9},{9,8},{10,11... | collective-permute-start | bytes 786440 | tf_op jit(solution)/shard_map/ppermute | solution.py:306
  13.1 9.3 %collective-permute-start.3 = (bf16[2,2,128,256]{3,2,1,0:T(8,128)(2,1)S(1)}, bf16[2,2,128,256]{3,2,1,0:T(8,128)(2,1)S(1)}, u32[]{:S(2)}, u32[]{:S(2)}) collective-permute-start(bf16[2,2,128,256]{3,2,1,0:T(8,128)(2,1)S(1)} %get-tuple-element.35), channel_id=1, source_target_pairs={{0,2},{1,3},{2,0},{3,1},{4,6},{5,7},{6,4},{7,5},{8,10},{9,11},{10,... | collective-permute-start | bytes 786440 | tf_op jit(solution)/shard_map/ppermute | solution.py:306
  16.5 3.7 %copy-start.12 = (f32[2]{0:T(128)S(1)}, f32[2]{0:T(128)}, u32[]{:S(2)}) copy-start(f32[2]{0:T(128)} %refs_1_.13) | copy-start | bytes 28
  18.0 4.4 %copy-start.6 = (bf16[256,256]{1,0:T(8,128)(2,1)S(1)}, bf16[256,256]{1,0:T(8,128)(2,1)}, u32[]{:S(2)}) copy-start(bf16[256,256]{1,0:T(8,128)(2,1)} %refs_6_.7) | copy-start | bytes 393220
  18.0 5.5 %collective-permute-start.7 = (bf16[2,2,128,256]{3,2,1,0:T(8,128)(2,1)S(1)}, bf16[2,2,128,256]{3,2,1,0:T(8,128)(2,1)S(1)}, u32[]{:S(2)}, u32[]{:S(2)}) collective-permute-start(bf16[2,2,128,256]{3,2,1,0:T(8,128)(2,1)S(1)} %get-tuple-element.44), channel_id=1, source_target_pairs={{0,1},{1,0},{2,3},{3,2},{4,5},{5,4},{6,7},{7,6},{8,9},{9,8},{10,11... | collective-permute-start | bytes 786440 | tf_op jit(solution)/shard_map/ppermute | solution.py:306
  18.2 9.4 %collective-permute-start.6 = (bf16[2,2,128,256]{3,2,1,0:T(8,128)(2,1)S(1)}, bf16[2,2,128,256]{3,2,1,0:T(8,128)(2,1)S(1)}, u32[]{:S(2)}, u32[]{:S(2)}) collective-permute-start(bf16[2,2,128,256]{3,2,1,0:T(8,128)(2,1)S(1)} %get-tuple-element.43), channel_id=1, source_target_pairs={{0,2},{1,3},{2,0},{3,1},{4,6},{5,7},{6,4},{7,5},{8,10},{9,11},{10,... | collective-permute-start | bytes 786440 | tf_op jit(solution)/shard_map/ppermute | solution.py:306

commit v7 on v6

--- a/solution.py
+++ b/solution.py
@@ -165,7 +165,7 @@
 
     def body(recv_ref, blocks_ref, h_ref, *refs):
         in_refs, (pre_ref, wn_ref, wo_ref, rem_ref, out_ref, *send_refs) = refs[:rounds], refs[rounds:]
-        rows = update(goes_to(recv_ref), h_ref, dict(enumerate(in_refs)), pre_ref, wn_ref[layer], wo_ref[layer], rem_ref)
+        rows = update(goes_to(recv_ref), h_ref, dict(zip(incoming, in_refs)), pre_ref, wn_ref[layer], wo_ref[layer], rem_ref)
         out_ref[...] = rows.reshape(steps, cells, width)
         for r in range(rounds):
             for k in range(sent):
@@ -175,7 +175,7 @@
 
     outs = [((steps, cells, width), BF16)] + [((steps, sent, block, width), BF16)] * rounds
     return call(
-        body, "far", outs, [receive, send_blocks], [hidden, *incoming, pre, neighbor, output, remote], after=after
+        body, "far", outs, [receive, send_blocks], [hidden, *incoming.values(), pre, neighbor, output, remote], after=after
     )
 
 
@@ -289,7 +289,7 @@
     incoming = []
     for s in range(showers):
         sends = pack(iterates, s, send_blocks, block)
-        incoming.append([lax.ppermute(sends[r], "dom", pairs[r]) for r in (0, 1)])
+        incoming.append({r: lax.ppermute(sends[r], "dom", pairs[r]) for r in (1, 0)})
     common = (step_embed, self_weight, neighbor_weight, local_columns, tile_values)
     rest = (neighbor_weight, output_weight, remote_values, receive_rows)
     hidden, pre = [None] * showers, [None] * showers
@@ -303,12 +303,12 @@
     for layer in range(1, layers):
         for s in range(showers):
             hidden[s], *sends = far(hidden[s], incoming[s], pre[s], layer - 1, *rest, send_blocks, token)
-            incoming[s] = [lax.ppermute(sends[r], "dom", pairs[r]) for r in (0, 1)]
+            incoming[s] = {r: lax.ppermute(sends[r], "dom", pairs[r]) for r in (1, 0)}
             pre[s] = near(hidden[s], layer, *common, ())
             token = (pre[s],)
     totals, running = (), [None] * showers
     for s in range(showers):
-        rounds = dict(enumerate(incoming[s]))
+        rounds = dict(incoming[s])
         if s > 0:
             pre[s] = middle(rounds.pop(0), pre[s], layers - 1, neighbor_weight, remote_values, receive_rows, totals)
         total, running[s] = finish(

time: 80.3 us -> 79.6 us (level)
  starting transfers between devices: 7.03 us -> 5.75 us
    ppermute x8, starting transfers between devices: 7.03 us -> 5.75 us  [the longest x4 3.04 us: local(): lax.ppermute(sends[r], 'dom', pairs[r])]
where the time goes in v7:
time: 79.6 us; the launch traced here: 79.2 us
  blocking collectives  49.5 us (62%)
  Pallas kernels  19.6 us (25%)
  starting transfers between devices  5.75 us (7%)
  waiting for transfers between devices  3.88 us (5%)
    all_to_all x1, blocking collectives, local(): lax.all_to_all(total.reshape(lax.axis_size('tm'), -1, width), 'tm', 0, 0)  27.8 us
    all_to_all x1, blocking collectives, local(): earlier = lax.all_to_all(exclusive_prefix(pieces), 'tm', 0, 0)  21.7 us
    pallas_call x15, Pallas kernels, call(): pl.pallas_call(inner, out_shape=[pltpu.VMEM(*o) for o in outs] + [pltpu.H...  19.6 us
    ppermute x4, waiting for transfers between devices, local(): incoming[s] = {r: lax.ppermute(sends[r], 'dom', pairs[r]) for r in (1, 0)}  3.87 us
    ppermute x4, starting transfers between devices, local(): lax.ppermute(sends[r], 'dom', pairs[r])  3.04 us
    ppermute x4, starting transfers between devices, local(): incoming[s] = {r: lax.ppermute(sends[r], 'dom', pairs[r]) for r in (1, 0)}  2.71 us
  transfers between devices with their start and end apart: 8, of which 2 were waited for; matrix products, arithmetic and copies ran while one was open for 0% of the time, Pallas kernels for 20%

profile of v7, /device:TPU:2, one launch (start us, length us, event | category | flops | bytes accessed | tf_op | source)
XLA Modules:
  0.0 79.2 jit_solution(16371017483725941620)
XLA Ops:
  0.0 1.4 %pack.2 = (bf16[2,2,128,256]{3,2,1,0:T(8,128)(2,1)S(1)}, bf16[2,2,128,256]{3,2,1,0:T(8,128)(2,1)S(1)}) custom-call(s32[1,2,2]{2,1,0:T(2,128)} %refs_1_.15, f32[2,2,512,256]{3,2,1,0:T(8,128)} %refs_1_.14), custom_call_target="tpu_custom_call" | custom-call | flops 1048576 | bytes 1024 | tf_op jit(solution)/shard_map/pack/pallas_call | solution.py:25
  1.5 2.3 %collective-permute-start = (bf16[2,2,128,256]{3,2,1,0:T(8,128)(2,1)S(1)}, bf16[2,2,128,256]{3,2,1,0:T(8,128)(2,1)S(1)}, u32[]{:S(2)}, u32[]{:S(2)}) collective-permute-start(bf16[2,2,128,256]{3,2,1,0:T(8,128)(2,1)S(1)} %get-tuple-element.28), channel_id=1, source_target_pairs={{0,2},{1,3},{2,0},{3,1},{4,6},{5,7},{6,4},{7,5},{8,10},{9,11},{10,... | collective-permute-start | bytes 786440 | tf_op jit(solution)/shard_map/ppermute | solution.py:292
  3.8 1.3 %pack.3 = (bf16[2,2,128,256]{3,2,1,0:T(8,128)(2,1)S(1)}, bf16[2,2,128,256]{3,2,1,0:T(8,128)(2,1)S(1)}) custom-call(s32[1,2,2]{2,1,0:T(2,128)} %refs_1_.15, f32[2,2,512,256]{3,2,1,0:T(8,128)} %refs_1_.14), custom_call_target="tpu_custom_call" | custom-call | flops 1048576 | bytes 1024 | tf_op jit(solution)/shard_map/pack/pallas_call | solution.py:25
  5.1 0.2 collective-permute-start.4
  5.3 0.5 collective-permute-start.5
  5.8 1.6 %near_first.2 = (f32[2,512,256]{2,1,0:T(8,128)S(1)}, bf16[2,512,256]{2,1,0:T(8,128)(2,1)S(1)}) custom-call(s32[4,4]{1,0:T(4,128)S(1)} %copy-done.7, f32[2,2,512,256]{3,2,1,0:T(8,128)S(1)} %copy-done, f32[2,256]{1,0:T(2,128)S(1)} %copy-done.8, bf16[2,256,256]{2,1,0:T(8,128)(2,1)S(1)} %copy-done.3, bf16[2,256,256]{2,1,0:T(8,128)(2,1)S(1)} %copy-done.1, ...), custom_call_target="tpu_custom_call" | custom-call | flops 1048576 | bytes 1024 | tf_op jit(solution)/shard_map/near_first/pallas_call | solution.py:25
  7.4 1.6 %near_first.3 = (f32[2,512,256]{2,1,0:T(8,128)S(1)}, bf16[2,512,256]{2,1,0:T(8,128)(2,1)S(1)}) custom-call(s32[4,4]{1,0:T(4,128)S(1)} %copy-done.7, f32[2,2,512,256]{3,2,1,0:T(8,128)S(1)} %copy-done, f32[2,256]{1,0:T(2,128)S(1)} %copy-done.8, bf16[2,256,256]{2,1,0:T(8,128)(2,1)S(1)} %copy-done.3, bf16[2,256,256]{2,1,0:T(8,128)(2,1)S(1)} %copy-done.1, ...), custom_call_target="tpu_custom_call" | custom-call | flops 1048576 | bytes 1024 | tf_op jit(solution)/shard_map/near_first/pallas_call | solution.py:25
  9.1 2.4 %noise_sums.1 = (f32[2,512,256]{2,1,0:T(8,128)S(1)}, f32[2,512,256]{2,1,0:T(8,128)S(1)}) custom-call(f32[2]{0:T(128)S(1)} %copy-done.11, bf16[2,2,512,256]{3,2,1,0:T(8,128)(2,1)} %refs_1_.11, f32[2,2,512,256]{3,2,1,0:T(8,128)} %refs_1_.14, f32[2,512,256]{2,1,0:T(8,128)S(1)} %get-tuple-element.31.refs_3_.refs_5_), custom_call_target="tpu_custom_call" | custom-call | flops 1048576 | bytes 1024 | tf_op jit(solution)/shard_map/noise_sums/pallas_call | solution.py:25
  11.5 1.4 %far.2 = (bf16[2,512,256]{2,1,0:T(8,128)(2,1)S(1)}, bf16[2,2,128,256]{3,2,1,0:T(8,128)(2,1)S(1)}, bf16[2,2,128,256]{3,2,1,0:T(8,128)(2,1)S(1)}) custom-call(s32[1,2,2]{2,1,0:T(2,128)S(1)} %copy-done.10, s32[1,2,2]{2,1,0:T(2,128)S(1)} %copy-done.9, bf16[2,512,256]{2,1,0:T(8,128)(2,1)S(1)} %get-tuple-element.27.refs_2_, ...), custom_call_target="tpu_custom_call" | custom-call | flops 1048576 | bytes 1024 | tf_op jit(solution)/shard_map/far/pallas_call | solution.py:25
  13.0 1.7 %collective-permute-start.2 = (bf16[2,2,128,256]{3,2,1,0:T(8,128)(2,1)S(1)}, bf16[2,2,128,256]{3,2,1,0:T(8,128)(2,1)S(1)}, u32[]{:S(2)}, u32[]{:S(2)}) collective-permute-start(bf16[2,2,128,256]{3,2,1,0:T(8,128)(2,1)S(1)} %get-tuple-element.34), channel_id=1, source_target_pairs={{0,2},{1,3},{2,0},{3,1},{4,6},{5,7},{6,4},{7,5},{8,10},{9,11},{10,... | collective-permute-start | bytes 786440 | tf_op jit(solution)/shard_map/ppermute | solution.py:306
  14.7 1.6 %near.2.refs_9_.refs_3_ = f32[2,512,256]{2,1,0:T(8,128)S(1)} custom-call(s32[4,4]{1,0:T(4,128)S(1)} %copy-done.7, bf16[2,512,256]{2,1,0:T(8,128)(2,1)S(1)} %get-tuple-element.33.refs_1_.refs_0_, f32[2,256]{1,0:T(2,128)S(1)} %copy-done.8, bf16[2,256,256]{2,1,0:T(8,128)(2,1)S(1)} %copy-done.3, bf16[2,256,256]{2,1,0:T(8,128)(2,1)S(1)} %copy-done.1, ...), custom_call_target="tpu_custom_call" | custom-call | flops 1048576 | bytes 1024 | tf_op jit(solution)/shard_map/near/pallas_call | solution.py:25
  16.4 1.4 %far.3 = (bf16[2,512,256]{2,1,0:T(8,128)(2,1)S(1)}, bf16[2,2,128,256]{3,2,1,0:T(8,128)(2,1)S(1)}, bf16[2,2,128,256]{3,2,1,0:T(8,128)(2,1)S(1)}) custom-call(s32[1,2,2]{2,1,0:T(2,128)S(1)} %copy-done.10, s32[1,2,2]{2,1,0:T(2,128)S(1)} %copy-done.9, bf16[2,512,256]{2,1,0:T(8,128)(2,1)S(1)} %get-tuple-element.38.refs_2_, ...), custom_call_target="tpu_custom_call" | custom-call | flops 1048576 | bytes 1024 | tf_op jit(solution)/shard_map/far/pallas_call | solution.py:25
  17.8 0.6 collective-permute-start.7
  18.4 0.4 collective-permute-start.6
  18.8 0.6 tables.1
  19.4 1.6 %near.3.refs_11_.refs_2_ = f32[2,512,256]{2,1,0:T(8,128)S(1)} custom-call(s32[4,4]{1,0:T(4,128)S(1)} %copy-done.7, bf16[2,512,256]{2,1,0:T(8,128)(2,1)S(1)} %get-tuple-element.41.refs_1_.refs_0_, f32[2,256]{1,0:T(2,128)S(1)} %copy-done.8, bf16[2,256,256]{2,1,0:T(8,128)(2,1)S(1)} %copy-done.3, bf16[2,256,256]{2,1,0:T(8,128)(2,1)S(1)} %copy-done.1, ...), custom_call_target="tpu_custom_call" | custom-call | flops 1048576 | bytes 1024 | tf_op jit(solution)/shard_map/near/pallas_call | solution.py:25
  21.0 0.6 collective-permute-done.2.refs_1_
  21.6 1.2 %finish.2 = (bf16[2,512,256]{2,1,0:T(8,128)(2,1)S(1)}, f32[2,512,256]{2,1,0:T(8,128)S(1)}) custom-call(bf16[2,512,256]{2,1,0:T(8,128)(2,1)S(1)} %get-tuple-element.33.refs_1_.refs_0_, bf16[2,2,128,256]{3,2,1,0:T(8,128)(2,1)S(1)} %collective-permute-done.2.refs_1_, bf16[2,2,128,256]{3,2,1,0:T(8,128)(2,1)S(1)} %collective-permute-done.3.refs_2_, ...), custom_call_target="tpu_custom_call" | custom-call | flops 1048576 | bytes 1024 | tf_op jit(solution)/shard_map/finish/pallas_call | solution.py:25
  22.8 1.1 %middle.1.refs_2_ = f32[2,512,256]{2,1,0:T(8,128)S(1)} custom-call(s32[1,2,2]{2,1,0:T(2,128)S(1)} %copy-done.10, bf16[2,2,128,256]{3,2,1,0:T(8,128)(2,1)S(1)} %collective-permute-done.7.refs_1_, f32[2,512,256]{2,1,0:T(8,128)S(1)} %near.3.refs_11_.refs_2_, bf16[2,256,256]{2,1,0:T(8,128)(2,1)S(1)} %copy-done.1, bf16[1,2,2,128,128]{4,3,2,1,0:T(8,128)(2,1)S(1)} %copy-done.5, ...), custom_call_target="tpu_custom_call" | custom-call | flops 1048576 | bytes 1024 | tf_op jit(solution)/shard_map/middle/pallas_call | solution.py:25
  23.8 3.3 %collective-permute-done.6.refs_1_ = bf16[2,2,128,256]{3,2,1,0:T(8,128)(2,1)S(1)} collective-permute-done((bf16[2,2,128,256]{3,2,1,0:T(8,128)(2,1)S(1)}, bf16[2,2,128,256]{3,2,1,0:T(8,128)(2,1)S(1)}, u32[]{:S(2)}, u32[]{:S(2)}) %collective-permute-start.6) | collective-permute-done | bytes 262176 | tf_op jit(solution)/shard_map/ppermute | solution.py:306
  27.1 0.9 %finish.3 = (bf16[2,512,256]{2,1,0:T(8,128)(2,1)S(1)}, f32[2,512,256]{2,1,0:T(8,128)S(1)}) custom-call(bf16[2,512,256]{2,1,0:T(8,128)(2,1)S(1)} %get-tuple-element.41.refs_1_.refs_0_, bf16[2,2,128,256]{3,2,1,0:T(8,128)(2,1)S(1)} %collective-permute-done.6.refs_1_, f32[2,512,256]{2,1,0:T(8,128)S(1)} %middle.1.refs_2_, ...), custom_call_target="tpu_custom_call", output_to_operand_aliasing={{0}: (10, {})} | custom-call | flops 1048576 | bytes 1024 | tf_op jit(solution)/shard_map/finish/pallas_call | solution.py:25
  28.1 27.8 %all_to_all.10.refs_0_ = bf16[32,32,256]{2,1,0:T(8,128)(2,1)S(1)} all-to-all(bf16[32,32,256]{2,1,0:T(8,128)(2,1)S(1)} %bitcast.2), channel_id=1, replica_groups=mesh['tm'=32,'dom'=8] {'tm'}, dimensions={0} | all-to-all | bytes 1048576 | tf_op jit(solution)/shard_map/all_to_all | solution.py:319
  55.9 21.7 %all_to_all.11 = bf16[32,32,256]{2,1,0:T(8,128)(2,1)S(1)} all-to-all(bf16[32,32,256]{2,1,0:T(8,128)(2,1)S(1)} %exclusive_prefix.1), channel_id=1, replica_groups=mesh['tm'=32,'dom'=8] {'tm'}, dimensions={0} | all-to-all | bytes 1048576 | tf_op jit(solution)/shard_map/all_to_all | solution.py:320
  77.7 1.4 %deliver.1 = f32[2,2,512,256]{3,2,1,0:T(8,128)} custom-call(f32[2,512,256]{2,1,0:T(8,128)S(1)} %get-tuple-element.42.refs_0_, f32[2,512,256]{2,1,0:T(8,128)S(1)} %get-tuple-element.47.refs_1_, bf16[2,512,256]{2,1,0:T(8,128)(2,1)S(1)} %bitcast.3), custom_call_target="tpu_custom_call" | custom-call | flops 1048576 | bytes 1024 | tf_op jit(solution)/shard_map/deliver/pallas_call | solution.py:25
  (35 shorter events, 0.2 us)
Async XLA Ops:
  0.0 5.8 %copy-start = (f32[2,2,512,256]{3,2,1,0:T(8,128)S(1)}, f32[2,2,512,256]{3,2,1,0:T(8,128)}, u32[]{:S(2)}) copy-start(f32[2,2,512,256]{3,2,1,0:T(8,128)} %refs_1_.14) | copy-start | bytes 6291460
  0.0 5.8 %copy-start.1 = (bf16[2,256,256]{2,1,0:T(8,128)(2,1)S(1)}, bf16[2,256,256]{2,1,0:T(8,128)(2,1)}, u32[]{:S(2)}) copy-start(bf16[2,256,256]{2,1,0:T(8,128)(2,1)} %refs_3_.11) | copy-start | bytes 786436
  0.0 5.8 %copy-start.2 = (bf16[4,4,128,128]{3,2,1,0:T(8,128)(2,1)S(1)}, bf16[4,4,128,128]{3,2,1,0:T(8,128)(2,1)}, u32[]{:S(2)}) copy-start(bf16[4,4,128,128]{3,2,1,0:T(8,128)(2,1)} %refs_5_.9) | copy-start | bytes 1572868
  0.0 5.8 %copy-start.7 = (s32[4,4]{1,0:T(4,128)S(1)}, s32[4,4]{1,0:T(4,128)}, u32[]{:S(2)}) copy-start(s32[4,4]{1,0:T(4,128)} %refs_0_.20) | copy-start | bytes 196
  0.0 5.8 %copy-start.3 = (bf16[2,256,256]{2,1,0:T(8,128)(2,1)S(1)}, bf16[2,256,256]{2,1,0:T(8,128)(2,1)}, u32[]{:S(2)}) copy-start(bf16[2,256,256]{2,1,0:T(8,128)(2,1)} %refs_3_.9) | copy-start | bytes 786436
  0.0 5.8 %copy-start.8 = (f32[2,256]{1,0:T(2,128)S(1)}, f32[2,256]{1,0:T(2,128)}, u32[]{:S(2)}) copy-start(f32[2,256]{1,0:T(2,128)} %refs_2_.9) | copy-start | bytes 6148
  1.5 10.0 %collective-permute-start = (bf16[2,2,128,256]{3,2,1,0:T(8,128)(2,1)S(1)}, bf16[2,2,128,256]{3,2,1,0:T(8,128)(2,1)S(1)}, u32[]{:S(2)}, u32[]{:S(2)}) collective-permute-start(bf16[2,2,128,256]{3,2,1,0:T(8,128)(2,1)S(1)} %get-tuple-element.28), channel_id=1, source_target_pairs={{0,2},{1,3},{2,0},{3,1},{4,6},{5,7},{6,4},{7,5},{8,10},{9,11},{10,... | collective-permute-start | bytes 786440 | tf_op jit(solution)/shard_map/ppermute | solution.py:292
  3.8 7.7 %collective-permute-start.1 = (bf16[2,2,128,256]{3,2,1,0:T(8,128)(2,1)S(1)}, bf16[2,2,128,256]{3,2,1,0:T(8,128)(2,1)S(1)}, u32[]{:S(2)}, u32[]{:S(2)}) collective-permute-start(bf16[2,2,128,256]{3,2,1,0:T(8,128)(2,1)S(1)} %get-tuple-element.29), channel_id=1, source_target_pairs={{0,1},{1,0},{2,3},{3,2},{4,5},{5,4},{6,7},{7,6},{8,9},{9,8},{10,11... | collective-permute-start | bytes 786440 | tf_op jit(solution)/shard_map/ppermute | solution.py:292
  5.1 11.3 %collective-permute-start.4 = (bf16[2,2,128,256]{3,2,1,0:T(8,128)(2,1)S(1)}, bf16[2,2,128,256]{3,2,1,0:T(8,128)(2,1)S(1)}, u32[]{:S(2)}, u32[]{:S(2)}) collective-permute-start(bf16[2,2,128,256]{3,2,1,0:T(8,128)(2,1)S(1)} %get-tuple-element.39), channel_id=1, source_target_pairs={{0,2},{1,3},{2,0},{3,1},{4,6},{5,7},{6,4},{7,5},{8,10},{9,11},{10,... | collective-permute-start | bytes 786440 | tf_op jit(solution)/shard_map/ppermute | solution.py:292
  5.3 11.1 %collective-permute-start.5 = (bf16[2,2,128,256]{3,2,1,0:T(8,128)(2,1)S(1)}, bf16[2,2,128,256]{3,2,1,0:T(8,128)(2,1)S(1)}, u32[]{:S(2)}, u32[]{:S(2)}) collective-permute-start(bf16[2,2,128,256]{3,2,1,0:T(8,128)(2,1)S(1)} %get-tuple-element.40), channel_id=1, source_target_pairs={{0,1},{1,0},{2,3},{3,2},{4,5},{5,4},{6,7},{7,6},{8,9},{9,8},{10,11... | collective-permute-start | bytes 786440 | tf_op jit(solution)/shard_map/ppermute | solution.py:292
  7.4 1.6 %copy-start.11 = (f32[2]{0:T(128)S(1)}, f32[2]{0:T(128)}, u32[]{:S(2)}) copy-start(f32[2]{0:T(128)} %refs_0_.14) | copy-start | bytes 28
  9.1 2.4 %copy-start.4 = (bf16[2,256,256]{2,1,0:T(8,128)(2,1)S(1)}, bf16[2,256,256]{2,1,0:T(8,128)(2,1)}, u32[]{:S(2)}) copy-start(bf16[2,256,256]{2,1,0:T(8,128)(2,1)} %refs_4_.13) | copy-start | bytes 786436
  9.1 2.4 %copy-start.5 = (bf16[1,2,2,128,128]{4,3,2,1,0:T(8,128)(2,1)S(1)}, bf16[1,2,2,128,128]{4,3,2,1,0:T(8,128)(2,1)}, u32[]{:S(2)}) copy-start(bf16[1,2,2,128,128]{4,3,2,1,0:T(8,128)(2,1)} %refs_5_.11) | copy-start | bytes 393220
  9.1 2.4 %copy-start.9 = (s32[1,2,2]{2,1,0:T(2,128)S(1)}, s32[1,2,2]{2,1,0:T(2,128)}, u32[]{:S(2)}) copy-start(s32[1,2,2]{2,1,0:T(2,128)} %refs_1_.15) | copy-start | bytes 52
  9.1 2.4 %copy-start.10 = (s32[1,2,2]{2,1,0:T(2,128)S(1)}, s32[1,2,2]{2,1,0:T(2,128)}, u32[]{:S(2)}) copy-start(s32[1,2,2]{2,1,0:T(2,128)} %refs_0_.21) | copy-start | bytes 52
  13.0 8.6 %collective-permute-start.2 = (bf16[2,2,128,256]{3,2,1,0:T(8,128)(2,1)S(1)}, bf16[2,2,128,256]{3,2,1,0:T(8,128)(2,1)S(1)}, u32[]{:S(2)}, u32[]{:S(2)}) collective-permute-start(bf16[2,2,128,256]{3,2,1,0:T(8,128)(2,1)S(1)} %get-tuple-element.34), channel_id=1, source_target_pairs={{0,2},{1,3},{2,0},{3,1},{4,6},{5,7},{6,4},{7,5},{8,10},{9,11},{10,... | collective-permute-start | bytes 786440 | tf_op jit(solution)/shard_map/ppermute | solution.py:306
  14.7 6.9 %collective-permute-start.3 = (bf16[2,2,128,256]{3,2,1,0:T(8,128)(2,1)S(1)}, bf16[2,2,128,256]{3,2,1,0:T(8,128)(2,1)S(1)}, u32[]{:S(2)}, u32[]{:S(2)}) collective-permute-start(bf16[2,2,128,256]{3,2,1,0:T(8,128)(2,1)S(1)} %get-tuple-element.35), channel_id=1, source_target_pairs={{0,1},{1,0},{2,3},{3,2},{4,5},{5,4},{6,7},{7,6},{8,9},{9,8},{10,11... | collective-permute-start | bytes 786440 | tf_op jit(solution)/shard_map/ppermute | solution.py:306
  16.3 2.5 %copy-start.12 = (f32[2]{0:T(128)S(1)}, f32[2]{0:T(128)}, u32[]{:S(2)}) copy-start(f32[2]{0:T(128)} %refs_1_.13) | copy-start | bytes 28
  17.8 3.8 %copy-start.6 = (bf16[256,256]{1,0:T(8,128)(2,1)S(1)}, bf16[256,256]{1,0:T(8,128)(2,1)}, u32[]{:S(2)}) copy-start(bf16[256,256]{1,0:T(8,128)(2,1)} %refs_6_.7) | copy-start | bytes 393220
  17.8 4.9 %collective-permute-start.7 = (bf16[2,2,128,256]{3,2,1,0:T(8,128)(2,1)S(1)}, bf16[2,2,128,256]{3,2,1,0:T(8,128)(2,1)S(1)}, u32[]{:S(2)}, u32[]{:S(2)}) collective-permute-start(bf16[2,2,128,256]{3,2,1,0:T(8,128)(2,1)S(1)} %get-tuple-element.44), channel_id=1, source_target_pairs={{0,1},{1,0},{2,3},{3,2},{4,5},{5,4},{6,7},{7,6},{8,9},{9,8},{10,11... | collective-permute-start | bytes 786440 | tf_op jit(solution)/shard_map/ppermute | solution.py:306
  18.4 8.7 %collective-permute-start.6 = (bf16[2,2,128,256]{3,2,1,0:T(8,128)(2,1)S(1)}, bf16[2,2,128,256]{3,2,1,0:T(8,128)(2,1)S(1)}, u32[]{:S(2)}, u32[]{:S(2)}) collective-permute-start(bf16[2,2,128,256]{3,2,1,0:T(8,128)(2,1)S(1)} %get-tuple-element.43), channel_id=1, source_target_pairs={{0,2},{1,3},{2,0},{3,1},{4,6},{5,7},{6,4},{7,5},{8,10},{9,11},{10,... | collective-permute-start | bytes 786440 | tf_op jit(solution)/shard_map/ppermute | solution.py:306
